TPU v7x, 128 devices: a whole 4x4x4 slice. The times are simulated.
128 devices in a mesh: group: 16 (over y, x_lo, core), fsdp: 8 (over x_hi, z).
Axes of the slice: x: 4 (x_hi: 2, x_lo: 2; x = x_hi * 2 + x_lo), y: 4, z: 4, core: 2. Of those that a mesh axis runs over, the one named last changes fastest.
Arguments:
- query_embeddings: bfloat16 [512, 4096], P(('group', 'fsdp')), may hold values from -4 to 4
- passage_embeddings: bfloat16 [512, 4096], P(('group', 'fsdp')), may hold values from -4 to 4
- positives: int32 [512], P(('group', 'fsdp')), may hold values from 0 to 511, each once
- logarithm_scale: float32 [], replicated, may hold values from 2.4 to 2.8
- residual_input: bfloat16 [128, 256, 4096], P(('group', 'fsdp')), may hold values from -6 to 6
- attention_head_outputs: bfloat16 [128, 256, 4096], P(('group', 'fsdp')), may hold values from -6 to 6
- output_weight: bfloat16 [4096, 4096], P('fsdp'), may hold values from -0.09375 to 0.09375
- adapter_down_weight: bfloat16 [4096, 16], replicated, may hold values from -0.09375 to 0.09375
- adapter_up_weight: bfloat16 [16, 4096], replicated, may hold values from -0.375 to 0.375
- final_norm_weight: float32 [4096], replicated, may hold values from 0.5 to 1.5
- lengths: int32 [128], P(('group', 'fsdp')), may hold values from 64 to 256
Outputs:
- loss: float32 [], replicated
- scale_grad: float32 [], replicated
- query_grad: float32 [512, 4096], P(('group', 'fsdp'))
- passage_grad: float32 [512, 4096], P(('group', 'fsdp'))
- attn_grad: bfloat16 [128, 256, 4096], P(('group', 'fsdp'))
- residual_grad: bfloat16 [128, 256, 4096], P(('group', 'fsdp'))
- lora_down_grad: float32 [4096, 16], replicated
- lora_up_grad: float32 [16, 4096], replicated
All inputs are finite; a program needn't handle non-finite values.
Results may differ from a plain program's by a relative error of at most 0.01.
Values may be sent and summed in bfloat16 or wider, within the bound.
No kernel may reach another device: no remote copies, remote signals or barrier semaphores. Data moves between devices by JAX's collectives and lax.ppermute only.
A program may use at most 128 MiB of HBM per device.

v0:
```python
import functools

import jax
import jax.numpy as jnp
from jax import lax
from jax.experimental import pallas as pl
from jax.experimental.pallas import tpu as pltpu
from jax.sharding import PartitionSpec as P


grad_scale = 512.0
adapter_scale = 2.0
epsilon = 1e-05
AX = ("group", "fsdp")
NT = (((1,), (1,)), ((), ()))
TN = (((0,), (0,)), ((), ()))
f32 = jnp.float32
bf16 = jnp.bfloat16


def coords(i):
    g, f = divmod(i, 8)
    return (f // 4) * 2 + (g // 2) % 2, g // 4, f % 4, g % 2


def device(x, y, z, c):
    x, y, z = x % 4, y % 4, z % 4
    return ((y * 2 + x % 2) * 2 + c) * 8 + (x // 2) * 4 + z


def table(move):
    return [(i, device(*move(*coords(i)))) for i in range(128)]


MOVES = {
    "core": table(lambda x, y, z, c: (x, y, z, 1 - c)),
    "xnear": table(lambda x, y, z, c: (x ^ 1, y, z, c)),
    "xflip": table(lambda x, y, z, c: (3 - x, y, z, c)),
    "ynear": table(lambda x, y, z, c: (x, y ^ 1, z, c)),
    "yflip": table(lambda x, y, z, c: (x, 3 - y, z, c)),
    "znear": table(lambda x, y, z, c: (x, y, z ^ 1, c)),
    "zflip": table(lambda x, y, z, c: (x, y, 3 - z, c)),
    "yup": table(lambda x, y, z, c: (x, y + 1, z, c)),
    "ydown": table(lambda x, y, z, c: (x, y - 1, z, c)),
    "zup": table(lambda x, y, z, c: (x, y, z + 1, c)),
    "zdown": table(lambda x, y, z, c: (x, y, z - 1, c)),
    "zfar": table(lambda x, y, z, c: (x, y, z + 2, c)),
}


def send(value, move):
    return lax.ppermute(value, AX, MOVES[move])


def ordered(bit, mine, other, axis=0):
    return jnp.where(
        bit == 0,
        jnp.concatenate([mine, other], axis=axis),
        jnp.concatenate([other, mine], axis=axis),
    )


def pick(value, start, size, axis=0):
    return lax.dynamic_slice_in_dim(value, start, size, axis=axis)


def block_kernel(copies, scal, *refs):
    n_src = 1 + max(src for src, *_ in copies)
    srcs = refs[:n_src]
    a_own, a_par, r_own, r_par, low, up, q_rows, q_f = refs[n_src : n_src + 8]
    hid_out, st_out, y_own, y_par, y_q = refs[n_src + 8 : n_src + 13]
    w_s, a_s, r_s, hid, hb_s, yo_s, yp_s, w_sem, in_sem, out_sem = refs[n_src + 13 :]
    half = pl.multiple_of(scal[12], 2048)
    inputs = [
        pltpu.make_async_copy(a_own, a_s.at[pl.ds(0, 256), :], in_sem.at[0]),
        pltpu.make_async_copy(a_par, a_s.at[pl.ds(256, 256), :], in_sem.at[1]),
        pltpu.make_async_copy(r_own.at[:, pl.ds(half, 2048)], r_s.at[pl.ds(0, 256), :], in_sem.at[2]),
        pltpu.make_async_copy(r_par, r_s.at[pl.ds(256, 256), :], in_sem.at[3]),
    ]
    for copy in inputs:
        copy.start()
    for src, src_row, src_col, rows, shard, dst_row, dst_col, cols in copies:
        ref = srcs[src]
        if src_col is None:
            view = ref.at[pl.ds(src_row, rows), :]
        else:
            view = ref.at[pl.ds(src_row, rows), pl.ds(pl.multiple_of(scal[src_col], 256), cols)]
        first = pl.multiple_of(scal[shard] * 512 + dst_row, 256)
        if isinstance(dst_col, tuple):
            col = pl.multiple_of(scal[dst_col[0]] * 256, 256)
        else:
            col = dst_col
        pltpu.make_async_copy(
            view, w_s.at[pl.ds(first, rows), pl.ds(col, cols)], w_sem.at[shard]
        ).start()
    for copy in inputs:
        copy.wait()
    hid[...] = r_s[...].astype(f32) + adapter_scale * jnp.dot(
        low[...], up[...], preferred_element_type=f32
    )

    def forward(shard, carry):
        rows = pl.ds(pl.multiple_of(scal[shard] * 512, 512), 512)
        pltpu.make_async_copy(w_s.at[rows, :], w_s.at[rows, :], w_sem.at[shard]).wait()
        hid[...] += jnp.dot(a_s[:, rows], w_s[rows, :], preferred_element_type=f32)
        return carry

    lax.fori_loop(0, 8, forward, 0)
    hid_copy = pltpu.make_async_copy(hid, hid_out, out_sem.at[2])
    hid_copy.start()
    value = hid[...]
    hb_s[pl.ds(0, 512), :] = value.astype(bf16)
    hb_s[pl.ds(512, 16), :] = q_rows[...]
    st_out[...] = jnp.zeros_like(st_out)
    st_out[:, 0:16] = lax.dot_general(hb_s[...], up[...], NT, preferred_element_type=f32)
    st_out[0:512, 16:17] = jnp.sum(value * value, axis=1, keepdims=True)
    st_out[0:256, 17:18] = jnp.sum(value[:256] * q_f[0:1, :], axis=1, keepdims=True)
    st_out[256:512, 17:18] = jnp.sum(value[256:] * q_f[1:2, :], axis=1, keepdims=True)

    def backward(shard, carry):
        columns = pl.ds(pl.multiple_of(scal[shard] * 512, 512), 512)
        part = lax.dot_general(hb_s[...], w_s[columns, :], NT, preferred_element_type=f32)
        yo_s[:, columns] = part[:256]
        yp_s[:, columns] = part[256:512].astype(bf16)
        y_q[:, columns] = part[512:]
        pltpu.make_async_copy(yo_s.at[:, columns], y_own.at[:, columns], out_sem.at[0]).start()
        pltpu.make_async_copy(yp_s.at[:, columns], y_par.at[:, columns], out_sem.at[1]).start()
        return carry

    lax.fori_loop(0, 8, backward, 0)
    pltpu.make_async_copy(yo_s, y_own, out_sem.at[0]).wait()
    pltpu.make_async_copy(yp_s, y_par, out_sem.at[1]).wait()
    hid_copy.wait()


def block_call(copies, srcs, scal, a_own, a_par, r_own, r_par, low, up, q_rows, q_f):
    vm = pl.BlockSpec(memory_space=pltpu.VMEM)
    anyspace = pl.BlockSpec(memory_space=pl.ANY)
    return pl.pallas_call(
        functools.partial(block_kernel, copies),
        out_shape=[
            jax.ShapeDtypeStruct((512, 2048), f32),
            jax.ShapeDtypeStruct((528, 128), f32),
            jax.ShapeDtypeStruct((256, 4096), f32),
            jax.ShapeDtypeStruct((256, 4096), bf16),
            jax.ShapeDtypeStruct((16, 4096), f32),
        ],
        in_specs=[pl.BlockSpec(memory_space=pltpu.SMEM)] + [anyspace] * (len(srcs) + 4) + [vm] * 4,
        out_specs=[anyspace, vm, anyspace, anyspace, vm],
        scratch_shapes=[
            pltpu.VMEM((4096, 2048), bf16),
            pltpu.VMEM((512, 4096), bf16),
            pltpu.VMEM((512, 2048), bf16),
            pltpu.VMEM((512, 2048), f32),
            pltpu.VMEM((528, 2048), bf16),
            pltpu.VMEM((256, 4096), f32),
            pltpu.VMEM((256, 4096), bf16),
            pltpu.SemaphoreType.DMA((8,)),
            pltpu.SemaphoreType.DMA((4,)),
            pltpu.SemaphoreType.DMA((3,)),
        ],
        compiler_params=pltpu.CompilerParams(vmem_limit_bytes=48 * 1024 * 1024),
        cost_estimate=pl.CostEstimate(
            flops=4 * 512 * 4096 * 2048, transcendentals=0, bytes_accessed=32 << 20
        ),
        name="block",
    )(scal, *srcs, a_own, a_par, r_own, r_par, low, up, q_rows, q_f)


REL = [(0, 0), (0, -1), (0, 1), (0, 2), (1, 0), (1, -1), (1, 1), (1, 2)]


def compute(
    query_embeddings,
    passage_embeddings,
    positives,
    logarithm_scale,
    residual_input,
    attention_head_outputs,
    output_weight,
    adapter_down_weight,
    adapter_up_weight,
    final_norm_weight,
    lengths,
):
    group = lax.axis_index("group")
    fsdp = lax.axis_index("fsdp")
    y, x_lo, c = group // 4, (group // 2) % 2, group % 2
    x_hi, z = fsdp // 4, fsdp % 4
    x = x_hi * 2 + x_lo
    half = c * 2048
    other_half = 2048 - half
    logit_scale = jnp.exp(logarithm_scale)
    a_own = attention_head_outputs.reshape(256, 4096)
    res_own = residual_input.reshape(256, 4096)

    extras = jnp.concatenate(
        [
            (positives // 16).astype(bf16)[:, None],
            (positives % 16).astype(bf16)[:, None],
            jnp.broadcast_to(lengths.astype(bf16)[:, None], (4, 1)),
            jnp.zeros((4, 125), bf16),
        ],
        axis=1,
    )
    both = jnp.concatenate([query_embeddings, passage_embeddings], axis=0)
    tags = jnp.concatenate([extras, extras], axis=0)
    mine = jnp.concatenate([pick(both, half, 2048, 1), tags], axis=1)
    theirs = send(jnp.concatenate([pick(both, other_half, 2048, 1), tags], axis=1), "core")
    q_chip = ordered(c, mine[:4], theirs[:4])
    p_chip = ordered(c, mine[4:, :2048], theirs[4:, :2048])
    len_par = theirs[0, 2050].astype(f32)

    s_g = pick(output_weight, half + y * 256, 256, 1)
    s_ab = pick(output_weight, half + 1024, 1024, 1)
    o_g = send(s_g, "xflip")
    o_ab = send(s_ab, "xflip")

    p_blk = ordered(z % 2, p_chip, send(p_chip, "znear"))
    p_blk = ordered(z // 2, p_blk, send(p_blk, "zflip"))
    p_blk = ordered(y % 2, p_blk, send(p_blk, "ynear"))
    p_blk = ordered(y // 2, p_blk, send(p_blk, "yflip"))
    q_blk = ordered(x % 2, q_chip, send(q_chip, "xnear"))
    q_blk = ordered(x // 2, q_blk, send(q_blk, "xflip"))

    ga = jnp.concatenate([s_g, o_g, s_ab[:, :256]], axis=0)
    up0 = send(ga, "zup")
    dn0 = send(ga, "zdown")
    up1 = send(jnp.concatenate([up0[:512], up0[1024:1280]], axis=0), "zup")
    dn1 = send(jnp.concatenate([dn0[512:1024], dn0[1280:]], axis=0), "zdown")
    y0 = jnp.concatenate([o_g, up0[:1024], dn0[:1024], up1[:512], dn1[:512]], axis=0)
    y_up = send(y0, "yup")
    y_dn = send(y0, "ydown")
    y_far0 = send(y_up[:1792], "yup")
    y_far1 = send(y_dn[1792:], "ydown")
    a_x = send(jnp.concatenate([up0[1024:], dn0[1024:], up1[512:], dn1[512:]], axis=0), "xflip")
    b0 = jnp.concatenate([s_ab[:, 256:], o_ab[:, 256:]], axis=0)
    b_up = send(b0, "zup")
    b_dn = send(b0, "zdown")
    b_far0 = send(b_up[:512], "zup")
    b_far1 = send(b_dn[512:], "zdown")

    q_feat = q_blk[:, :2048]
    positive = (q_blk[:, 2048].astype(f32) * 16 + q_blk[:, 2049].astype(f32)).astype(jnp.int32)
    row = jnp.arange(128, dtype=jnp.int32)
    row_c, row_z, row_y = (row // 4) % 2, (row // 8) % 4, row // 32
    passage_id = (((row_y * 2 + x_lo) * 2 + row_c) * 8 + x_hi * 4 + row_z) * 4 + row % 4
    partial = lax.dot_general(q_feat, p_blk, NT, preferred_element_type=f32)
    logits = logit_scale * (partial + send(partial, "core"))
    hit = positive[:, None] == passage_id[None, :]
    m = jnp.max(logits, axis=1)
    e = jnp.exp(logits - m[:, None])
    stats = jnp.stack(
        [m, jnp.sum(e, 1), jnp.sum(e * logits, 1), jnp.sum(jnp.where(hit, logits, 0.0), 1)]
    )
    for move in ("xnear", "xflip"):
        got = send(stats, move)
        top = jnp.maximum(stats[0], got[0])
        fa, fb = jnp.exp(stats[0] - top), jnp.exp(got[0] - top)
        stats = jnp.stack(
            [
                top,
                stats[1] * fa + got[1] * fb,
                stats[2] * fa + got[2] * fb,
                stats[3] + got[3],
            ]
        )
    log_norm = stats[0] + jnp.log(stats[1])
    loss_rows = log_norm - stats[3]
    scale_rows = stats[2] / stats[1] - stats[3]
    weight_half = jnp.exp(logits - log_norm[:, None]).astype(bf16)
    hot = hit.astype(bf16)
    q_part = jnp.dot(weight_half, p_blk, preferred_element_type=f32) - jnp.dot(
        hot, p_blk, preferred_element_type=f32
    )
    p_part = lax.dot_general(weight_half, q_feat, TN, preferred_element_type=f32) - lax.dot_general(
        hot, q_feat, TN, preferred_element_type=f32
    )
    xh, xl = x // 2, x % 2
    q_sum = pick(q_part, 16 * xh, 16) + send(pick(q_part, 16 * (1 - xh), 16), "xflip")
    q_sum = pick(q_sum, 8 * xl, 8) + send(pick(q_sum, 8 * (1 - xl), 8), "xnear")
    q_sum = logit_scale * q_sum

    a_own, res_own, _ = lax.optimization_barrier((a_own, res_own, q_sum))
    a_par = send(a_own, "core")
    r_par = send(pick(res_own, other_half, 2048, 1), "core")
    low = jnp.concatenate(
        [
            jnp.dot(a_own, adapter_down_weight, preferred_element_type=f32),
            jnp.dot(a_par, adapter_down_weight, preferred_element_type=f32),
        ],
        axis=0,
    ).astype(bf16)
    up_half = pick(adapter_up_weight, half, 2048, 1)
    gain = pick(final_norm_weight, half, 2048)
    q_own = pick(q_sum, 4 * c, 1) * gain[None]
    q_par = pick(q_sum, 4 * (1 - c), 1) * gain[None]
    q_f = jnp.concatenate([q_own, q_par, jnp.zeros((6, 2048), f32)], axis=0)
    q_hi = q_f[:2].astype(bf16)
    q_lo = (q_f[:2] - q_hi.astype(f32)).astype(bf16)
    q_rows = jnp.concatenate([q_hi, q_lo, jnp.zeros((12, 2048), bf16)], axis=0)

    shard_ids = [(x_hi ^ du) * 4 + (z + dz) % 4 for du, dz in REL]
    scal = jnp.stack(shard_ids + [(y + dy) % 4 for dy in (0, -1, 1, 2)] + [half]).astype(jnp.int32)
    srcs, copies = [output_weight], [(0, 0, 12, 512, 0, 0, 0, 2048)]

    def land(value, shards, dst_col, cols, at=0):
        if not any(value is known for known in srcs):
            srcs.append(value)
        index = [value is known for known in srcs].index(True)
        for shard, dst_row, rows in shards:
            copies.append((index, at, None, rows, shard, dst_row, dst_col, cols))
            at += rows

    whole = lambda shard: (shard, 0, 512)
    seven = [whole(shard) for shard in (4, 1, 5, 2, 6, 3, 7)]
    land(y0, seven, (8,), 256)
    land(y_up, seven, (9,), 256)
    land(y_dn, seven, (10,), 256)
    land(y_far0, seven[:3] + [(2, 0, 256)], (11,), 256)
    land(y_far1, [(2, 256, 256)] + seven[4:], (11,), 256)
    land(o_ab, [whole(4)], 1024, 1024)
    land(up0, [whole(1)], 1024, 256, 1024)
    land(dn0, [whole(2)], 1024, 256, 1024)
    land(up1, [(3, 0, 256)], 1024, 256, 512)
    land(dn1, [(3, 256, 256)], 1024, 256, 512)
    land(a_x, [whole(5), whole(6), whole(7)], 1024, 256)
    land(b_up, [whole(1), whole(5)], 1280, 768)
    land(b_dn, [whole(2), whole(6)], 1280, 768)
    land(b_far0, [whole(3)], 1280, 768)
    land(b_far1, [whole(7)], 1280, 768)
    hidden, stats_own, y_own, y_par, y_q = block_call(
        copies, srcs, scal, a_own, a_par, res_own, r_par, low, up_half, q_rows, q_f
    )

    v_own, v_par = y_q[0:1] + y_q[2:3], y_q[1:2] + y_q[3:4]
    packed = jnp.concatenate([stats_own, v_par.reshape(32, 128)], axis=0)
    got = send(packed, "core")
    y_got = send(y_par, "core")
    tok = stats_own[:512] + jnp.concatenate([got[256:512], got[:256]], axis=0)
    qu_own = stats_own[512, :16] + stats_own[514, :16] + got[513, :16] + got[515, :16]
    qu_par = stats_own[513, :16] + stats_own[515, :16] + got[512, :16] + got[514, :16]
    v = v_own + got[528:].reshape(1, 4096)
    position = jnp.arange(256, dtype=jnp.int32).astype(f32)
    len_own = lengths[0].astype(f32)
    w_tok = jnp.concatenate(
        [
            grad_scale * (position < len_own).astype(f32) / len_own,
            grad_scale * (position < len_par).astype(f32) / len_par,
        ]
    )
    inv = lax.rsqrt(tok[:, 16] / 4096 + epsilon)
    lead = inv * w_tok
    back = inv * inv * inv * (w_tok * tok[:, 17] / 4096)
    qu = jnp.concatenate(
        [jnp.broadcast_to(qu_own[None], (256, 16)), jnp.broadcast_to(qu_par[None], (256, 16))], 0
    )
    low_grad = (adapter_scale * (lead[:, None] * qu - back[:, None] * tok[:, :16])).astype(bf16)
    q_tok = jnp.concatenate(
        [jnp.broadcast_to(q_own, (256, 2048)), jnp.broadcast_to(q_par, (256, 2048))], axis=0
    )
    res_grad = (lead[:, None] * q_tok - back[:, None] * hidden).astype(bf16)
    r_got = send(res_grad[256:], "core")
    residual_grad = ordered(c, res_grad[:256], r_got, axis=1)
    attn_grad = (
        lead[:256, None] * v
        - back[:256, None] * (y_own + y_got.astype(f32))
        + lax.dot_general(low_grad[:256], adapter_down_weight, NT, preferred_element_type=f32)
    ).astype(bf16)

    up_part = adapter_scale * lax.dot_general(low, res_grad, TN, preferred_element_type=f32)
    down_part = lax.dot_general(
        low_grad[:256], pick(a_own, half, 2048, 1), TN, preferred_element_type=f32
    ) + lax.dot_general(low_grad[256:], pick(a_par, half, 2048, 1), TN, preferred_element_type=f32)
    my_row = (x * 2 + c) * 4
    sums = jnp.stack([jnp.sum(pick(loss_rows, my_row, 4)), jnp.sum(pick(scale_rows, my_row, 4))])
    tail = jnp.pad(sums[None], ((0, 7), (0, 2046)))
    total = jnp.concatenate([down_part / 128, up_part / 128, tail], axis=0)
    sides = [[i for i in range(128) if coords(i)[3] == side] for side in range(2)]
    swap = lambda value: lax.all_to_all(
        value, AX, 0, 0, axis_index_groups=sides, tiled=True
    )
    part = jnp.sum(swap(total.reshape(64, 1280)), axis=0, keepdims=True)
    total = swap(jnp.broadcast_to(part, (64, 1280))).reshape(40, 2048)
    mate = send(total, "core")
    loss = (total[32, 0] + mate[32, 0]) / 512
    scale_grad = (total[32, 1] + mate[32, 1]) / 512
    lora_down = ordered(c, total[:16], mate[:16], axis=1).T
    lora_up = ordered(c, total[16:32], mate[16:32], axis=1)

    p_sum = p_part
    for bit, n, move, name in (
        (y // 2, 64, "yflip", "r_y0"),
        (y % 2, 32, "ynear", "r_y1"),
        (z // 2, 16, "zflip", "r_z0"),
        (z % 2, 8, "znear", "r_z1"),
    ):
        got = send(pick(p_sum, n * (1 - bit), n), move)
        if name == "r_y0":
            got, p_sum, _ = lax.optimization_barrier((got, p_sum, stats_own))
        p_sum = pick(p_sum, n * bit, n) + got
    p_sum = logit_scale * p_sum
    keep = jnp.concatenate([pick(q_sum, 4 * c, 4), pick(p_sum, 4 * c, 4)], axis=0)
    give = jnp.concatenate([pick(q_sum, 4 * (1 - c), 4), pick(p_sum, 4 * (1 - c), 4)], axis=0)
    grads = ordered(c, keep, send(give, "core"), axis=1)
    return (
        loss,
        scale_grad,
        grads[:4],
        grads[4:],
        attn_grad[None],
        residual_grad[None],
        lora_down,
        lora_up,
    )


def solution(mesh):
    placed = (
        P(AX, None),
        P(AX, None),
        P(AX),
        P(),
        P(AX, None, None),
        P(AX, None, None),
        P("fsdp", None),
        P(),
        P(),
        P(),
        P(AX),
    )
    return jax.shard_map(
        compute,
        mesh=mesh,
        in_specs=placed,
        out_specs=(
            P(),
            P(),
            P(AX, None),
            P(AX, None),
            P(AX, None, None),
            P(AX, None, None),
            P(),
            P(),
        ),
        check_vma=False,
    )
```

profile of v0, /device:TPU:1, one launch (start us, length us, event | category | flops | bytes accessed | tf_op | source)
XLA Modules:
  0.0 259.4 jit_solution(10852104282042209915)
XLA Ops:
  1.8 3.4 %collective-permute-start = (bf16[512,256]{1,0:T(8,128)(2,1)S(1)}, bf16[512,256]{1,0:T(8,128)(2,1)S(1)}, u32[]{:S(2)}, u32[]{:S(2)}) collective-permute-start(bf16[512,256]{1,0:T(8,128)(2,1)S(1)} %get-tuple-element.41), channel_id=1, source_target_pairs={{0,20},{1,21},{2,22},{3,23},{4,16},{5,17},{6,18},{7,19},{8,28},{9,... | collective-permute-start | bytes 786440 | tf_op jit(solution)/shard_map/ppermute | solution.py:52
  8.7 2.3 constant_dynamic-slice_fusion.14
  20.0 3.7 %collective-permute-start.19 = (bf16[16,2048]{1,0:T(8,128)(2,1)S(1)}, bf16[16,2048]{1,0:T(8,128)(2,1)S(1)}, u32[]{:S(2)}, u32[]{:S(2)}) collective-permute-start(bf16[16,2048]{1,0:T(8,128)(2,1)S(1)} %maximum_select_fusion.9), channel_id=1, source_target_pairs={{0,3},{1,2},{2,1},{3,0},{4,7},{5,6},{6,5},{7,4},{8,11},{9,10},{10,... | collective-permute-start | bytes 196616 | tf_op jit(solution)/shard_map/ppermute | solution.py:52
  23.6 2.6 collective-permute-start.17
  27.6 11.0 %collective-permute-done.17 = bf16[16,2176]{1,0:T(8,128)(2,1)S(1)} collective-permute-done((bf16[16,2176]{1,0:T(8,128)(2,1)S(1)}, bf16[16,2176]{1,0:T(8,128)(2,1)S(1)}, u32[]{:S(2)}, u32[]{:S(2)}) %collective-permute-start.17) | collective-permute-done | bytes 69664 | tf_op jit(solution)/shard_map/ppermute | solution.py:52
  38.7 2.8 %collective-permute-start.21 = (bf16[64,2048]{1,0:T(8,128)(2,1)S(1)}, bf16[64,2048]{1,0:T(8,128)(2,1)S(1)}, u32[]{:S(2)}, u32[]{:S(2)}) collective-permute-start(bf16[64,2048]{1,0:T(8,128)(2,1)S(1)} %maximum_select_fusion.2), channel_id=1, source_target_pairs={{0,96},{1,97},{2,98},{3,99},{4,100},{5,101},{6,102},{7,103},{8,104... | collective-permute-start | bytes 786440 | tf_op jit(solution)/shard_map/ppermute | solution.py:52
  42.1 5.0 %collective-permute-done.21 = bf16[64,2048]{1,0:T(8,128)(2,1)S(1)} collective-permute-done((bf16[64,2048]{1,0:T(8,128)(2,1)S(1)}, bf16[64,2048]{1,0:T(8,128)(2,1)S(1)}, u32[]{:S(2)}, u32[]{:S(2)}) %collective-permute-start.21) | collective-permute-done | bytes 262176 | tf_op jit(solution)/shard_map/ppermute | solution.py:52
  50.8 2.2 collective-permute-start.2
  53.5 2.7 %collective-permute-done.23 = f32[4,32]{1,0:T(4,128)S(1)} collective-permute-done((f32[4,32]{1,0:T(4,128)S(1)}, f32[4,32]{1,0:T(4,128)S(1)}, u32[]{:S(2)}, u32[]{:S(2)}) %collective-permute-start.23) | collective-permute-done | bytes 544 | tf_op jit(solution)/shard_map/ppermute | solution.py:52
  56.8 3.5 %collective-permute-done.24 = f32[4,32]{1,0:T(4,128)S(1)} collective-permute-done((f32[4,32]{1,0:T(4,128)S(1)}, f32[4,32]{1,0:T(4,128)S(1)}, u32[]{:S(2)}, u32[]{:S(2)}) %collective-permute-start.24) | collective-permute-done | bytes 544 | tf_op jit(solution)/shard_map/ppermute | solution.py:52
  63.6 2.4 collective-permute-done.25
  66.1 4.7 %collective-permute-done.1.refs_7_ = bf16[1536,256]{1,0:T(8,128)(2,1)S(1)} collective-permute-done((bf16[1536,256]{1,0:T(8,128)(2,1)S(1)}, bf16[1536,256]{1,0:T(8,128)(2,1)S(1)}, u32[]{:S(2)}, u32[]{:S(2)}) %collective-permute-start.1) | collective-permute-done | bytes 786464 | tf_op jit(solution)/shard_map/ppermute | solution.py:52
  71.2 2.7 %collective-permute-start.4 = (bf16[768,256]{1,0:T(8,128)(2,1)S(1)}, bf16[768,256]{1,0:T(8,128)(2,1)S(1)}, u32[]{:S(2)}, u32[]{:S(2)}) collective-permute-start(bf16[768,256]{1,0:T(8,128)(2,1)S(1)} %pad_maximum_fusion.4), channel_id=1, source_target_pairs={{0,3},{1,0},{2,1},{3,2},{4,7},{5,4},{6,5},{7,6},{8,11},{9,8},{10,9... | collective-permute-start | bytes 1179656 | tf_op jit(solution)/shard_map/ppermute | solution.py:52
  74.0 8.3 %collective-permute-done.3.refs_9_ = bf16[768,256]{1,0:T(8,128)(2,1)S(1)} collective-permute-done((bf16[768,256]{1,0:T(8,128)(2,1)S(1)}, bf16[768,256]{1,0:T(8,128)(2,1)S(1)}, u32[]{:S(2)}, u32[]{:S(2)}) %collective-permute-start.3) | collective-permute-done | bytes 393248 | tf_op jit(solution)/shard_map/ppermute | solution.py:52
  86.3 2.7 %collective-permute-start.6 = (bf16[3584,256]{1,0:T(8,128)(2,1)S(1)}, bf16[3584,256]{1,0:T(8,128)(2,1)S(1)}, u32[]{:S(2)}, u32[]{:S(2)}) collective-permute-start(bf16[3584,256]{1,0:T(8,128)(2,1)S(1)} %slice_dynamic-update-slice_fusion.2.refs_1_), channel_id=1, source_target_pairs={{0,96},{1,97},{2,98},{3,99},{4,100},{5,101},{6,102},{7,103},{8,104... | collective-permute-start | bytes 5505032 | tf_op jit(solution)/shard_map/ppermute | solution.py:52
  91.2 2.8 %collective-permute-start.12 = (bf16[1024,768]{1,0:T(8,128)(2,1)S(1)}, bf16[1024,768]{1,0:T(8,128)(2,1)S(1)}, u32[]{:S(2)}, u32[]{:S(2)}) collective-permute-start(bf16[1024,768]{1,0:T(8,128)(2,1)S(1)} %pad_maximum_fusion), channel_id=1, source_target_pairs={{0,3},{1,0},{2,1},{3,2},{4,7},{5,4},{6,5},{7,6},{8,11},{9,8},{10,9... | collective-permute-start | bytes 4718600 | tf_op jit(solution)/shard_map/ppermute | solution.py:52
  94.2 29.6 %collective-permute-done.5.refs_2_ = bf16[3584,256]{1,0:T(8,128)(2,1)S(1)} collective-permute-done((bf16[3584,256]{1,0:T(8,128)(2,1)S(1)}, bf16[3584,256]{1,0:T(8,128)(2,1)S(1)}, u32[]{:S(2)}, u32[]{:S(2)}) %collective-permute-start.5) | collective-permute-done | bytes 1835040 | tf_op jit(solution)/shard_map/ppermute | solution.py:52
  123.8 2.3 collective-permute-start.28
  136.0 2.9 %collective-permute-start.14 = (bf16[512,768]{1,0:T(8,128)(2,1)}, bf16[512,768]{1,0:T(8,128)(2,1)}, u32[]{:S(2)}, u32[]{:S(2)}) collective-permute-start(bf16[512,768]{1,0:T(8,128)(2,1)} %slice.302), channel_id=1, source_target_pairs={{0,3},{1,0},{2,1},{3,2},{4,7},{5,4},{6,5},{7,6},{8,11},{9,8},{10,9... | collective-permute-start | bytes 2359304 | tf_op jit(solution)/shard_map/ppermute | solution.py:52
  139.8 14.4 %collective-permute-done.10.refs_11_ = bf16[1536,256]{1,0:T(8,128)(2,1)} collective-permute-done((bf16[1536,256]{1,0:T(8,128)(2,1)}, bf16[1536,256]{1,0:T(8,128)(2,1)}, u32[]{:S(2)}, u32[]{:S(2)}) %collective-permute-start.10) | collective-permute-done | bytes 786464 | tf_op jit(solution)/shard_map/ppermute | solution.py:52
  155.4 29.5 %block.1 = (f32[512,2048]{1,0:T(8,128)}, f32[528,128]{1,0:T(8,128)S(1)}, f32[256,4096]{1,0:T(8,128)}, bf16[256,4096]{1,0:T(8,128)(2,1)}, f32[16,4096]{1,0:T(8,128)S(1)}) custom-call(s32[13]{0:T(128)S(1)} %stack.86.scal, bf16[512,4096]{1,0:T(8,128)(2,1)} %refs_0_.1, bf16[3584,256]{1,0:T(8,128)(2,1)} %copy-done.23, bf16[3584,256]{1,0:T(8,128)(2,1)} %copy-done.17, ...), custom_call_target="tpu_custom_call" | custom-call | flops 17179869184 | bytes 33554432 | tf_op jit(solution)/shard_map/block/pallas_call | solution.py:139
  185.2 2.7 %collective-permute-start.29 = (f32[560,128]{1,0:T(8,128)S(1)}, f32[560,128]{1,0:T(8,128)S(1)}, u32[]{:S(2)}, u32[]{:S(2)}) collective-permute-start(f32[560,128]{1,0:T(8,128)S(1)} %pad_maximum_fusion.5), channel_id=1, source_target_pairs={{0,8},{1,9},{2,10},{3,11},{4,12},{5,13},{6,14},{7,15},{8,0},{9,1},... | collective-permute-start | bytes 860168 | tf_op jit(solution)/shard_map/ppermute | solution.py:52
  188.0 2.3 collective-permute-done.32
  191.1 2.8 %collective-permute-start.33 = (f32[16,2048]{1,0:T(8,128)}, f32[16,2048]{1,0:T(8,128)S(1)}, u32[]{:S(2)}, u32[]{:S(2)}) collective-permute-start(f32[16,2048]{1,0:T(8,128)} %constant_dynamic-slice_fusion.6), channel_id=1, source_target_pairs={{0,3},{1,2},{2,1},{3,0},{4,7},{5,6},{6,5},{7,4},{8,11},{9,10},{10,... | collective-permute-start | bytes 393224 | tf_op jit(solution)/shard_map/ppermute | solution.py:52
  202.7 6.1 %all-to-all-start = ((f32[64,1,1280]{2,1,0:T(1,128)}), f32[64,1,1280]{2,1,0:T(1,128)S(1)}, u32[]{:S(2)}, u32[]{:S(2)}) async-start(f32[64,1,1280]{2,1,0:T(1,128)} %all_to_all.13), calls=%async_computation | async-start | bytes 655360 | tf_op jit(solution)/shard_map/all_to_all | solution.py:380
  208.8 4.0 %collective-permute-start.37 = (bf16[256,2048]{1,0:T(8,128)(2,1)}, bf16[256,2048]{1,0:T(8,128)(2,1)}, u32[]{:S(2)}, u32[]{:S(2)}) collective-permute-start(bf16[256,2048]{1,0:T(8,128)(2,1)} %get-tuple-element.43), channel_id=1, source_target_pairs={{0,8},{1,9},{2,10},{3,11},{4,12},{5,13},{6,14},{7,15},{8,0},{9,1},... | collective-permute-start | bytes 3145736 | tf_op jit(solution)/shard_map/ppermute | solution.py:52
  214.5 2.9 %collective-permute-done.34 = f32[8,2048]{1,0:T(8,128)S(1)} collective-permute-done((f32[8,2048]{1,0:T(8,128)S(1)}, f32[8,2048]{1,0:T(8,128)S(1)}, u32[]{:S(2)}, u32[]{:S(2)}) %collective-permute-start.34) | collective-permute-done | bytes 65568 | tf_op jit(solution)/shard_map/ppermute | solution.py:52
  220.8 10.2 %all-to-all-start.1 = ((f32[64,1,1280]{2,1,0:T(1,128)}), f32[64,1,1280]{2,1,0:T(1,128)S(1)}, u32[]{:S(2)}, u32[]{:S(2)}) async-start(f32[64,1,1280]{2,1,0:T(1,128)} %broadcast_in_dim.102), calls=%async_computation.1 | async-start | bytes 655360 | tf_op jit(solution)/shard_map/all_to_all | solution.py:380
  231.7 9.1 %all-to-all-done.1 = f32[64,1,1280]{2,1,0:T(1,128)S(1)} async-done(((f32[64,1,1280]{2,1,0:T(1,128)}), f32[64,1,1280]{2,1,0:T(1,128)S(1)}, u32[]{:S(2)}, u32[]{:S(2)}) %all-to-all-start.1) | async-done | bytes 327712 | tf_op jit(solution)/shard_map/all_to_all | solution.py:380
  241.6 2.2 collective-permute-start.30
  249.2 3.8 %maximum_select_fusion = bf16[1,256,4096]{2,1,0:T(8,128)(2,1)} fusion(bf16[1,256,2048]{2,1,0:T(8,128)(2,1)} %bitcast.48, bf16[1,256,2048]{2,1,0:T(8,128)(2,1)S(1)} %copy-done.12, pred[]{:T(512)S(6)} %eq.71), kind=kLoop, calls=%fused_computation.10 | loop fusion | flops 9437184 | bytes 4194305 | tf_op jit(solution)/shard_map/jit(_where)/select_n | solution.py:56
  253.0 4.1 %fusion.3 = bf16[1,256,4096]{2,1,0:T(8,128)(2,1)} fusion(f32[256,4096]{1,0:T(8,128)S(1)} %copy-done.9, bf16[256,4096]{1,0:T(8,128)(2,1)} %collective-permute-done.36, f32[256]{0:T(256)S(1)} %slice.279, f32[4096]{0:T(1024)S(1)} %bitcast.164, f32[256]{0:T(256)S(1)} %slice.275, bf16[4096,16]{0,1:T(8,128)(2,1)S(1)} %copy-done, bf16[512,16]{1,0:T(8,128)(2,1)S(1)} %fusion.11), kind=kOutput, calls=%fused_computation.9 | convolution fusion | flops 40894464 | bytes 8603648 | tf_op jit(solution)/shard_map/dot_general | solution.py:368
  (244 shorter events, 59.0 us)
Async XLA Ops:
  1.8 47.2 %collective-permute-start = (bf16[512,256]{1,0:T(8,128)(2,1)S(1)}, bf16[512,256]{1,0:T(8,128)(2,1)S(1)}, u32[]{:S(2)}, u32[]{:S(2)}) collective-permute-start(bf16[512,256]{1,0:T(8,128)(2,1)S(1)} %get-tuple-element.41), channel_id=1, source_target_pairs={{0,20},{1,21},{2,22},{3,23},{4,16},{5,17},{6,18},{7,19},{8,28},{9,... | collective-permute-start | bytes 786440 | tf_op jit(solution)/shard_map/ppermute | solution.py:52
  7.7 6.8 %collective-permute-start.15 = (bf16[8,2176]{1,0:T(8,128)(2,1)S(1)}, bf16[8,2176]{1,0:T(8,128)(2,1)S(1)}, u32[]{:S(2)}, u32[]{:S(2)}) collective-permute-start(bf16[8,2176]{1,0:T(8,128)(2,1)S(1)} %get-tuple-element.73), channel_id=1, source_target_pairs={{0,8},{1,9},{2,10},{3,11},{4,12},{5,13},{6,14},{7,15},{8,0},{9,1},... | collective-permute-start | bytes 104456 | tf_op jit(solution)/shard_map/ppermute | solution.py:52
  11.0 78.0 %collective-permute-start.9 = (bf16[512,1024]{1,0:T(8,128)(2,1)}, bf16[512,1024]{1,0:T(8,128)(2,1)}, u32[]{:S(2)}, u32[]{:S(2)}) collective-permute-start(bf16[512,1024]{1,0:T(8,128)(2,1)} %constant_dynamic-slice_fusion.14), channel_id=1, source_target_pairs={{0,20},{1,21},{2,22},{3,23},{4,16},{5,17},{6,18},{7,19},{8,28},{9,... | collective-permute-start | bytes 3145736 | tf_op jit(solution)/shard_map/ppermute | solution.py:52
  20.0 6.2 %collective-permute-start.19 = (bf16[16,2048]{1,0:T(8,128)(2,1)S(1)}, bf16[16,2048]{1,0:T(8,128)(2,1)S(1)}, u32[]{:S(2)}, u32[]{:S(2)}) collective-permute-start(bf16[16,2048]{1,0:T(8,128)(2,1)S(1)} %maximum_select_fusion.9), channel_id=1, source_target_pairs={{0,3},{1,2},{2,1},{3,0},{4,7},{5,6},{6,5},{7,4},{8,11},{9,10},{10,... | collective-permute-start | bytes 196616 | tf_op jit(solution)/shard_map/ppermute | solution.py:52
  23.6 14.9 %collective-permute-start.17 = (bf16[16,2176]{1,0:T(8,128)(2,1)S(1)}, bf16[16,2176]{1,0:T(8,128)(2,1)S(1)}, u32[]{:S(2)}, u32[]{:S(2)}) collective-permute-start(bf16[16,2176]{1,0:T(8,128)(2,1)S(1)} %maximum_select_fusion.8), channel_id=1, source_target_pairs={{0,20},{1,21},{2,22},{3,23},{4,16},{5,17},{6,18},{7,19},{8,28},{9,... | collective-permute-start | bytes 208904 | tf_op jit(solution)/shard_map/ppermute | solution.py:52
  26.2 12.4 %collective-permute-start.20 = (bf16[32,2048]{1,0:T(8,128)(2,1)S(1)}, bf16[32,2048]{1,0:T(8,128)(2,1)S(1)}, u32[]{:S(2)}, u32[]{:S(2)}) collective-permute-start(bf16[32,2048]{1,0:T(8,128)(2,1)S(1)} %maximum_select_fusion.6), channel_id=1, source_target_pairs={{0,32},{1,33},{2,34},{3,35},{4,36},{5,37},{6,38},{7,39},{8,40},{9,... | collective-permute-start | bytes 393224 | tf_op jit(solution)/shard_map/ppermute | solution.py:52
  38.7 8.4 %collective-permute-start.21 = (bf16[64,2048]{1,0:T(8,128)(2,1)S(1)}, bf16[64,2048]{1,0:T(8,128)(2,1)S(1)}, u32[]{:S(2)}, u32[]{:S(2)}) collective-permute-start(bf16[64,2048]{1,0:T(8,128)(2,1)S(1)} %maximum_select_fusion.2), channel_id=1, source_target_pairs={{0,96},{1,97},{2,98},{3,99},{4,100},{5,101},{6,102},{7,103},{8,104... | collective-permute-start | bytes 786440 | tf_op jit(solution)/shard_map/ppermute | solution.py:52
  47.3 5.7 %collective-permute-start.22 = (f32[32,128]{1,0:T(8,128)S(1)}, f32[32,128]{1,0:T(8,128)S(1)}, u32[]{:S(2)}, u32[]{:S(2)}) collective-permute-start(f32[32,128]{1,0:T(8,128)S(1)} %fusion.19), channel_id=1, source_target_pairs={{0,8},{1,9},{2,10},{3,11},{4,12},{5,13},{6,14},{7,15},{8,0},{9,1},... | collective-permute-start | bytes 49160 | tf_op jit(solution)/shard_map/ppermute | solution.py:52
  49.1 21.7 %collective-permute-start.1 = (bf16[1536,256]{1,0:T(8,128)(2,1)S(1)}, bf16[1536,256]{1,0:T(8,128)(2,1)S(1)}, u32[]{:S(2)}, u32[]{:S(2)}) collective-permute-start(bf16[1536,256]{1,0:T(8,128)(2,1)S(1)} %pad_maximum_fusion.1), channel_id=1, source_target_pairs={{0,1},{1,2},{2,3},{3,0},{4,5},{5,6},{6,7},{7,4},{8,9},{9,10},{10,1... | collective-permute-start | bytes 2359304 | tf_op jit(solution)/shard_map/ppermute | solution.py:52
  50.8 20.2 %collective-permute-start.2 = (bf16[1536,256]{1,0:T(8,128)(2,1)S(1)}, bf16[1536,256]{1,0:T(8,128)(2,1)S(1)}, u32[]{:S(2)}, u32[]{:S(2)}) collective-permute-start(bf16[1536,256]{1,0:T(8,128)(2,1)S(1)} %pad_maximum_fusion.1), channel_id=1, source_target_pairs={{0,3},{1,0},{2,1},{3,2},{4,7},{5,4},{6,5},{7,6},{8,11},{9,8},{10,9... | collective-permute-start | bytes 2359304 | tf_op jit(solution)/shard_map/ppermute | solution.py:52
  60.6 5.4 %collective-permute-start.25 = (f32[16,2048]{1,0:T(8,128)S(1)}, f32[16,2048]{1,0:T(8,128)S(1)}, u32[]{:S(2)}, u32[]{:S(2)}) collective-permute-start(f32[16,2048]{1,0:T(8,128)S(1)} %constant_dynamic-slice_fusion.13), channel_id=1, source_target_pairs={{0,20},{1,21},{2,22},{3,23},{4,16},{5,17},{6,18},{7,19},{8,28},{9,... | collective-permute-start | bytes 393224 | tf_op jit(solution)/shard_map/ppermute | solution.py:52
  66.0 18.5 %collective-permute-start.26 = (f32[8,2048]{1,0:T(8,128)S(1)}, f32[8,2048]{1,0:T(8,128)S(1)}, u32[]{:S(2)}, u32[]{:S(2)}) collective-permute-start(f32[8,2048]{1,0:T(8,128)S(1)} %constant_dynamic-slice_fusion.12), channel_id=1, source_target_pairs={{0,16},{1,17},{2,18},{3,19},{4,20},{5,21},{6,22},{7,23},{8,24},{9,... | collective-permute-start | bytes 196616 | tf_op jit(solution)/shard_map/ppermute | solution.py:52
  70.9 11.4 %collective-permute-start.3 = (bf16[768,256]{1,0:T(8,128)(2,1)S(1)}, bf16[768,256]{1,0:T(8,128)(2,1)S(1)}, u32[]{:S(2)}, u32[]{:S(2)}) collective-permute-start(bf16[768,256]{1,0:T(8,128)(2,1)S(1)} %pad_maximum_fusion.3), channel_id=1, source_target_pairs={{0,1},{1,2},{2,3},{3,0},{4,5},{5,6},{6,7},{7,4},{8,9},{9,10},{10,1... | collective-permute-start | bytes 1179656 | tf_op jit(solution)/shard_map/ppermute | solution.py:52
  71.2 11.2 %collective-permute-start.4 = (bf16[768,256]{1,0:T(8,128)(2,1)S(1)}, bf16[768,256]{1,0:T(8,128)(2,1)S(1)}, u32[]{:S(2)}, u32[]{:S(2)}) collective-permute-start(bf16[768,256]{1,0:T(8,128)(2,1)S(1)} %pad_maximum_fusion.4), channel_id=1, source_target_pairs={{0,3},{1,0},{2,1},{3,2},{4,7},{5,4},{6,5},{7,6},{8,11},{9,8},{10,9... | collective-permute-start | bytes 1179656 | tf_op jit(solution)/shard_map/ppermute | solution.py:52
  82.4 41.4 %collective-permute-start.5 = (bf16[3584,256]{1,0:T(8,128)(2,1)S(1)}, bf16[3584,256]{1,0:T(8,128)(2,1)S(1)}, u32[]{:S(2)}, u32[]{:S(2)}) collective-permute-start(bf16[3584,256]{1,0:T(8,128)(2,1)S(1)} %slice_dynamic-update-slice_fusion.2.refs_1_), channel_id=1, source_target_pairs={{0,32},{1,33},{2,34},{3,35},{4,36},{5,37},{6,38},{7,39},{8,40},{9,... | collective-permute-start | bytes 5505032 | tf_op jit(solution)/shard_map/ppermute | solution.py:52
  84.5 51.5 %collective-permute-start.27 = (bf16[256,4096]{1,0:T(8,128)(2,1)S(1)}, bf16[256,4096]{1,0:T(8,128)(2,1)S(1)}, u32[]{:S(2)}, u32[]{:S(2)}) collective-permute-start(bf16[256,4096]{1,0:T(8,128)(2,1)S(1)} %bitcast.157), channel_id=1, source_target_pairs={{0,8},{1,9},{2,10},{3,11},{4,12},{5,13},{6,14},{7,15},{8,0},{9,1},... | collective-permute-start | bytes 6291464 | tf_op jit(solution)/shard_map/ppermute | solution.py:52
  86.3 42.0 %collective-permute-start.6 = (bf16[3584,256]{1,0:T(8,128)(2,1)S(1)}, bf16[3584,256]{1,0:T(8,128)(2,1)S(1)}, u32[]{:S(2)}, u32[]{:S(2)}) collective-permute-start(bf16[3584,256]{1,0:T(8,128)(2,1)S(1)} %slice_dynamic-update-slice_fusion.2.refs_1_), channel_id=1, source_target_pairs={{0,96},{1,97},{2,98},{3,99},{4,100},{5,101},{6,102},{7,103},{8,104... | collective-permute-start | bytes 5505032 | tf_op jit(solution)/shard_map/ppermute | solution.py:52
  90.5 40.6 %collective-permute-start.11 = (bf16[1024,768]{1,0:T(8,128)(2,1)S(1)}, bf16[1024,768]{1,0:T(8,128)(2,1)S(1)}, u32[]{:S(2)}, u32[]{:S(2)}) collective-permute-start(bf16[1024,768]{1,0:T(8,128)(2,1)S(1)} %pad_maximum_fusion), channel_id=1, source_target_pairs={{0,1},{1,2},{2,3},{3,0},{4,5},{5,6},{6,7},{7,4},{8,9},{9,10},{10,1... | collective-permute-start | bytes 4718600 | tf_op jit(solution)/shard_map/ppermute | solution.py:52
  91.2 43.5 %collective-permute-start.12 = (bf16[1024,768]{1,0:T(8,128)(2,1)S(1)}, bf16[1024,768]{1,0:T(8,128)(2,1)S(1)}, u32[]{:S(2)}, u32[]{:S(2)}) collective-permute-start(bf16[1024,768]{1,0:T(8,128)(2,1)S(1)} %pad_maximum_fusion), channel_id=1, source_target_pairs={{0,3},{1,0},{2,1},{3,2},{4,7},{5,4},{6,5},{7,6},{8,11},{9,8},{10,9... | collective-permute-start | bytes 4718600 | tf_op jit(solution)/shard_map/ppermute | solution.py:52
  123.8 12.1 %collective-permute-start.28 = (bf16[256,2048]{1,0:T(8,128)(2,1)S(1)}, bf16[256,2048]{1,0:T(8,128)(2,1)S(1)}, u32[]{:S(2)}, u32[]{:S(2)}) collective-permute-start(bf16[256,2048]{1,0:T(8,128)(2,1)S(1)} %constant_dynamic-slice_fusion.11), channel_id=1, source_target_pairs={{0,8},{1,9},{2,10},{3,11},{4,12},{5,13},{6,14},{7,15},{8,0},{9,1},... | collective-permute-start | bytes 3145736 | tf_op jit(solution)/shard_map/ppermute | solution.py:52
  128.2 27.1 %collective-permute-start.7 = (bf16[1792,256]{1,0:T(8,128)(2,1)}, bf16[1792,256]{1,0:T(8,128)(2,1)}, u32[]{:S(2)}, u32[]{:S(2)}) collective-permute-start(bf16[1792,256]{1,0:T(8,128)(2,1)} %slice.294), channel_id=1, source_target_pairs={{0,32},{1,33},{2,34},{3,35},{4,36},{5,37},{6,38},{7,39},{8,40},{9,... | collective-permute-start | bytes 2752520 | tf_op jit(solution)/shard_map/ppermute | solution.py:52
  131.1 24.3 %collective-permute-start.8 = (bf16[1792,256]{1,0:T(8,128)(2,1)}, bf16[1792,256]{1,0:T(8,128)(2,1)}, u32[]{:S(2)}, u32[]{:S(2)}) collective-permute-start(bf16[1792,256]{1,0:T(8,128)(2,1)} %slice.295), channel_id=1, source_target_pairs={{0,96},{1,97},{2,98},{3,99},{4,100},{5,101},{6,102},{7,103},{8,104... | collective-permute-start | bytes 2752520 | tf_op jit(solution)/shard_map/ppermute | solution.py:52
  134.7 19.5 %collective-permute-start.10 = (bf16[1536,256]{1,0:T(8,128)(2,1)}, bf16[1536,256]{1,0:T(8,128)(2,1)}, u32[]{:S(2)}, u32[]{:S(2)}) collective-permute-start(bf16[1536,256]{1,0:T(8,128)(2,1)} %pad_maximum_fusion.2), channel_id=1, source_target_pairs={{0,20},{1,21},{2,22},{3,23},{4,16},{5,17},{6,18},{7,19},{8,28},{9,... | collective-permute-start | bytes 2359304 | tf_op jit(solution)/shard_map/ppermute | solution.py:52
  135.9 19.5 %collective-permute-start.13 = (bf16[512,768]{1,0:T(8,128)(2,1)}, bf16[512,768]{1,0:T(8,128)(2,1)}, u32[]{:S(2)}, u32[]{:S(2)}) collective-permute-start(bf16[512,768]{1,0:T(8,128)(2,1)} %slice.301), channel_id=1, source_target_pairs={{0,1},{1,2},{2,3},{3,0},{4,5},{5,6},{6,7},{7,4},{8,9},{9,10},{10,1... | collective-permute-start | bytes 2359304 | tf_op jit(solution)/shard_map/ppermute | solution.py:52
  136.0 19.4 %collective-permute-start.14 = (bf16[512,768]{1,0:T(8,128)(2,1)}, bf16[512,768]{1,0:T(8,128)(2,1)}, u32[]{:S(2)}, u32[]{:S(2)}) collective-permute-start(bf16[512,768]{1,0:T(8,128)(2,1)} %slice.302), channel_id=1, source_target_pairs={{0,3},{1,0},{2,1},{3,2},{4,7},{5,4},{6,5},{7,6},{8,11},{9,8},{10,9... | collective-permute-start | bytes 2359304 | tf_op jit(solution)/shard_map/ppermute | solution.py:52
  154.2 30.7 %collective-permute-start.31 = (f32[64,2048]{1,0:T(8,128)}, f32[64,2048]{1,0:T(8,128)S(1)}, u32[]{:S(2)}, u32[]{:S(2)}) collective-permute-start(f32[64,2048]{1,0:T(8,128)} %constant_dynamic-slice_fusion.8), channel_id=1, source_target_pairs={{0,96},{1,97},{2,98},{3,99},{4,100},{5,101},{6,102},{7,103},{8,104... | collective-permute-start | bytes 1572872 | tf_op jit(solution)/shard_map/ppermute | solution.py:52
  185.2 8.6 %collective-permute-start.29 = (f32[560,128]{1,0:T(8,128)S(1)}, f32[560,128]{1,0:T(8,128)S(1)}, u32[]{:S(2)}, u32[]{:S(2)}) collective-permute-start(f32[560,128]{1,0:T(8,128)S(1)} %pad_maximum_fusion.5), channel_id=1, source_target_pairs={{0,8},{1,9},{2,10},{3,11},{4,12},{5,13},{6,14},{7,15},{8,0},{9,1},... | collective-permute-start | bytes 860168 | tf_op jit(solution)/shard_map/ppermute | solution.py:52
  187.9 65.1 %collective-permute-start.36 = (bf16[256,4096]{1,0:T(8,128)(2,1)}, bf16[256,4096]{1,0:T(8,128)(2,1)}, u32[]{:S(2)}, u32[]{:S(2)}) collective-permute-start(bf16[256,4096]{1,0:T(8,128)(2,1)} %get-tuple-element.25), channel_id=1, source_target_pairs={{0,8},{1,9},{2,10},{3,11},{4,12},{5,13},{6,14},{7,15},{8,0},{9,1},... | collective-permute-start | bytes 6291464 | tf_op jit(solution)/shard_map/ppermute | solution.py:52
  191.1 21.8 %collective-permute-start.33 = (f32[16,2048]{1,0:T(8,128)}, f32[16,2048]{1,0:T(8,128)S(1)}, u32[]{:S(2)}, u32[]{:S(2)}) collective-permute-start(f32[16,2048]{1,0:T(8,128)} %constant_dynamic-slice_fusion.6), channel_id=1, source_target_pairs={{0,3},{1,2},{2,1},{3,0},{4,7},{5,6},{6,5},{7,4},{8,11},{9,10},{10,... | collective-permute-start | bytes 393224 | tf_op jit(solution)/shard_map/ppermute | solution.py:52
  202.7 17.0 %all-to-all-start = ((f32[64,1,1280]{2,1,0:T(1,128)}), f32[64,1,1280]{2,1,0:T(1,128)S(1)}, u32[]{:S(2)}, u32[]{:S(2)}) async-start(f32[64,1,1280]{2,1,0:T(1,128)} %all_to_all.13), calls=%async_computation | async-start | bytes 655360 | tf_op jit(solution)/shard_map/all_to_all | solution.py:380
  208.8 40.4 %collective-permute-start.37 = (bf16[256,2048]{1,0:T(8,128)(2,1)}, bf16[256,2048]{1,0:T(8,128)(2,1)}, u32[]{:S(2)}, u32[]{:S(2)}) collective-permute-start(bf16[256,2048]{1,0:T(8,128)(2,1)} %get-tuple-element.43), channel_id=1, source_target_pairs={{0,8},{1,9},{2,10},{3,11},{4,12},{5,13},{6,14},{7,15},{8,0},{9,1},... | collective-permute-start | bytes 3145736 | tf_op jit(solution)/shard_map/ppermute | solution.py:52
  220.8 20.0 %all-to-all-start.1 = ((f32[64,1,1280]{2,1,0:T(1,128)}), f32[64,1,1280]{2,1,0:T(1,128)S(1)}, u32[]{:S(2)}, u32[]{:S(2)}) async-start(f32[64,1,1280]{2,1,0:T(1,128)} %broadcast_in_dim.102), calls=%async_computation.1 | async-start | bytes 655360 | tf_op jit(solution)/shard_map/all_to_all | solution.py:380
  (40 other events, 564.4 us)
where the time goes:
time: 260 us; the launch traced here: 259 us
  waiting for transfers between devices  99.3 us (38%)
  starting transfers between devices  74.6 us (29%)
  Pallas kernels  29.5 us (11%)
  local copies, waits for them, and re-layouts  22.9 us (9%)
  other arithmetic  15 us (6%)
  matrix products  9.4 us (4%)
  between operations  8.83 us (3%)
    ppermute x38, waiting for transfers between devices, send(): return lax.ppermute(value, AX, MOVES[move])  90.2 us
    ppermute x38, starting transfers between devices, send(): return lax.ppermute(value, AX, MOVES[move])  58.3 us
    pallas_call x1, Pallas kernels, block_call(): pl.pallas_call(functools.partial(block_kernel, copies), out_shape=[jax.Sh...  29.5 us
    all_to_all x2, starting transfers between devices, compute(): lax.all_to_all(value, AX, 0, 0, axis_index_groups=sides, tiled=True)  16.3 us
    all_to_all x2, waiting for transfers between devices, compute(): lax.all_to_all(value, AX, 0, 0, axis_index_groups=sides, tiled=True)  9.1 us
  transfers between devices with their start and end apart: 40, of which 17 were waited for; matrix products, arithmetic and copies ran while one was open for 15% of the time, Pallas kernels for 11%

commit v1 on v0

--- a/solution.py
+++ b/solution.py
@@ -64,107 +64,150 @@
     return lax.dynamic_slice_in_dim(value, start, size, axis=axis)
 
 
-def block_kernel(copies, scal, *refs):
-    n_src = 1 + max(src for src, *_ in copies)
+def block_kernel(copies, n_src, first, scal, *refs):
     srcs = refs[:n_src]
     a_own, a_par, r_own, r_par, low, up, q_rows, q_f = refs[n_src : n_src + 8]
-    hid_out, st_out, y_own, y_par, y_q = refs[n_src + 8 : n_src + 13]
-    w_s, a_s, r_s, hid, hb_s, yo_s, yp_s, w_sem, in_sem, out_sem = refs[n_src + 13 :]
+    rest = refs[n_src + 8 :]
+    if first:
+        hid_out, st_out, y_out = rest[:3]
+        w_s, a_s, r_s, hid, hb_s, y_s, w_sem, in_sem, out_sem = rest[3:]
+    else:
+        y_in, st_in, _, hid_out, st_out, y_own, y_par, y_q = rest[:8]
+        w_s, a_s, r_s, hid, hb_s, y_s, w_sem, in_sem, out_sem, yo_s, yp_s = rest[8:]
     half = pl.multiple_of(scal[12], 2048)
     inputs = [
         pltpu.make_async_copy(a_own, a_s.at[pl.ds(0, 256), :], in_sem.at[0]),
         pltpu.make_async_copy(a_par, a_s.at[pl.ds(256, 256), :], in_sem.at[1]),
-        pltpu.make_async_copy(r_own.at[:, pl.ds(half, 2048)], r_s.at[pl.ds(0, 256), :], in_sem.at[2]),
-        pltpu.make_async_copy(r_par, r_s.at[pl.ds(256, 256), :], in_sem.at[3]),
     ]
+    for j in range(4):
+        col = pl.multiple_of(scal[8 + j] * 256, 256)
+        here = pl.ds(j * 256, 256)
+        far = pl.ds(pl.multiple_of(half + col, 256), 256)
+        inputs.append(
+            pltpu.make_async_copy(
+                r_own.at[:, far], r_s.at[pl.ds(0, 256), here], in_sem.at[2 + 2 * j]
+            )
+        )
+        inputs.append(
+            pltpu.make_async_copy(
+                r_par.at[:, pl.ds(col, 256)], r_s.at[pl.ds(256, 256), here], in_sem.at[3 + 2 * j]
+            )
+        )
     for copy in inputs:
         copy.start()
-    for src, src_row, src_col, rows, shard, dst_row, dst_col, cols in copies:
-        ref = srcs[src]
-        if src_col is None:
-            view = ref.at[pl.ds(src_row, rows), :]
+    for src, src_row, src_col, from_half, rows, shard, dst_row, block in copies:
+        if from_half:
+            col = half + pl.multiple_of(scal[8 + block] * 256, 256)
         else:
-            view = ref.at[pl.ds(src_row, rows), pl.ds(pl.multiple_of(scal[src_col], 256), cols)]
-        first = pl.multiple_of(scal[shard] * 512 + dst_row, 256)
-        if isinstance(dst_col, tuple):
-            col = pl.multiple_of(scal[dst_col[0]] * 256, 256)
-        else:
-            col = dst_col
+            col = src_col
+        row = pl.multiple_of(scal[shard] * 512 + dst_row, 256)
         pltpu.make_async_copy(
-            view, w_s.at[pl.ds(first, rows), pl.ds(col, cols)], w_sem.at[shard]
+            srcs[src].at[pl.ds(src_row, rows), pl.ds(col, 256)],
+            w_s.at[pl.ds(row, rows), pl.ds(block * 256, 256)],
+            w_sem.at[block],
         ).start()
+    if not first:
+        y_copy = pltpu.make_async_copy(y_in, y_s, in_sem.at[10])
+        y_copy.start()
     for copy in inputs:
         copy.wait()
-    hid[...] = r_s[...].astype(f32) + adapter_scale * jnp.dot(
-        low[...], up[...], preferred_element_type=f32
-    )
-
-    def forward(shard, carry):
-        rows = pl.ds(pl.multiple_of(scal[shard] * 512, 512), 512)
-        pltpu.make_async_copy(w_s.at[rows, :], w_s.at[rows, :], w_sem.at[shard]).wait()
-        hid[...] += jnp.dot(a_s[:, rows], w_s[rows, :], preferred_element_type=f32)
+    st_out[...] = jnp.zeros_like(st_out) if first else st_in[...]
+
+    def forward(j, carry):
+        here = pl.ds(pl.multiple_of(j * 256, 256), 256)
+        col = pl.ds(pl.multiple_of(scal[8 + j] * 256, 256), 256)
+        pltpu.make_async_copy(w_s.at[:, here], w_s.at[:, here], w_sem.at[j]).wait()
+        value = (
+            r_s[:, here].astype(f32)
+            + adapter_scale * jnp.dot(low[...], up[:, col], preferred_element_type=f32)
+            + jnp.dot(a_s[...], w_s[:, here], preferred_element_type=f32)
+        )
+        hid[:, here] = value
+        pltpu.make_async_copy(hid.at[:, here], hid_out.at[:, col], out_sem.at[2]).start()
+        hb_s[pl.ds(0, 512), here] = value.astype(bf16)
+        hb_s[pl.ds(512, 16), here] = q_rows[:, col]
+        st_out[:, 0:16] += lax.dot_general(
+            hb_s[:, here], up[:, col], NT, preferred_element_type=f32
+        )
+        st_out[0:512, 16:17] += jnp.sum(value * value, axis=1, keepdims=True)
+        st_out[0:256, 17:18] += jnp.sum(value[:256] * q_f[0:1, col], axis=1, keepdims=True)
+        st_out[256:512, 17:18] += jnp.sum(value[256:] * q_f[1:2, col], axis=1, keepdims=True)
         return carry
 
-    lax.fori_loop(0, 8, forward, 0)
-    hid_copy = pltpu.make_async_copy(hid, hid_out, out_sem.at[2])
-    hid_copy.start()
-    value = hid[...]
-    hb_s[pl.ds(0, 512), :] = value.astype(bf16)
-    hb_s[pl.ds(512, 16), :] = q_rows[...]
-    st_out[...] = jnp.zeros_like(st_out)
-    st_out[:, 0:16] = lax.dot_general(hb_s[...], up[...], NT, preferred_element_type=f32)
-    st_out[0:512, 16:17] = jnp.sum(value * value, axis=1, keepdims=True)
-    st_out[0:256, 17:18] = jnp.sum(value[:256] * q_f[0:1, :], axis=1, keepdims=True)
-    st_out[256:512, 17:18] = jnp.sum(value[256:] * q_f[1:2, :], axis=1, keepdims=True)
+    lax.fori_loop(0, 4, forward, 0)
+    if not first:
+        y_copy.wait()
 
     def backward(shard, carry):
         columns = pl.ds(pl.multiple_of(scal[shard] * 512, 512), 512)
         part = lax.dot_general(hb_s[...], w_s[columns, :], NT, preferred_element_type=f32)
-        yo_s[:, columns] = part[:256]
-        yp_s[:, columns] = part[256:512].astype(bf16)
-        y_q[:, columns] = part[512:]
-        pltpu.make_async_copy(yo_s.at[:, columns], y_own.at[:, columns], out_sem.at[0]).start()
-        pltpu.make_async_copy(yp_s.at[:, columns], y_par.at[:, columns], out_sem.at[1]).start()
+        if first:
+            y_s[:, columns] = part
+            pltpu.make_async_copy(y_s.at[:, columns], y_out.at[:, columns], out_sem.at[0]).start()
+        else:
+            part += y_s[:, columns]
+            yo_s[:, columns] = part[:256]
+            yp_s[:, columns] = part[256:512].astype(bf16)
+            y_q[:, columns] = part[512:]
+            pltpu.make_async_copy(yo_s.at[:, columns], y_own.at[:, columns], out_sem.at[0]).start()
+            pltpu.make_async_copy(yp_s.at[:, columns], y_par.at[:, columns], out_sem.at[1]).start()
         return carry
 
     lax.fori_loop(0, 8, backward, 0)
-    pltpu.make_async_copy(yo_s, y_own, out_sem.at[0]).wait()
-    pltpu.make_async_copy(yp_s, y_par, out_sem.at[1]).wait()
-    hid_copy.wait()
-
-
-def block_call(copies, srcs, scal, a_own, a_par, r_own, r_par, low, up, q_rows, q_f):
+    if first:
+        pltpu.make_async_copy(y_s, y_out, out_sem.at[0]).wait()
+    else:
+        pltpu.make_async_copy(yo_s, y_own, out_sem.at[0]).wait()
+        pltpu.make_async_copy(yp_s, y_par, out_sem.at[1]).wait()
+    pltpu.make_async_copy(hid, hid, out_sem.at[2]).wait()
+
+
+def block_call(copies, srcs, scal, a_own, a_par, r_own, r_par, low, up, q_rows, q_f, carry):
     vm = pl.BlockSpec(memory_space=pltpu.VMEM)
     anyspace = pl.BlockSpec(memory_space=pl.ANY)
-    return pl.pallas_call(
-        functools.partial(block_kernel, copies),
-        out_shape=[
-            jax.ShapeDtypeStruct((512, 2048), f32),
-            jax.ShapeDtypeStruct((528, 128), f32),
+    first = carry is None
+    shapes = [jax.ShapeDtypeStruct((512, 2048), f32), jax.ShapeDtypeStruct((528, 128), f32)]
+    args = [scal, *srcs, a_own, a_par, r_own, r_par, low, up, q_rows, q_f]
+    in_specs = [pl.BlockSpec(memory_space=pltpu.SMEM)] + [anyspace] * (len(srcs) + 4) + [vm] * 4
+    scratch = [
+        pltpu.VMEM((4096, 1024), bf16),
+        pltpu.VMEM((512, 4096), bf16),
+        pltpu.VMEM((512, 1024), bf16),
+        pltpu.VMEM((512, 1024), f32),
+        pltpu.VMEM((528, 1024), bf16),
+        pltpu.VMEM((528, 4096), f32),
+        pltpu.SemaphoreType.DMA((4,)),
+        pltpu.SemaphoreType.DMA((11,)),
+        pltpu.SemaphoreType.DMA((3,)),
+    ]
+    if first:
+        shapes += [jax.ShapeDtypeStruct((528, 4096), f32)]
+        out_specs = [anyspace, vm, anyspace]
+        aliases = {}
+    else:
+        shapes += [
             jax.ShapeDtypeStruct((256, 4096), f32),
             jax.ShapeDtypeStruct((256, 4096), bf16),
             jax.ShapeDtypeStruct((16, 4096), f32),
-        ],
-        in_specs=[pl.BlockSpec(memory_space=pltpu.SMEM)] + [anyspace] * (len(srcs) + 4) + [vm] * 4,
-        out_specs=[anyspace, vm, anyspace, anyspace, vm],
-        scratch_shapes=[
-            pltpu.VMEM((4096, 2048), bf16),
-            pltpu.VMEM((512, 4096), bf16),
-            pltpu.VMEM((512, 2048), bf16),
-            pltpu.VMEM((512, 2048), f32),
-            pltpu.VMEM((528, 2048), bf16),
-            pltpu.VMEM((256, 4096), f32),
-            pltpu.VMEM((256, 4096), bf16),
-            pltpu.SemaphoreType.DMA((8,)),
-            pltpu.SemaphoreType.DMA((4,)),
-            pltpu.SemaphoreType.DMA((3,)),
-        ],
-        compiler_params=pltpu.CompilerParams(vmem_limit_bytes=48 * 1024 * 1024),
+        ]
+        out_specs = [anyspace, vm, anyspace, anyspace, vm]
+        scratch += [pltpu.VMEM((256, 4096), f32), pltpu.VMEM((256, 4096), bf16)]
+        in_specs += [anyspace, vm, anyspace]
+        args += [carry[2], carry[1], carry[0]]
+        aliases = {len(args) - 1: 0}
+    return pl.pallas_call(
+        functools.partial(block_kernel, copies, len(srcs), first),
+        out_shape=shapes,
+        in_specs=in_specs,
+        out_specs=out_specs,
+        scratch_shapes=scratch,
+        input_output_aliases=aliases,
+        compiler_params=pltpu.CompilerParams(vmem_limit_bytes=44 * 1024 * 1024),
         cost_estimate=pl.CostEstimate(
-            flops=4 * 512 * 4096 * 2048, transcendentals=0, bytes_accessed=32 << 20
+            flops=4 * 512 * 4096 * 1024, transcendentals=0, bytes_accessed=24 << 20
         ),
-        name="block",
-    )(scal, *srcs, a_own, a_par, r_own, r_par, low, up, q_rows, q_f)
+        name="block_first" if first else "block_last",
+    )(*args)
 
 
 REL = [(0, 0), (0, -1), (0, 1), (0, 2), (1, 0), (1, -1), (1, 1), (1, 2)]
@@ -216,23 +259,25 @@
     o_g = send(s_g, "xflip")
     o_ab = send(s_ab, "xflip")
 
-    p_blk = ordered(z % 2, p_chip, send(p_chip, "znear"))
+    p_blk = ordered(y % 2, p_chip, send(p_chip, "ynear"))
+    p_blk = ordered(y // 2, p_blk, send(p_blk, "yflip"))
+    p_blk = ordered(z % 2, p_blk, send(p_blk, "znear"))
     p_blk = ordered(z // 2, p_blk, send(p_blk, "zflip"))
-    p_blk = ordered(y % 2, p_blk, send(p_blk, "ynear"))
-    p_blk = ordered(y // 2, p_blk, send(p_blk, "yflip"))
     q_blk = ordered(x % 2, q_chip, send(q_chip, "xnear"))
-    q_blk = ordered(x // 2, q_blk, send(q_blk, "xflip"))
+    q_far, q_blk, _ = lax.optimization_barrier((send(q_blk, "xflip"), q_blk, p_blk))
+    q_blk = ordered(x // 2, q_blk, q_far)
 
     ga = jnp.concatenate([s_g, o_g, s_ab[:, :256]], axis=0)
     up0 = send(ga, "zup")
     dn0 = send(ga, "zdown")
     up1 = send(jnp.concatenate([up0[:512], up0[1024:1280]], axis=0), "zup")
     dn1 = send(jnp.concatenate([dn0[512:1024], dn0[1280:]], axis=0), "zdown")
-    y0 = jnp.concatenate([o_g, up0[:1024], dn0[:1024], up1[:512], dn1[:512]], axis=0)
-    y_up = send(y0, "yup")
-    y_dn = send(y0, "ydown")
-    y_far0 = send(y_up[:1792], "yup")
-    y_far1 = send(y_dn[1792:], "ydown")
+    ya = jnp.concatenate([o_g, up0[:1024], dn0[:1024]], axis=0)
+    yb = jnp.concatenate([up1[:512], dn1[:512]], axis=0)
+    ya_u, ya_d = send(ya, "yup"), send(ya, "ydown")
+    yb_u, yb_d = send(yb, "yup"), send(yb, "ydown")
+    y_far0 = send(ya_u[:1792], "yup")
+    y_far1 = send(jnp.concatenate([ya_d[1792:], yb_d], axis=0), "ydown")
     a_x = send(jnp.concatenate([up0[1024:], dn0[1024:], up1[512:], dn1[512:]], axis=0), "xflip")
     b0 = jnp.concatenate([s_ab[:, 256:], o_ab[:, 256:]], axis=0)
     b_up = send(b0, "zup")
@@ -243,7 +288,7 @@
     q_feat = q_blk[:, :2048]
     positive = (q_blk[:, 2048].astype(f32) * 16 + q_blk[:, 2049].astype(f32)).astype(jnp.int32)
     row = jnp.arange(128, dtype=jnp.int32)
-    row_c, row_z, row_y = (row // 4) % 2, (row // 8) % 4, row // 32
+    row_c, row_y, row_z = (row // 4) % 2, (row // 8) % 4, row // 32
     passage_id = (((row_y * 2 + x_lo) * 2 + row_c) * 8 + x_hi * 4 + row_z) * 4 + row % 4
     partial = lax.dot_general(q_feat, p_blk, NT, preferred_element_type=f32)
     logits = logit_scale * (partial + send(partial, "core"))
@@ -301,36 +346,49 @@
     q_rows = jnp.concatenate([q_hi, q_lo, jnp.zeros((12, 2048), bf16)], axis=0)
 
     shard_ids = [(x_hi ^ du) * 4 + (z + dz) % 4 for du, dz in REL]
-    scal = jnp.stack(shard_ids + [(y + dy) % 4 for dy in (0, -1, 1, 2)] + [half]).astype(jnp.int32)
-    srcs, copies = [output_weight], [(0, 0, 12, 512, 0, 0, 0, 2048)]
-
-    def land(value, shards, dst_col, cols, at=0):
-        if not any(value is known for known in srcs):
-            srcs.append(value)
-        index = [value is known for known in srcs].index(True)
-        for shard, dst_row, rows in shards:
-            copies.append((index, at, None, rows, shard, dst_row, dst_col, cols))
-            at += rows
+    ring = [(y + dy) % 4 for dy in (0, -1, 1, 2)]
+    numbers = lambda blocks: jnp.stack(
+        shard_ids + [jnp.asarray(block, jnp.int32) for block in blocks] + [half]
+    ).astype(jnp.int32)
+
+    class Plan:
+        def __init__(self):
+            self.srcs, self.copies = [output_weight], []
+            for block in range(4):
+                self.copies.append((0, 0, 0, True, 512, 0, 0, block))
+
+        def land(self, value, pieces, block, at=0, column=0):
+            if not any(value is known for known in self.srcs):
+                self.srcs.append(value)
+            index = [value is known for known in self.srcs].index(True)
+            for shard, dst_row, rows in pieces:
+                self.copies.append((index, at, column, False, rows, shard, dst_row, block))
+                at += rows
 
     whole = lambda shard: (shard, 0, 512)
-    seven = [whole(shard) for shard in (4, 1, 5, 2, 6, 3, 7)]
-    land(y0, seven, (8,), 256)
-    land(y_up, seven, (9,), 256)
-    land(y_dn, seven, (10,), 256)
-    land(y_far0, seven[:3] + [(2, 0, 256)], (11,), 256)
-    land(y_far1, [(2, 256, 256)] + seven[4:], (11,), 256)
-    land(o_ab, [whole(4)], 1024, 1024)
-    land(up0, [whole(1)], 1024, 256, 1024)
-    land(dn0, [whole(2)], 1024, 256, 1024)
-    land(up1, [(3, 0, 256)], 1024, 256, 512)
-    land(dn1, [(3, 256, 256)], 1024, 256, 512)
-    land(a_x, [whole(5), whole(6), whole(7)], 1024, 256)
-    land(b_up, [whole(1), whole(5)], 1280, 768)
-    land(b_dn, [whole(2), whole(6)], 1280, 768)
-    land(b_far0, [whole(3)], 1280, 768)
-    land(b_far1, [whole(7)], 1280, 768)
+    five, two = [whole(shard) for shard in (4, 1, 5, 2, 6)], [whole(3), whole(7)]
+    early, late = Plan(), Plan()
+    for block, (va, vb) in enumerate(((ya, yb), (ya_u, yb_u), (ya_d, yb_d))):
+        early.land(va, five, block)
+        early.land(vb, two, block)
+    early.land(o_ab, [whole(4)], 3)
+    early.land(up0, [whole(1)], 3, 1024)
+    early.land(dn0, [whole(2)], 3, 1024)
+    early.land(up1, [(3, 0, 256)], 3, 512)
+    early.land(dn1, [(3, 256, 256)], 3, 512)
+    early.land(a_x, [whole(5), whole(6), whole(7)], 3)
+    for k in range(3):
+        late.land(o_ab, [whole(4)], 1 + k, 0, 256 + 256 * k)
+        late.land(b_up, [whole(1), whole(5)], 1 + k, 0, 256 * k)
+        late.land(b_dn, [whole(2), whole(6)], 1 + k, 0, 256 * k)
+        late.land(b_far0, [whole(3)], 1 + k, 0, 256 * k)
+        late.land(b_far1, [whole(7)], 1 + k, 0, 256 * k)
+    late.land(y_far0, five[:3] + [(2, 0, 256)], 0)
+    late.land(y_far1, [(2, 256, 256), five[4]] + two, 0)
+    shared = (a_own, a_par, res_own, r_par, low, up_half, q_rows, q_f)
+    carry = block_call(early.copies, early.srcs, numbers(ring[:3] + [4]), *shared, None)
     hidden, stats_own, y_own, y_par, y_q = block_call(
-        copies, srcs, scal, a_own, a_par, res_own, r_par, low, up_half, q_rows, q_f
+        late.copies, late.srcs, numbers(ring[3:] + [5, 6, 7]), *shared, carry
     )
 
     v_own, v_par = y_q[0:1] + y_q[2:3], y_q[1:2] + y_q[3:4]
@@ -380,6 +438,7 @@
     swap = lambda value: lax.all_to_all(
         value, AX, 0, 0, axis_index_groups=sides, tiled=True
     )
+    packed_total = total
     part = jnp.sum(swap(total.reshape(64, 1280)), axis=0, keepdims=True)
     total = swap(jnp.broadcast_to(part, (64, 1280))).reshape(40, 2048)
     mate = send(total, "core")
@@ -389,15 +448,14 @@
     lora_up = ordered(c, total[16:32], mate[16:32], axis=1)
 
     p_sum = p_part
-    for bit, n, move, name in (
-        (y // 2, 64, "yflip", "r_y0"),
-        (y % 2, 32, "ynear", "r_y1"),
-        (z // 2, 16, "zflip", "r_z0"),
-        (z % 2, 8, "znear", "r_z1"),
+    for bit, n, move, until in (
+        (z // 2, 64, "zflip", stats_own),
+        (z % 2, 32, "znear", packed_total),
+        (y // 2, 16, "yflip", part),
+        (y % 2, 8, "ynear", attn_grad),
     ):
         got = send(pick(p_sum, n * (1 - bit), n), move)
-        if name == "r_y0":
-            got, p_sum, _ = lax.optimization_barrier((got, p_sum, stats_own))
+        got, p_sum, _ = lax.optimization_barrier((got, p_sum, until))
         p_sum = pick(p_sum, n * bit, n) + got
     p_sum = logit_scale * p_sum
     keep = jnp.concatenate([pick(q_sum, 4 * c, 4), pick(p_sum, 4 * c, 4)], axis=0)

time: 260 us -> 277 us (1.065)
  waiting for transfers between devices: 99.3 us -> 76.9 us
  local copies, waits for them, and re-layouts: 22.9 us -> 38.4 us
  starting transfers between devices: 74.6 us -> 84.1 us
  other arithmetic: 15 us -> 22.2 us
  Pallas kernels: 29.5 us -> 34.5 us
    ppermute x38 -> x40, waiting for transfers between devices: 90.2 us -> 68.9 us  [send(): return lax.ppermute(value, AX, MOVES[move])]
    unnamed x60 -> x100, local copies, waits for them, and re-layouts: 1.95 us -> 14.1 us
    ppermute x38 -> x40, starting transfers between devices: 58.3 us -> 68 us  [send(): return lax.ppermute(value, AX, MOVES[move])]
    pallas_call x1 -> x2, Pallas kernels: 29.5 us -> 34.5 us  [block_call(): pl.pallas_call(functools.partial(block_kernel, copies, len(srcs), first),...]
  transfers between devices with their start and end apart: 40 -> 42, of which waited for: 17 -> 16; matrix products, arithmetic and copies ran while one was open for 15% -> 20% of each run, Pallas kernels for 11% -> 13%
where the time goes in v1:
time: 277 us; the launch traced here: 276 us
  starting transfers between devices  84.1 us (30%)
  waiting for transfers between devices  76.9 us (28%)
  local copies, waits for them, and re-layouts  38.4 us (14%)
  Pallas kernels  34.5 us (12%)
  other arithmetic  22.2 us (8%)
  matrix products  11 us (4%)
  between operations  8.99 us (3%)
    ppermute x40, waiting for transfers between devices, send(): return lax.ppermute(value, AX, MOVES[move])  68.9 us
    ppermute x40, starting transfers between devices, send(): return lax.ppermute(value, AX, MOVES[move])  68 us
    pallas_call x2, Pallas kernels, block_call(): pl.pallas_call(functools.partial(block_kernel, copies, len(srcs), first),...  34.5 us
    all_to_all x2, starting transfers between devices, compute(): lax.all_to_all(value, AX, 0, 0, axis_index_groups=sides, tiled=True)  16.1 us
    unnamed x100, local copies, waits for them, and re-layouts  14.1 us
    all_to_all x2, waiting for transfers between devices, compute(): lax.all_to_all(value, AX, 0, 0, axis_index_groups=sides, tiled=True)  7.97 us
    dynamic_slice x13, local copies, waits for them, and re-layouts, pick(): return lax.dynamic_slice_in_dim(value, start, size, axis=axis)  7.56 us
  transfers between devices with their start and end apart: 42, of which 16 were waited for; matrix products, arithmetic and copies ran while one was open for 20% of the time, Pallas kernels for 13%

profile of v1, /device:TPU:1, one launch (start us, length us, event | category | flops | bytes accessed | tf_op | source)
XLA Modules:
  0.0 276.2 jit_solution(1538941717120816708)
XLA Ops:
  1.8 3.4 %collective-permute-start.5 = (bf16[512,256]{1,0:T(8,128)(2,1)S(1)}, bf16[512,256]{1,0:T(8,128)(2,1)S(1)}, u32[]{:S(2)}, u32[]{:S(2)}) collective-permute-start(bf16[512,256]{1,0:T(8,128)(2,1)S(1)} %get-tuple-element.62), channel_id=1, source_target_pairs={{0,20},{1,21},{2,22},{3,23},{4,16},{5,17},{6,18},{7,19},{8,28},{9,... | collective-permute-start | bytes 786440 | tf_op jit(solution)/shard_map/ppermute | solution.py:52
  8.7 2.3 constant_dynamic-slice_fusion.15
  12.3 2.1 constant_dynamic-slice_fusion.1
  20.2 2.9 %collective-permute-start.19 = (bf16[16,2048]{1,0:T(8,128)(2,1)S(1)}, bf16[16,2048]{1,0:T(8,128)(2,1)S(1)}, u32[]{:S(2)}, u32[]{:S(2)}) collective-permute-start(bf16[16,2048]{1,0:T(8,128)(2,1)S(1)} %maximum_select_fusion.9), channel_id=1, source_target_pairs={{0,96},{1,97},{2,98},{3,99},{4,100},{5,101},{6,102},{7,103},{8,104... | collective-permute-start | bytes 196616 | tf_op jit(solution)/shard_map/ppermute | solution.py:52
  29.6 3.7 %collective-permute-start.21 = (bf16[64,2048]{1,0:T(8,128)(2,1)S(1)}, bf16[64,2048]{1,0:T(8,128)(2,1)S(1)}, u32[]{:S(2)}, u32[]{:S(2)}) collective-permute-start(bf16[64,2048]{1,0:T(8,128)(2,1)S(1)} %maximum_select_fusion.2), channel_id=1, source_target_pairs={{0,3},{1,2},{2,1},{3,0},{4,7},{5,6},{6,5},{7,4},{8,11},{9,10},{10,... | collective-permute-start | bytes 786440 | tf_op jit(solution)/shard_map/ppermute | solution.py:52
  33.2 2.6 collective-permute-start.17
  38.6 3.6 %collective-permute-start.22 = (f32[32,128]{1,0:T(8,128)S(1)}, f32[32,128]{1,0:T(8,128)S(1)}, u32[]{:S(2)}, u32[]{:S(2)}) collective-permute-start(f32[32,128]{1,0:T(8,128)S(1)} %fusion.18), channel_id=1, source_target_pairs={{0,8},{1,9},{2,10},{3,11},{4,12},{5,13},{6,14},{7,15},{8,0},{9,1},... | collective-permute-start | bytes 49160 | tf_op jit(solution)/shard_map/ppermute | solution.py:52
  43.7 2.7 collective-permute-start.7
  46.4 2.6 collective-permute-start.24
  51.1 2.6 collective-permute-start.25
  60.1 3.7 %collective-permute-start.27 = (bf16[256,4096]{1,0:T(8,128)(2,1)S(1)}, bf16[256,4096]{1,0:T(8,128)(2,1)S(1)}, u32[]{:S(2)}, u32[]{:S(2)}) collective-permute-start(bf16[256,4096]{1,0:T(8,128)(2,1)S(1)} %bitcast.160), channel_id=1, source_target_pairs={{0,8},{1,9},{2,10},{3,11},{4,12},{5,13},{6,14},{7,15},{8,0},{9,1},... | collective-permute-start | bytes 6291464 | tf_op jit(solution)/shard_map/ppermute | solution.py:52
  64.2 2.7 collective-permute-start.12
  67.2 2.8 %collective-permute-start.10 = (bf16[2560,256]{1,0:T(8,128)(2,1)S(1)}, bf16[2560,256]{1,0:T(8,128)(2,1)S(1)}, u32[]{:S(2)}, u32[]{:S(2)}) collective-permute-start(bf16[2560,256]{1,0:T(8,128)(2,1)S(1)} %pad_maximum_fusion.1.refs_1_), channel_id=1, source_target_pairs={{0,96},{1,97},{2,98},{3,99},{4,100},{5,101},{6,102},{7,103},{8,104... | collective-permute-start | bytes 3932168 | tf_op jit(solution)/shard_map/ppermute | solution.py:52
  70.0 5.0 %collective-permute-done.11.refs_10_ = bf16[768,256]{1,0:T(8,128)(2,1)S(1)} collective-permute-done((bf16[768,256]{1,0:T(8,128)(2,1)S(1)}, bf16[768,256]{1,0:T(8,128)(2,1)S(1)}, u32[]{:S(2)}, u32[]{:S(2)}) %collective-permute-start.11) | collective-permute-done | bytes 393248 | tf_op jit(solution)/shard_map/ppermute | solution.py:52
  76.0 2.7 collective-permute-start.13
  81.0 26.9 %collective-permute-done.13.refs_6_ = bf16[1024,256]{1,0:T(8,128)(2,1)S(1)} collective-permute-done((bf16[1024,256]{1,0:T(8,128)(2,1)}, bf16[1024,256]{1,0:T(8,128)(2,1)S(1)}, u32[]{:S(2)}, u32[]{:S(2)}) %collective-permute-start.13) | collective-permute-done | bytes 524320 | tf_op jit(solution)/shard_map/ppermute | solution.py:52
  110.1 2.5 collective-permute-start.28
  113.5 2.5 collective-permute-start.30
  119.8 21.7 %collective-permute-done.2.refs_3_ = bf16[1024,768]{1,0:T(8,128)(2,1)S(1)} collective-permute-done((bf16[1024,768]{1,0:T(8,128)(2,1)S(1)}, bf16[1024,768]{1,0:T(8,128)(2,1)S(1)}, u32[]{:S(2)}, u32[]{:S(2)}) %collective-permute-start.2) | collective-permute-done | bytes 1572896 | tf_op jit(solution)/shard_map/ppermute | solution.py:52
  141.5 3.3 %collective-permute-start.14 = (bf16[1792,256]{1,0:T(8,128)(2,1)}, bf16[1792,256]{1,0:T(8,128)(2,1)}, u32[]{:S(2)}, u32[]{:S(2)}) collective-permute-start(bf16[1792,256]{1,0:T(8,128)(2,1)} %pad_maximum_fusion.2), channel_id=1, source_target_pairs={{0,96},{1,97},{2,98},{3,99},{4,100},{5,101},{6,102},{7,103},{8,104... | collective-permute-start | bytes 2752520 | tf_op jit(solution)/shard_map/ppermute | solution.py:52
  149.1 2.5 collective-permute-start.33
  164.3 17.1 %block_first.1 = (f32[512,2048]{1,0:T(8,128)}, f32[528,128]{1,0:T(8,128)S(1)}, f32[528,4096]{1,0:T(8,128)}) custom-call(s32[13]{0:T(128)S(1)} %stack.105.scal, bf16[512,4096]{1,0:T(8,128)(2,1)} %refs_0_.3, bf16[2560,256]{1,0:T(8,128)(2,1)S(1)} %copy-done.8, bf16[1024,256]{1,0:T(8,128)(2,1)} %pad_maximum_fusion.5.refs_2_, bf16[2560,256]{1,0:T(8,128)(2,1)S(1)} %copy-done.10, ...), custom_call_target="tpu_custom_call" | custom-call | flops 8589934592 | bytes 25165824 | tf_op jit(solution)/shard_map/block_first/pallas_call | solution.py:198
  181.5 17.5 %block_last.1 = (f32[512,2048]{1,0:T(8,128)}, f32[528,128]{1,0:T(8,128)S(1)}, f32[256,4096]{1,0:T(8,128)}, bf16[256,4096]{1,0:T(8,128)(2,1)}, f32[16,4096]{1,0:T(8,128)S(1)}) custom-call(s32[13]{0:T(128)S(1)} %stack.95.scal, bf16[512,4096]{1,0:T(8,128)(2,1)} %refs_0_.3, bf16[512,1024]{1,0:T(8,128)(2,1)S(1)} %copy-done.2, ...), custom_call_target="tpu_custom_call", output_to_operand_aliasing={{0}: (19, {})} | custom-call | flops 8589934592 | bytes 25165824 | tf_op jit(solution)/shard_map/block_last/pallas_call | solution.py:198
  199.0 4.2 %collective-permute-start.31 = (f32[560,128]{1,0:T(8,128)S(1)}, f32[560,128]{1,0:T(8,128)S(1)}, u32[]{:S(2)}, u32[]{:S(2)}) collective-permute-start(f32[560,128]{1,0:T(8,128)S(1)} %pad_maximum_fusion.8), channel_id=1, source_target_pairs={{0,8},{1,9},{2,10},{3,11},{4,12},{5,13},{6,14},{7,15},{8,0},{9,1},... | collective-permute-start | bytes 860168 | tf_op jit(solution)/shard_map/ppermute | solution.py:52
  217.8 8.0 %all-to-all-start = ((f32[64,1,1280]{2,1,0:T(1,128)}), f32[64,1,1280]{2,1,0:T(1,128)S(1)}, u32[]{:S(2)}, u32[]{:S(2)}) async-start(f32[64,1,1280]{2,1,0:T(1,128)} %all_to_all.13), calls=%async_computation | async-start | bytes 655360 | tf_op jit(solution)/shard_map/all_to_all | solution.py:438
  229.0 2.8 %collective-permute-start.35 = (f32[16,2048]{1,0:T(8,128)S(1)}, f32[16,2048]{1,0:T(8,128)S(1)}, u32[]{:S(2)}, u32[]{:S(2)}) collective-permute-start(f32[16,2048]{1,0:T(8,128)S(1)} %constant_dynamic-slice_fusion.6), channel_id=1, source_target_pairs={{0,96},{1,97},{2,98},{3,99},{4,100},{5,101},{6,102},{7,103},{8,104... | collective-permute-start | bytes 393224 | tf_op jit(solution)/shard_map/ppermute | solution.py:52
  231.8 5.2 %collective-permute-done.35 = f32[16,2048]{1,0:T(8,128)S(1)} collective-permute-done((f32[16,2048]{1,0:T(8,128)S(1)}, f32[16,2048]{1,0:T(8,128)S(1)}, u32[]{:S(2)}, u32[]{:S(2)}) %collective-permute-start.35) | collective-permute-done | bytes 131104 | tf_op jit(solution)/shard_map/ppermute | solution.py:52
  238.1 8.2 %all-to-all-start.1 = ((f32[64,1,1280]{2,1,0:T(1,128)}), f32[64,1,1280]{2,1,0:T(1,128)S(1)}, u32[]{:S(2)}, u32[]{:S(2)}) async-start(f32[64,1,1280]{2,1,0:T(1,128)} %broadcast_in_dim.102), calls=%async_computation.1 | async-start | bytes 655360 | tf_op jit(solution)/shard_map/all_to_all | solution.py:438
  248.0 8.0 %all-to-all-done.1 = f32[64,1,1280]{2,1,0:T(1,128)S(1)} async-done(((f32[64,1,1280]{2,1,0:T(1,128)}), f32[64,1,1280]{2,1,0:T(1,128)S(1)}, u32[]{:S(2)}, u32[]{:S(2)}) %all-to-all-start.1) | async-done | bytes 327712 | tf_op jit(solution)/shard_map/all_to_all | solution.py:438
  256.8 2.4 collective-permute-start.32
  264.5 5.3 %add_convert_fusion = bf16[256,4096]{1,0:T(8,128)(2,1)} fusion(f32[256,4096]{1,0:T(8,128)} %get-tuple-element.44, bf16[256,4096]{1,0:T(8,128)(2,1)} %collective-permute-done.37, f32[256]{0:T(256)S(1)} %slice.277, f32[4096]{0:T(1024)S(1)} %bitcast.170, f32[256]{0:T(256)S(1)} %slice.273, bf16[4096,16]{0,1:T(8,128)(2,1)S(1)} %copy-done, ...), kind=kOutput, calls=%fused_computation.3 | convolution fusion | flops 40894464 | bytes 8603648 | tf_op jit(solution)/shard_map/dot_general | solution.py:426
  271.2 2.1 maximum_select_fusion
  (295 shorter events, 82.2 us)
Async XLA Ops:
  1.8 41.7 %collective-permute-start.5 = (bf16[512,256]{1,0:T(8,128)(2,1)S(1)}, bf16[512,256]{1,0:T(8,128)(2,1)S(1)}, u32[]{:S(2)}, u32[]{:S(2)}) collective-permute-start(bf16[512,256]{1,0:T(8,128)(2,1)S(1)} %get-tuple-element.62), channel_id=1, source_target_pairs={{0,20},{1,21},{2,22},{3,23},{4,16},{5,17},{6,18},{7,19},{8,28},{9,... | collective-permute-start | bytes 786440 | tf_op jit(solution)/shard_map/ppermute | solution.py:52
  7.7 9.3 %collective-permute-start.15 = (bf16[8,2176]{1,0:T(8,128)(2,1)S(1)}, bf16[8,2176]{1,0:T(8,128)(2,1)S(1)}, u32[]{:S(2)}, u32[]{:S(2)}) collective-permute-start(bf16[8,2176]{1,0:T(8,128)(2,1)S(1)} %get-tuple-element.95), channel_id=1, source_target_pairs={{0,8},{1,9},{2,10},{3,11},{4,12},{5,13},{6,14},{7,15},{8,0},{9,1},... | collective-permute-start | bytes 104456 | tf_op jit(solution)/shard_map/ppermute | solution.py:52
  11.0 67.8 %collective-permute-start = (bf16[512,1024]{1,0:T(8,128)(2,1)}, bf16[512,1024]{1,0:T(8,128)(2,1)S(1)}, u32[]{:S(2)}, u32[]{:S(2)}) collective-permute-start(bf16[512,1024]{1,0:T(8,128)(2,1)} %constant_dynamic-slice_fusion.15), channel_id=1, source_target_pairs={{0,20},{1,21},{2,22},{3,23},{4,16},{5,17},{6,18},{7,19},{8,28},{9,... | collective-permute-start | bytes 3145736 | tf_op jit(solution)/shard_map/ppermute | solution.py:52
  18.6 14.6 %collective-permute-start.16 = (bf16[8,2176]{1,0:T(8,128)(2,1)S(1)}, bf16[8,2176]{1,0:T(8,128)(2,1)S(1)}, u32[]{:S(2)}, u32[]{:S(2)}) collective-permute-start(bf16[8,2176]{1,0:T(8,128)(2,1)S(1)} %maximum_select_fusion.10), channel_id=1, source_target_pairs={{0,16},{1,17},{2,18},{3,19},{4,20},{5,21},{6,22},{7,23},{8,24},{9,... | collective-permute-start | bytes 104456 | tf_op jit(solution)/shard_map/ppermute | solution.py:52
  29.6 7.7 %collective-permute-start.21 = (bf16[64,2048]{1,0:T(8,128)(2,1)S(1)}, bf16[64,2048]{1,0:T(8,128)(2,1)S(1)}, u32[]{:S(2)}, u32[]{:S(2)}) collective-permute-start(bf16[64,2048]{1,0:T(8,128)(2,1)S(1)} %maximum_select_fusion.2), channel_id=1, source_target_pairs={{0,3},{1,2},{2,1},{3,0},{4,7},{5,6},{6,5},{7,4},{8,11},{9,10},{10,... | collective-permute-start | bytes 786440 | tf_op jit(solution)/shard_map/ppermute | solution.py:52
  43.6 20.3 %collective-permute-start.6 = (bf16[1536,256]{1,0:T(8,128)(2,1)S(1)}, bf16[1536,256]{1,0:T(8,128)(2,1)S(1)}, u32[]{:S(2)}, u32[]{:S(2)}) collective-permute-start(bf16[1536,256]{1,0:T(8,128)(2,1)S(1)} %pad_maximum_fusion.3), channel_id=1, source_target_pairs={{0,1},{1,2},{2,3},{3,0},{4,5},{5,6},{6,7},{7,4},{8,9},{9,10},{10,1... | collective-permute-start | bytes 2359304 | tf_op jit(solution)/shard_map/ppermute | solution.py:52
  43.7 20.4 %collective-permute-start.7 = (bf16[1536,256]{1,0:T(8,128)(2,1)S(1)}, bf16[1536,256]{1,0:T(8,128)(2,1)S(1)}, u32[]{:S(2)}, u32[]{:S(2)}) collective-permute-start(bf16[1536,256]{1,0:T(8,128)(2,1)S(1)} %pad_maximum_fusion.3), channel_id=1, source_target_pairs={{0,3},{1,0},{2,1},{3,2},{4,7},{5,4},{6,5},{7,6},{8,11},{9,8},{10,9... | collective-permute-start | bytes 2359304 | tf_op jit(solution)/shard_map/ppermute | solution.py:52
  51.1 5.4 %collective-permute-start.25 = (f32[16,2048]{1,0:T(8,128)S(1)}, f32[16,2048]{1,0:T(8,128)S(1)}, u32[]{:S(2)}, u32[]{:S(2)}) collective-permute-start(f32[16,2048]{1,0:T(8,128)S(1)} %constant_dynamic-slice_fusion.13), channel_id=1, source_target_pairs={{0,20},{1,21},{2,22},{3,23},{4,16},{5,17},{6,18},{7,19},{8,28},{9,... | collective-permute-start | bytes 393224 | tf_op jit(solution)/shard_map/ppermute | solution.py:52
  60.1 85.6 %collective-permute-start.27 = (bf16[256,4096]{1,0:T(8,128)(2,1)S(1)}, bf16[256,4096]{1,0:T(8,128)(2,1)S(1)}, u32[]{:S(2)}, u32[]{:S(2)}) collective-permute-start(bf16[256,4096]{1,0:T(8,128)(2,1)S(1)} %bitcast.160), channel_id=1, source_target_pairs={{0,8},{1,9},{2,10},{3,11},{4,12},{5,13},{6,14},{7,15},{8,0},{9,1},... | collective-permute-start | bytes 6291464 | tf_op jit(solution)/shard_map/ppermute | solution.py:52
  64.0 11.0 %collective-permute-start.11 = (bf16[768,256]{1,0:T(8,128)(2,1)S(1)}, bf16[768,256]{1,0:T(8,128)(2,1)S(1)}, u32[]{:S(2)}, u32[]{:S(2)}) collective-permute-start(bf16[768,256]{1,0:T(8,128)(2,1)S(1)} %pad_maximum_fusion.6), channel_id=1, source_target_pairs={{0,1},{1,2},{2,3},{3,0},{4,5},{5,6},{6,7},{7,4},{8,9},{9,10},{10,1... | collective-permute-start | bytes 1179656 | tf_op jit(solution)/shard_map/ppermute | solution.py:52
  64.2 10.8 %collective-permute-start.12 = (bf16[768,256]{1,0:T(8,128)(2,1)S(1)}, bf16[768,256]{1,0:T(8,128)(2,1)S(1)}, u32[]{:S(2)}, u32[]{:S(2)}) collective-permute-start(bf16[768,256]{1,0:T(8,128)(2,1)S(1)} %pad_maximum_fusion.7), channel_id=1, source_target_pairs={{0,3},{1,0},{2,1},{3,2},{4,7},{5,4},{6,5},{7,6},{8,11},{9,8},{10,9... | collective-permute-start | bytes 1179656 | tf_op jit(solution)/shard_map/ppermute | solution.py:52
  67.2 42.9 %collective-permute-start.10 = (bf16[2560,256]{1,0:T(8,128)(2,1)S(1)}, bf16[2560,256]{1,0:T(8,128)(2,1)S(1)}, u32[]{:S(2)}, u32[]{:S(2)}) collective-permute-start(bf16[2560,256]{1,0:T(8,128)(2,1)S(1)} %pad_maximum_fusion.1.refs_1_), channel_id=1, source_target_pairs={{0,96},{1,97},{2,98},{3,99},{4,100},{5,101},{6,102},{7,103},{8,104... | collective-permute-start | bytes 3932168 | tf_op jit(solution)/shard_map/ppermute | solution.py:52
  76.0 31.9 %collective-permute-start.13 = (bf16[1024,256]{1,0:T(8,128)(2,1)}, bf16[1024,256]{1,0:T(8,128)(2,1)S(1)}, u32[]{:S(2)}, u32[]{:S(2)}) collective-permute-start(bf16[1024,256]{1,0:T(8,128)(2,1)} %pad_maximum_fusion.5.refs_2_), channel_id=1, source_target_pairs={{0,96},{1,97},{2,98},{3,99},{4,100},{5,101},{6,102},{7,103},{8,104... | collective-permute-start | bytes 1572872 | tf_op jit(solution)/shard_map/ppermute | solution.py:52
  78.8 34.8 %collective-permute-start.8 = (bf16[2560,256]{1,0:T(8,128)(2,1)S(1)}, bf16[2560,256]{1,0:T(8,128)(2,1)S(1)}, u32[]{:S(2)}, u32[]{:S(2)}) collective-permute-start(bf16[2560,256]{1,0:T(8,128)(2,1)S(1)} %pad_maximum_fusion.1.refs_1_), channel_id=1, source_target_pairs={{0,32},{1,33},{2,34},{3,35},{4,36},{5,37},{6,38},{7,39},{8,40},{9,... | collective-permute-start | bytes 3932168 | tf_op jit(solution)/shard_map/ppermute | solution.py:52
  79.9 37.8 %collective-permute-start.1 = (bf16[1024,768]{1,0:T(8,128)(2,1)S(1)}, bf16[1024,768]{1,0:T(8,128)(2,1)S(1)}, u32[]{:S(2)}, u32[]{:S(2)}) collective-permute-start(bf16[1024,768]{1,0:T(8,128)(2,1)S(1)} %pad_maximum_fusion), channel_id=1, source_target_pairs={{0,1},{1,2},{2,3},{3,0},{4,5},{5,6},{6,7},{7,4},{8,9},{9,10},{10,1... | collective-permute-start | bytes 4718600 | tf_op jit(solution)/shard_map/ppermute | solution.py:52
  107.9 33.6 %collective-permute-start.2 = (bf16[1024,768]{1,0:T(8,128)(2,1)S(1)}, bf16[1024,768]{1,0:T(8,128)(2,1)S(1)}, u32[]{:S(2)}, u32[]{:S(2)}) collective-permute-start(bf16[1024,768]{1,0:T(8,128)(2,1)S(1)} %pad_maximum_fusion), channel_id=1, source_target_pairs={{0,3},{1,0},{2,1},{3,2},{4,7},{5,4},{6,5},{7,6},{8,11},{9,8},{10,9... | collective-permute-start | bytes 4718600 | tf_op jit(solution)/shard_map/ppermute | solution.py:52
  110.1 39.0 %collective-permute-start.28 = (bf16[256,2048]{1,0:T(8,128)(2,1)}, bf16[256,2048]{1,0:T(8,128)(2,1)}, u32[]{:S(2)}, u32[]{:S(2)}) collective-permute-start(bf16[256,2048]{1,0:T(8,128)(2,1)} %constant_dynamic-slice_fusion.11), channel_id=1, source_target_pairs={{0,8},{1,9},{2,10},{3,11},{4,12},{5,13},{6,14},{7,15},{8,0},{9,1},... | collective-permute-start | bytes 3145736 | tf_op jit(solution)/shard_map/ppermute | solution.py:52
  113.5 38.7 %collective-permute-start.30 = (bf16[1536,256]{1,0:T(8,128)(2,1)}, bf16[1536,256]{1,0:T(8,128)(2,1)}, u32[]{:S(2)}, u32[]{:S(2)}) collective-permute-start(bf16[1536,256]{1,0:T(8,128)(2,1)} %pad_maximum_fusion.4), channel_id=1, source_target_pairs={{0,20},{1,21},{2,22},{3,23},{4,16},{5,17},{6,18},{7,19},{8,28},{9,... | collective-permute-start | bytes 2359304 | tf_op jit(solution)/shard_map/ppermute | solution.py:52
  117.7 33.9 %collective-permute-start.29 = (bf16[1024,256]{1,0:T(8,128)(2,1)}, bf16[1024,256]{1,0:T(8,128)(2,1)}, u32[]{:S(2)}, u32[]{:S(2)}) collective-permute-start(bf16[1024,256]{1,0:T(8,128)(2,1)} %pad_maximum_fusion.5.refs_2_), channel_id=1, source_target_pairs={{0,32},{1,33},{2,34},{3,35},{4,36},{5,37},{6,38},{7,39},{8,40},{9,... | collective-permute-start | bytes 1572872 | tf_op jit(solution)/shard_map/ppermute | solution.py:52
  141.5 39.9 %collective-permute-start.14 = (bf16[1792,256]{1,0:T(8,128)(2,1)}, bf16[1792,256]{1,0:T(8,128)(2,1)}, u32[]{:S(2)}, u32[]{:S(2)}) collective-permute-start(bf16[1792,256]{1,0:T(8,128)(2,1)} %pad_maximum_fusion.2), channel_id=1, source_target_pairs={{0,96},{1,97},{2,98},{3,99},{4,100},{5,101},{6,102},{7,103},{8,104... | collective-permute-start | bytes 2752520 | tf_op jit(solution)/shard_map/ppermute | solution.py:52
  145.8 35.7 %collective-permute-start.9 = (bf16[1792,256]{1,0:T(8,128)(2,1)}, bf16[1792,256]{1,0:T(8,128)(2,1)}, u32[]{:S(2)}, u32[]{:S(2)}) collective-permute-start(bf16[1792,256]{1,0:T(8,128)(2,1)} %slice.291), channel_id=1, source_target_pairs={{0,32},{1,33},{2,34},{3,35},{4,36},{5,37},{6,38},{7,39},{8,40},{9,... | collective-permute-start | bytes 2752520 | tf_op jit(solution)/shard_map/ppermute | solution.py:52
  149.1 54.1 %collective-permute-start.33 = (f32[64,2048]{1,0:T(8,128)}, f32[64,2048]{1,0:T(8,128)S(1)}, u32[]{:S(2)}, u32[]{:S(2)}) collective-permute-start(f32[64,2048]{1,0:T(8,128)} %constant_dynamic-slice_fusion.8), channel_id=1, source_target_pairs={{0,3},{1,2},{2,1},{3,0},{4,7},{5,6},{6,5},{7,4},{8,11},{9,10},{10,... | collective-permute-start | bytes 1572872 | tf_op jit(solution)/shard_map/ppermute | solution.py:52
  151.6 29.8 %collective-permute-start.3 = (bf16[512,768]{1,0:T(8,128)(2,1)}, bf16[512,768]{1,0:T(8,128)(2,1)S(1)}, u32[]{:S(2)}, u32[]{:S(2)}) collective-permute-start(bf16[512,768]{1,0:T(8,128)(2,1)} %slice.287), channel_id=1, source_target_pairs={{0,1},{1,2},{2,3},{3,0},{4,5},{5,6},{6,7},{7,4},{8,9},{9,10},{10,1... | collective-permute-start | bytes 2359304 | tf_op jit(solution)/shard_map/ppermute | solution.py:52
  152.3 29.2 %collective-permute-start.4 = (bf16[512,768]{1,0:T(8,128)(2,1)}, bf16[512,768]{1,0:T(8,128)(2,1)S(1)}, u32[]{:S(2)}, u32[]{:S(2)}) collective-permute-start(bf16[512,768]{1,0:T(8,128)(2,1)} %slice.288), channel_id=1, source_target_pairs={{0,3},{1,0},{2,1},{3,2},{4,7},{5,4},{6,5},{7,6},{8,11},{9,8},{10,9... | collective-permute-start | bytes 2359304 | tf_op jit(solution)/shard_map/ppermute | solution.py:52
  199.0 5.4 %collective-permute-start.31 = (f32[560,128]{1,0:T(8,128)S(1)}, f32[560,128]{1,0:T(8,128)S(1)}, u32[]{:S(2)}, u32[]{:S(2)}) collective-permute-start(f32[560,128]{1,0:T(8,128)S(1)} %pad_maximum_fusion.8), channel_id=1, source_target_pairs={{0,8},{1,9},{2,10},{3,11},{4,12},{5,13},{6,14},{7,15},{8,0},{9,1},... | collective-permute-start | bytes 860168 | tf_op jit(solution)/shard_map/ppermute | solution.py:52
  203.2 61.3 %collective-permute-start.37 = (bf16[256,4096]{1,0:T(8,128)(2,1)}, bf16[256,4096]{1,0:T(8,128)(2,1)}, u32[]{:S(2)}, u32[]{:S(2)}) collective-permute-start(bf16[256,4096]{1,0:T(8,128)(2,1)} %get-tuple-element.45), channel_id=1, source_target_pairs={{0,8},{1,9},{2,10},{3,11},{4,12},{5,13},{6,14},{7,15},{8,0},{9,1},... | collective-permute-start | bytes 6291464 | tf_op jit(solution)/shard_map/ppermute | solution.py:52
  204.2 23.7 %collective-permute-start.34 = (f32[32,2048]{1,0:T(8,128)}, f32[32,2048]{1,0:T(8,128)}, u32[]{:S(2)}, u32[]{:S(2)}) collective-permute-start(f32[32,2048]{1,0:T(8,128)} %constant_dynamic-slice_fusion.7), channel_id=1, source_target_pairs={{0,1},{1,0},{2,3},{3,2},{4,5},{5,4},{6,7},{7,6},{8,9},{9,8},{10,11... | collective-permute-start | bytes 786440 | tf_op jit(solution)/shard_map/ppermute | solution.py:52
  217.8 19.1 %all-to-all-start = ((f32[64,1,1280]{2,1,0:T(1,128)}), f32[64,1,1280]{2,1,0:T(1,128)S(1)}, u32[]{:S(2)}, u32[]{:S(2)}) async-start(f32[64,1,1280]{2,1,0:T(1,128)} %all_to_all.13), calls=%async_computation | async-start | bytes 655360 | tf_op jit(solution)/shard_map/all_to_all | solution.py:438
  225.8 45.3 %collective-permute-start.39 = (bf16[256,2048]{1,0:T(8,128)(2,1)}, bf16[256,2048]{1,0:T(8,128)(2,1)S(1)}, u32[]{:S(2)}, u32[]{:S(2)}) collective-permute-start(bf16[256,2048]{1,0:T(8,128)(2,1)} %get-tuple-element.65), channel_id=1, source_target_pairs={{0,8},{1,9},{2,10},{3,11},{4,12},{5,13},{6,14},{7,15},{8,0},{9,1},... | collective-permute-start | bytes 3145736 | tf_op jit(solution)/shard_map/ppermute | solution.py:52
  229.0 8.0 %collective-permute-start.35 = (f32[16,2048]{1,0:T(8,128)S(1)}, f32[16,2048]{1,0:T(8,128)S(1)}, u32[]{:S(2)}, u32[]{:S(2)}) collective-permute-start(f32[16,2048]{1,0:T(8,128)S(1)} %constant_dynamic-slice_fusion.6), channel_id=1, source_target_pairs={{0,96},{1,97},{2,98},{3,99},{4,100},{5,101},{6,102},{7,103},{8,104... | collective-permute-start | bytes 393224 | tf_op jit(solution)/shard_map/ppermute | solution.py:52
  238.1 17.8 %all-to-all-start.1 = ((f32[64,1,1280]{2,1,0:T(1,128)}), f32[64,1,1280]{2,1,0:T(1,128)S(1)}, u32[]{:S(2)}, u32[]{:S(2)}) async-start(f32[64,1,1280]{2,1,0:T(1,128)} %broadcast_in_dim.102), calls=%async_computation.1 | async-start | bytes 655360 | tf_op jit(solution)/shard_map/all_to_all | solution.py:438
  246.9 22.8 %collective-permute-start.36 = (f32[8,2048]{1,0:T(8,128)}, f32[8,2048]{1,0:T(8,128)}, u32[]{:S(2)}, u32[]{:S(2)}) collective-permute-start(f32[8,2048]{1,0:T(8,128)} %constant_dynamic-slice_fusion.5), channel_id=1, source_target_pairs={{0,32},{1,33},{2,34},{3,35},{4,36},{5,37},{6,38},{7,39},{8,40},{9,... | collective-permute-start | bytes 196616 | tf_op jit(solution)/shard_map/ppermute | solution.py:52
  (62 other events, 650.4 us)

commit v2 on v1

--- a/solution.py
+++ b/solution.py
@@ -164,7 +164,7 @@
 
 def block_call(copies, srcs, scal, a_own, a_par, r_own, r_par, low, up, q_rows, q_f, carry):
     vm = pl.BlockSpec(memory_space=pltpu.VMEM)
-    anyspace = pl.BlockSpec(memory_space=pl.ANY)
+    anyspace = pl.BlockSpec(memory_space=pltpu.HBM)
     first = carry is None
     shapes = [jax.ShapeDtypeStruct((512, 2048), f32), jax.ShapeDtypeStruct((528, 128), f32)]
     args = [scal, *srcs, a_own, a_par, r_own, r_par, low, up, q_rows, q_f]
@@ -195,6 +195,10 @@
         in_specs += [anyspace, vm, anyspace]
         args += [carry[2], carry[1], carry[0]]
         aliases = {len(args) - 1: 0}
+    args = [
+        pltpu.with_memory_space_constraint(arg, pltpu.HBM) if spec is anyspace else arg
+        for arg, spec in zip(args, in_specs)
+    ]
     return pl.pallas_call(
         functools.partial(block_kernel, copies, len(srcs), first),
         out_shape=shapes,
@@ -261,6 +265,7 @@
 
     p_blk = ordered(y % 2, p_chip, send(p_chip, "ynear"))
     p_blk = ordered(y // 2, p_blk, send(p_blk, "yflip"))
+    p_half = p_blk
     p_blk = ordered(z % 2, p_blk, send(p_blk, "znear"))
     p_blk = ordered(z // 2, p_blk, send(p_blk, "zflip"))
     q_blk = ordered(x % 2, q_chip, send(q_chip, "xnear"))
@@ -313,6 +318,7 @@
     log_norm = stats[0] + jnp.log(stats[1])
     loss_rows = log_norm - stats[3]
     scale_rows = stats[2] / stats[1] - stats[3]
+    loss_sums = jnp.sum(jnp.stack([loss_rows, scale_rows]), axis=1) / 8
     weight_half = jnp.exp(logits - log_norm[:, None]).astype(bf16)
     hot = hit.astype(bf16)
     q_part = jnp.dot(weight_half, p_blk, preferred_element_type=f32) - jnp.dot(
@@ -326,7 +332,7 @@
     q_sum = pick(q_sum, 8 * xl, 8) + send(pick(q_sum, 8 * (1 - xl), 8), "xnear")
     q_sum = logit_scale * q_sum
 
-    a_own, res_own, _ = lax.optimization_barrier((a_own, res_own, q_sum))
+    a_own, res_own, _ = lax.optimization_barrier((a_own, res_own, p_half))
     a_par = send(a_own, "core")
     r_par = send(pick(res_own, other_half, 2048, 1), "core")
     low = jnp.concatenate(
@@ -430,9 +436,7 @@
     down_part = lax.dot_general(
         low_grad[:256], pick(a_own, half, 2048, 1), TN, preferred_element_type=f32
     ) + lax.dot_general(low_grad[256:], pick(a_par, half, 2048, 1), TN, preferred_element_type=f32)
-    my_row = (x * 2 + c) * 4
-    sums = jnp.stack([jnp.sum(pick(loss_rows, my_row, 4)), jnp.sum(pick(scale_rows, my_row, 4))])
-    tail = jnp.pad(sums[None], ((0, 7), (0, 2046)))
+    tail = jnp.pad(loss_sums[None], ((0, 7), (0, 2046)))
     total = jnp.concatenate([down_part / 128, up_part / 128, tail], axis=0)
     sides = [[i for i in range(128) if coords(i)[3] == side] for side in range(2)]
     swap = lambda value: lax.all_to_all(

time: 277 us -> 282 us (1.018)
  waiting for transfers between devices: 76.9 us -> 83.2 us
  local copies, waits for them, and re-layouts: 38.4 us -> 32.8 us
  Pallas kernels: 34.5 us -> 38.5 us
    unnamed x100 -> x64, local copies, waits for them, and re-layouts: 14.1 us -> 7.19 us
    ppermute x40, waiting for transfers between devices: 68.9 us -> 75.2 us  [send(): return lax.ppermute(value, AX, MOVES[move])]
    ppermute x40, starting transfers between devices: 68 us -> 62 us  [send(): return lax.ppermute(value, AX, MOVES[move])]
    pallas_call x2, Pallas kernels: 34.5 us -> 38.5 us  [block_call(): pl.pallas_call(functools.partial(block_kernel, copies, len(srcs), first),...]
    all_to_all x2, starting transfers between devices: 16.1 us -> 19.5 us  [compute(): lax.all_to_all(value, AX, 0, 0, axis_index_groups=sides, tiled=True)]
  transfers between devices with their start and end apart: 42 -> 42, of which waited for: 16 -> 15; matrix products, arithmetic and copies ran while one was open for 20% -> 21% of each run, Pallas kernels for 13% -> 14%
where the time goes in v2:
time: 282 us; the launch traced here: 281 us
  waiting for transfers between devices  83.2 us (30%)
  starting transfers between devices  81.4 us (29%)
  Pallas kernels  38.5 us (14%)
  local copies, waits for them, and re-layouts  32.8 us (12%)
  other arithmetic  24.6 us (9%)
  matrix products  12.2 us (4%)
  between operations  8.58 us (3%)
    ppermute x40, waiting for transfers between devices, send(): return lax.ppermute(value, AX, MOVES[move])  75.2 us
    ppermute x40, starting transfers between devices, send(): return lax.ppermute(value, AX, MOVES[move])  62 us
    pallas_call x2, Pallas kernels, block_call(): pl.pallas_call(functools.partial(block_kernel, copies, len(srcs), first),...  38.5 us
    all_to_all x2, starting transfers between devices, compute(): lax.all_to_all(value, AX, 0, 0, axis_index_groups=sides, tiled=True)  19.5 us
    dynamic_slice x13, local copies, waits for them, and re-layouts, pick(): return lax.dynamic_slice_in_dim(value, start, size, axis=axis)  8.58 us
    all_to_all x2, waiting for transfers between devices, compute(): lax.all_to_all(value, AX, 0, 0, axis_index_groups=sides, tiled=True)  7.98 us
    unnamed x64, local copies, waits for them, and re-layouts  7.19 us
  transfers between devices with their start and end apart: 42, of which 15 were waited for; matrix products, arithmetic and copies ran while one was open for 21% of the time, Pallas kernels for 14%

profile of v2, /device:TPU:1, one launch (start us, length us, event | category | flops | bytes accessed | tf_op | source)
XLA Modules:
  0.0 281.3 jit_solution(18434323144366239662)
XLA Ops:
  2.6 3.3 %collective-permute-start.5 = (bf16[512,256]{1,0:T(8,128)(2,1)}, bf16[512,256]{1,0:T(8,128)(2,1)}, u32[]{:S(2)}, u32[]{:S(2)}) collective-permute-start(bf16[512,256]{1,0:T(8,128)(2,1)} %get-tuple-element.63), channel_id=1, source_target_pairs={{0,20},{1,21},{2,22},{3,23},{4,16},{5,17},{6,18},{7,19},{8,28},{9,... | collective-permute-start | bytes 786440 | tf_op jit(solution)/shard_map/ppermute | solution.py:52
  9.4 2.3 constant_dynamic-slice_fusion.15
  29.6 2.6 collective-permute-start.21
  34.3 2.3 collective-permute-start.23
  38.4 3.8 %collective-permute-done.23 = bf16[64,2048]{1,0:T(8,128)(2,1)S(1)} collective-permute-done((bf16[64,2048]{1,0:T(8,128)(2,1)S(1)}, bf16[64,2048]{1,0:T(8,128)(2,1)S(1)}, u32[]{:S(2)}, u32[]{:S(2)}) %collective-permute-start.23) | collective-permute-done | bytes 262176 | tf_op jit(solution)/shard_map/ppermute | solution.py:52
  48.6 2.4 collective-permute-start.7
  51.0 2.2 collective-permute-start.26
  55.7 2.2 collective-permute-start.27
  61.3 3.4 %collective-permute-done.28 = f32[8,2048]{1,0:T(8,128)S(1)} collective-permute-done((f32[8,2048]{1,0:T(8,128)S(1)}, f32[8,2048]{1,0:T(8,128)S(1)}, u32[]{:S(2)}, u32[]{:S(2)}) %collective-permute-start.28) | collective-permute-done | bytes 65568 | tf_op jit(solution)/shard_map/ppermute | solution.py:52
  64.7 3.3 %collective-permute-done.6.refs_8_ = bf16[1536,256]{1,0:T(8,128)(2,1)S(1)} collective-permute-done((bf16[1536,256]{1,0:T(8,128)(2,1)S(1)}, bf16[1536,256]{1,0:T(8,128)(2,1)S(1)}, u32[]{:S(2)}, u32[]{:S(2)}) %collective-permute-start.6) | collective-permute-done | bytes 786464 | tf_op jit(solution)/shard_map/ppermute | solution.py:52
  68.3 2.7 collective-permute-start.12
  72.2 2.3 collective-permute-start.10
  74.5 4.0 %collective-permute-done.11.refs_10_ = bf16[768,256]{1,0:T(8,128)(2,1)S(1)} collective-permute-done((bf16[768,256]{1,0:T(8,128)(2,1)S(1)}, bf16[768,256]{1,0:T(8,128)(2,1)S(1)}, u32[]{:S(2)}, u32[]{:S(2)}) %collective-permute-start.11) | collective-permute-done | bytes 393248 | tf_op jit(solution)/shard_map/ppermute | solution.py:52
  79.6 2.3 collective-permute-start.13
  83.0 29.0 %collective-permute-done.13.refs_6_ = bf16[1024,256]{1,0:T(8,128)(2,1)S(1)} collective-permute-done((bf16[1024,256]{1,0:T(8,128)(2,1)}, bf16[1024,256]{1,0:T(8,128)(2,1)S(1)}, u32[]{:S(2)}, u32[]{:S(2)}) %collective-permute-start.13) | collective-permute-done | bytes 524320 | tf_op jit(solution)/shard_map/ppermute | solution.py:52
  113.9 2.9 %collective-permute-start.19 = (bf16[256,2048]{1,0:T(8,128)(2,1)}, bf16[256,2048]{1,0:T(8,128)(2,1)}, u32[]{:S(2)}, u32[]{:S(2)}) collective-permute-start(bf16[256,2048]{1,0:T(8,128)(2,1)} %constant_dynamic-slice_fusion.13), channel_id=1, source_target_pairs={{0,8},{1,9},{2,10},{3,11},{4,12},{5,13},{6,14},{7,15},{8,0},{9,1},... | collective-permute-start | bytes 3145736 | tf_op jit(solution)/shard_map/ppermute | solution.py:52
  116.8 2.3 collective-permute-start.30
  122.0 3.3 %collective-permute-start.14 = (bf16[1792,256]{1,0:T(8,128)(2,1)}, bf16[1792,256]{1,0:T(8,128)(2,1)}, u32[]{:S(2)}, u32[]{:S(2)}) collective-permute-start(bf16[1792,256]{1,0:T(8,128)(2,1)} %pad_maximum_fusion.2), channel_id=1, source_target_pairs={{0,96},{1,97},{2,98},{3,99},{4,100},{5,101},{6,102},{7,103},{8,104... | collective-permute-start | bytes 2752520 | tf_op jit(solution)/shard_map/ppermute | solution.py:52
  125.3 19.7 %collective-permute-done.2.refs_3_ = bf16[1024,768]{1,0:T(8,128)(2,1)S(1)} collective-permute-done((bf16[1024,768]{1,0:T(8,128)(2,1)S(1)}, bf16[1024,768]{1,0:T(8,128)(2,1)S(1)}, u32[]{:S(2)}, u32[]{:S(2)}) %collective-permute-start.2) | collective-permute-done | bytes 1572896 | tf_op jit(solution)/shard_map/ppermute | solution.py:52
  147.9 2.5 collective-permute-start.33
  150.4 2.7 collective-permute-start.4
  153.0 19.8 %block_first.1 = (f32[512,2048]{1,0:T(8,128)S(1)}, f32[528,128]{1,0:T(8,128)S(1)}, f32[528,4096]{1,0:T(8,128)}) custom-call(s32[13]{0:T(128)S(1)} %stack.101.scal, bf16[512,4096]{1,0:T(8,128)(2,1)} %refs_0_.3, bf16[2560,256]{1,0:T(8,128)(2,1)} %copy-done.17, bf16[1024,256]{1,0:T(8,128)(2,1)} %pad_maximum_fusion.5.refs_2_, bf16[2560,256]{1,0:T(8,128)(2,1)} %copy-done.22, ...), custom_call_target="tpu_custom_call" | custom-call | flops 8589934592 | bytes 25165824 | tf_op jit(solution)/shard_map/block_first/pallas_call | solution.py:202
  177.1 18.7 %block_last.1 = (f32[512,2048]{1,0:T(8,128)}, f32[528,128]{1,0:T(8,128)S(1)}, f32[256,4096]{1,0:T(8,128)S(1)}, bf16[256,4096]{1,0:T(8,128)(2,1)S(1)}, f32[16,4096]{1,0:T(8,128)S(1)}) custom-call(s32[13]{0:T(128)S(1)} %stack.91.scal, bf16[512,4096]{1,0:T(8,128)(2,1)} %refs_0_.3, bf16[512,1024]{1,0:T(8,128)(2,1)} %copy-done.13, ...), custom_call_target="tpu_custom_call", output_to_operand_aliasing={{0}: (19, {})} | custom-call | flops 8589934592 | bytes 25165824 | tf_op jit(solution)/shard_map/block_last/pallas_call | solution.py:202
  195.8 4.7 %collective-permute-start.31 = (f32[560,128]{1,0:T(8,128)S(1)}, f32[560,128]{1,0:T(8,128)S(1)}, u32[]{:S(2)}, u32[]{:S(2)}) collective-permute-start(f32[560,128]{1,0:T(8,128)S(1)} %pad_maximum_fusion.8), channel_id=1, source_target_pairs={{0,8},{1,9},{2,10},{3,11},{4,12},{5,13},{6,14},{7,15},{8,0},{9,1},... | collective-permute-start | bytes 860168 | tf_op jit(solution)/shard_map/ppermute | solution.py:52
  217.0 12.0 %all-to-all-start = ((f32[64,1,1280]{2,1,0:T(1,128)}), f32[64,1,1280]{2,1,0:T(1,128)}, u32[]{:S(2)}, u32[]{:S(2)}) async-start(f32[64,1,1280]{2,1,0:T(1,128)} %all_to_all.13), calls=%async_computation | async-start | bytes 655360 | tf_op jit(solution)/shard_map/all_to_all | solution.py:442
  231.6 2.7 collective-permute-start.35
  236.1 4.0 %collective-permute-done.35 = f32[16,2048]{1,0:T(8,128)S(1)} collective-permute-done((f32[16,2048]{1,0:T(8,128)S(1)}, f32[16,2048]{1,0:T(8,128)S(1)}, u32[]{:S(2)}, u32[]{:S(2)}) %collective-permute-start.35) | collective-permute-done | bytes 131104 | tf_op jit(solution)/shard_map/ppermute | solution.py:52
  242.2 7.5 %all-to-all-start.1 = ((f32[64,1,1280]{2,1,0:T(1,128)}), f32[64,1,1280]{2,1,0:T(1,128)S(1)}, u32[]{:S(2)}, u32[]{:S(2)}) async-start(f32[64,1,1280]{2,1,0:T(1,128)} %broadcast_in_dim.99), calls=%async_computation.1 | async-start | bytes 655360 | tf_op jit(solution)/shard_map/all_to_all | solution.py:442
  251.4 8.0 %all-to-all-done.1 = f32[64,1,1280]{2,1,0:T(1,128)S(1)} async-done(((f32[64,1,1280]{2,1,0:T(1,128)}), f32[64,1,1280]{2,1,0:T(1,128)S(1)}, u32[]{:S(2)}, u32[]{:S(2)}) %all-to-all-start.1) | async-done | bytes 327712 | tf_op jit(solution)/shard_map/all_to_all | solution.py:442
  260.3 2.4 collective-permute-start.32
  268.0 5.3 %add_convert_fusion = bf16[256,4096]{1,0:T(8,128)(2,1)} fusion(f32[256,4096]{1,0:T(8,128)} %copy-done.3, bf16[256,4096]{1,0:T(8,128)(2,1)} %collective-permute-done.37, f32[256]{0:T(256)} %slice.277, f32[4096]{0:T(1024)S(1)} %bitcast.126, f32[256]{0:T(256)} %slice.273, bf16[4096,16]{0,1:T(8,128)(2,1)S(1)} %copy-done, bf16[512,16]{1,0:T(8,128)(2,1)S(1)} %fusion.10), kind=kOutput, calls=%fused_computation.3 | convolution fusion | flops 40894464 | bytes 8603648 | tf_op jit(solution)/shard_map/dot_general | solution.py:432
  274.6 3.7 %maximum_select_fusion = bf16[1,256,4096]{2,1,0:T(8,128)(2,1)} fusion(bf16[1,256,2048]{2,1,0:T(8,128)(2,1)} %bitcast.42, bf16[1,256,2048]{2,1,0:T(8,128)(2,1)S(1)} %copy-done.7, pred[]{:T(512)S(6)} %eq.71), kind=kLoop, calls=%fused_computation.9 | loop fusion | flops 9437184 | bytes 4194305 | tf_op jit(solution)/shard_map/jit(_where)/select_n | solution.py:56
  (260 shorter events, 82.9 us)
Async XLA Ops:
  2.6 44.5 %collective-permute-start.5 = (bf16[512,256]{1,0:T(8,128)(2,1)}, bf16[512,256]{1,0:T(8,128)(2,1)}, u32[]{:S(2)}, u32[]{:S(2)}) collective-permute-start(bf16[512,256]{1,0:T(8,128)(2,1)} %get-tuple-element.63), channel_id=1, source_target_pairs={{0,20},{1,21},{2,22},{3,23},{4,16},{5,17},{6,18},{7,19},{8,28},{9,... | collective-permute-start | bytes 786440 | tf_op jit(solution)/shard_map/ppermute | solution.py:52
  8.4 10.2 %collective-permute-start.15 = (bf16[8,2176]{1,0:T(8,128)(2,1)S(1)}, bf16[8,2176]{1,0:T(8,128)(2,1)S(1)}, u32[]{:S(2)}, u32[]{:S(2)}) collective-permute-start(bf16[8,2176]{1,0:T(8,128)(2,1)S(1)} %get-tuple-element.96), channel_id=1, source_target_pairs={{0,8},{1,9},{2,10},{3,11},{4,12},{5,13},{6,14},{7,15},{8,0},{9,1},... | collective-permute-start | bytes 104456 | tf_op jit(solution)/shard_map/ppermute | solution.py:52
  11.7 70.3 %collective-permute-start = (bf16[512,1024]{1,0:T(8,128)(2,1)}, bf16[512,1024]{1,0:T(8,128)(2,1)S(1)}, u32[]{:S(2)}, u32[]{:S(2)}) collective-permute-start(bf16[512,1024]{1,0:T(8,128)(2,1)} %constant_dynamic-slice_fusion.15), channel_id=1, source_target_pairs={{0,20},{1,21},{2,22},{3,23},{4,16},{5,17},{6,18},{7,19},{8,28},{9,... | collective-permute-start | bytes 3145736 | tf_op jit(solution)/shard_map/ppermute | solution.py:52
  18.7 10.9 %collective-permute-start.20 = (bf16[8,2176]{1,0:T(8,128)(2,1)S(1)}, bf16[8,2176]{1,0:T(8,128)(2,1)S(1)}, u32[]{:S(2)}, u32[]{:S(2)}) collective-permute-start(bf16[8,2176]{1,0:T(8,128)(2,1)S(1)} %maximum_select_fusion.10), channel_id=1, source_target_pairs={{0,16},{1,17},{2,18},{3,19},{4,20},{5,21},{6,22},{7,23},{8,24},{9,... | collective-permute-start | bytes 104456 | tf_op jit(solution)/shard_map/ppermute | solution.py:52
  27.9 6.3 %collective-permute-start.22 = (bf16[32,2048]{1,0:T(8,128)(2,1)S(1)}, bf16[32,2048]{1,0:T(8,128)(2,1)S(1)}, u32[]{:S(2)}, u32[]{:S(2)}) collective-permute-start(bf16[32,2048]{1,0:T(8,128)(2,1)S(1)} %maximum_select_fusion.6), channel_id=1, source_target_pairs={{0,1},{1,0},{2,3},{3,2},{4,5},{5,4},{6,7},{7,6},{8,9},{9,8},{10,11... | collective-permute-start | bytes 393224 | tf_op jit(solution)/shard_map/ppermute | solution.py:52
  29.6 12.6 %collective-permute-start.21 = (bf16[16,2176]{1,0:T(8,128)(2,1)S(1)}, bf16[16,2176]{1,0:T(8,128)(2,1)S(1)}, u32[]{:S(2)}, u32[]{:S(2)}) collective-permute-start(bf16[16,2176]{1,0:T(8,128)(2,1)S(1)} %maximum_select_fusion.8), channel_id=1, source_target_pairs={{0,20},{1,21},{2,22},{3,23},{4,16},{5,17},{6,18},{7,19},{8,28},{9,... | collective-permute-start | bytes 208904 | tf_op jit(solution)/shard_map/ppermute | solution.py:52
  32.2 81.7 %collective-permute-start.18 = (bf16[256,4096]{1,0:T(8,128)(2,1)S(1)}, bf16[256,4096]{1,0:T(8,128)(2,1)S(1)}, u32[]{:S(2)}, u32[]{:S(2)}) collective-permute-start(bf16[256,4096]{1,0:T(8,128)(2,1)S(1)} %bitcast.117), channel_id=1, source_target_pairs={{0,8},{1,9},{2,10},{3,11},{4,12},{5,13},{6,14},{7,15},{8,0},{9,1},... | collective-permute-start | bytes 6291464 | tf_op jit(solution)/shard_map/ppermute | solution.py:52
  34.3 7.9 %collective-permute-start.23 = (bf16[64,2048]{1,0:T(8,128)(2,1)S(1)}, bf16[64,2048]{1,0:T(8,128)(2,1)S(1)}, u32[]{:S(2)}, u32[]{:S(2)}) collective-permute-start(bf16[64,2048]{1,0:T(8,128)(2,1)S(1)} %maximum_select_fusion.2), channel_id=1, source_target_pairs={{0,3},{1,2},{2,1},{3,0},{4,7},{5,6},{6,5},{7,4},{8,11},{9,10},{10,... | collective-permute-start | bytes 786440 | tf_op jit(solution)/shard_map/ppermute | solution.py:52
  48.2 19.8 %collective-permute-start.6 = (bf16[1536,256]{1,0:T(8,128)(2,1)S(1)}, bf16[1536,256]{1,0:T(8,128)(2,1)S(1)}, u32[]{:S(2)}, u32[]{:S(2)}) collective-permute-start(bf16[1536,256]{1,0:T(8,128)(2,1)S(1)} %pad_maximum_fusion.3), channel_id=1, source_target_pairs={{0,1},{1,2},{2,3},{3,0},{4,5},{5,6},{6,7},{7,4},{8,9},{9,10},{10,1... | collective-permute-start | bytes 2359304 | tf_op jit(solution)/shard_map/ppermute | solution.py:52
  48.6 19.6 %collective-permute-start.7 = (bf16[1536,256]{1,0:T(8,128)(2,1)S(1)}, bf16[1536,256]{1,0:T(8,128)(2,1)S(1)}, u32[]{:S(2)}, u32[]{:S(2)}) collective-permute-start(bf16[1536,256]{1,0:T(8,128)(2,1)S(1)} %pad_maximum_fusion.3), channel_id=1, source_target_pairs={{0,3},{1,0},{2,1},{3,2},{4,7},{5,4},{6,5},{7,6},{8,11},{9,8},{10,9... | collective-permute-start | bytes 2359304 | tf_op jit(solution)/shard_map/ppermute | solution.py:52
  68.1 10.5 %collective-permute-start.11 = (bf16[768,256]{1,0:T(8,128)(2,1)S(1)}, bf16[768,256]{1,0:T(8,128)(2,1)S(1)}, u32[]{:S(2)}, u32[]{:S(2)}) collective-permute-start(bf16[768,256]{1,0:T(8,128)(2,1)S(1)} %pad_maximum_fusion.6), channel_id=1, source_target_pairs={{0,1},{1,2},{2,3},{3,0},{4,5},{5,6},{6,7},{7,4},{8,9},{9,10},{10,1... | collective-permute-start | bytes 1179656 | tf_op jit(solution)/shard_map/ppermute | solution.py:52
  68.3 10.3 %collective-permute-start.12 = (bf16[768,256]{1,0:T(8,128)(2,1)S(1)}, bf16[768,256]{1,0:T(8,128)(2,1)S(1)}, u32[]{:S(2)}, u32[]{:S(2)}) collective-permute-start(bf16[768,256]{1,0:T(8,128)(2,1)S(1)} %pad_maximum_fusion.7), channel_id=1, source_target_pairs={{0,3},{1,0},{2,1},{3,2},{4,7},{5,4},{6,5},{7,6},{8,11},{9,8},{10,9... | collective-permute-start | bytes 1179656 | tf_op jit(solution)/shard_map/ppermute | solution.py:52
  72.2 44.6 %collective-permute-start.10 = (bf16[2560,256]{1,0:T(8,128)(2,1)S(1)}, bf16[2560,256]{1,0:T(8,128)(2,1)S(1)}, u32[]{:S(2)}, u32[]{:S(2)}) collective-permute-start(bf16[2560,256]{1,0:T(8,128)(2,1)S(1)} %pad_maximum_fusion.1.refs_1_), channel_id=1, source_target_pairs={{0,96},{1,97},{2,98},{3,99},{4,100},{5,101},{6,102},{7,103},{8,104... | collective-permute-start | bytes 3932168 | tf_op jit(solution)/shard_map/ppermute | solution.py:52
  79.6 32.4 %collective-permute-start.13 = (bf16[1024,256]{1,0:T(8,128)(2,1)}, bf16[1024,256]{1,0:T(8,128)(2,1)S(1)}, u32[]{:S(2)}, u32[]{:S(2)}) collective-permute-start(bf16[1024,256]{1,0:T(8,128)(2,1)} %pad_maximum_fusion.5.refs_2_), channel_id=1, source_target_pairs={{0,96},{1,97},{2,98},{3,99},{4,100},{5,101},{6,102},{7,103},{8,104... | collective-permute-start | bytes 1572872 | tf_op jit(solution)/shard_map/ppermute | solution.py:52
  81.8 37.3 %collective-permute-start.8 = (bf16[2560,256]{1,0:T(8,128)(2,1)S(1)}, bf16[2560,256]{1,0:T(8,128)(2,1)S(1)}, u32[]{:S(2)}, u32[]{:S(2)}) collective-permute-start(bf16[2560,256]{1,0:T(8,128)(2,1)S(1)} %pad_maximum_fusion.1.refs_1_), channel_id=1, source_target_pairs={{0,32},{1,33},{2,34},{3,35},{4,36},{5,37},{6,38},{7,39},{8,40},{9,... | collective-permute-start | bytes 3932168 | tf_op jit(solution)/shard_map/ppermute | solution.py:52
  83.0 39.0 %collective-permute-start.1 = (bf16[1024,768]{1,0:T(8,128)(2,1)S(1)}, bf16[1024,768]{1,0:T(8,128)(2,1)S(1)}, u32[]{:S(2)}, u32[]{:S(2)}) collective-permute-start(bf16[1024,768]{1,0:T(8,128)(2,1)S(1)} %pad_maximum_fusion), channel_id=1, source_target_pairs={{0,1},{1,2},{2,3},{3,0},{4,5},{5,6},{6,7},{7,4},{8,9},{9,10},{10,1... | collective-permute-start | bytes 4718600 | tf_op jit(solution)/shard_map/ppermute | solution.py:52
  111.9 33.1 %collective-permute-start.2 = (bf16[1024,768]{1,0:T(8,128)(2,1)S(1)}, bf16[1024,768]{1,0:T(8,128)(2,1)S(1)}, u32[]{:S(2)}, u32[]{:S(2)}) collective-permute-start(bf16[1024,768]{1,0:T(8,128)(2,1)S(1)} %pad_maximum_fusion), channel_id=1, source_target_pairs={{0,3},{1,0},{2,1},{3,2},{4,7},{5,4},{6,5},{7,6},{8,11},{9,8},{10,9... | collective-permute-start | bytes 4718600 | tf_op jit(solution)/shard_map/ppermute | solution.py:52
  113.9 33.9 %collective-permute-start.19 = (bf16[256,2048]{1,0:T(8,128)(2,1)}, bf16[256,2048]{1,0:T(8,128)(2,1)}, u32[]{:S(2)}, u32[]{:S(2)}) collective-permute-start(bf16[256,2048]{1,0:T(8,128)(2,1)} %constant_dynamic-slice_fusion.13), channel_id=1, source_target_pairs={{0,8},{1,9},{2,10},{3,11},{4,12},{5,13},{6,14},{7,15},{8,0},{9,1},... | collective-permute-start | bytes 3145736 | tf_op jit(solution)/shard_map/ppermute | solution.py:52
  116.8 33.5 %collective-permute-start.30 = (bf16[1536,256]{1,0:T(8,128)(2,1)}, bf16[1536,256]{1,0:T(8,128)(2,1)}, u32[]{:S(2)}, u32[]{:S(2)}) collective-permute-start(bf16[1536,256]{1,0:T(8,128)(2,1)} %pad_maximum_fusion.4), channel_id=1, source_target_pairs={{0,20},{1,21},{2,22},{3,23},{4,16},{5,17},{6,18},{7,19},{8,28},{9,... | collective-permute-start | bytes 2359304 | tf_op jit(solution)/shard_map/ppermute | solution.py:52
  119.2 31.1 %collective-permute-start.29 = (bf16[1024,256]{1,0:T(8,128)(2,1)}, bf16[1024,256]{1,0:T(8,128)(2,1)S(1)}, u32[]{:S(2)}, u32[]{:S(2)}) collective-permute-start(bf16[1024,256]{1,0:T(8,128)(2,1)} %pad_maximum_fusion.5.refs_2_), channel_id=1, source_target_pairs={{0,32},{1,33},{2,34},{3,35},{4,36},{5,37},{6,38},{7,39},{8,40},{9,... | collective-permute-start | bytes 1572872 | tf_op jit(solution)/shard_map/ppermute | solution.py:52
  122.0 53.0 %collective-permute-start.14 = (bf16[1792,256]{1,0:T(8,128)(2,1)}, bf16[1792,256]{1,0:T(8,128)(2,1)}, u32[]{:S(2)}, u32[]{:S(2)}) collective-permute-start(bf16[1792,256]{1,0:T(8,128)(2,1)} %pad_maximum_fusion.2), channel_id=1, source_target_pairs={{0,96},{1,97},{2,98},{3,99},{4,100},{5,101},{6,102},{7,103},{8,104... | collective-permute-start | bytes 2752520 | tf_op jit(solution)/shard_map/ppermute | solution.py:52
  145.0 29.9 %collective-permute-start.9 = (bf16[1792,256]{1,0:T(8,128)(2,1)}, bf16[1792,256]{1,0:T(8,128)(2,1)}, u32[]{:S(2)}, u32[]{:S(2)}) collective-permute-start(bf16[1792,256]{1,0:T(8,128)(2,1)} %slice.291), channel_id=1, source_target_pairs={{0,32},{1,33},{2,34},{3,35},{4,36},{5,37},{6,38},{7,39},{8,40},{9,... | collective-permute-start | bytes 2752520 | tf_op jit(solution)/shard_map/ppermute | solution.py:52
  147.9 52.8 %collective-permute-start.33 = (f32[64,2048]{1,0:T(8,128)}, f32[64,2048]{1,0:T(8,128)S(1)}, u32[]{:S(2)}, u32[]{:S(2)}) collective-permute-start(f32[64,2048]{1,0:T(8,128)} %constant_dynamic-slice_fusion.8), channel_id=1, source_target_pairs={{0,3},{1,2},{2,1},{3,0},{4,7},{5,6},{6,5},{7,4},{8,11},{9,10},{10,... | collective-permute-start | bytes 1572872 | tf_op jit(solution)/shard_map/ppermute | solution.py:52
  150.3 25.6 %collective-permute-start.3 = (bf16[512,768]{1,0:T(8,128)(2,1)S(1)}, bf16[512,768]{1,0:T(8,128)(2,1)S(1)}, u32[]{:S(2)}, u32[]{:S(2)}) collective-permute-start(bf16[512,768]{1,0:T(8,128)(2,1)S(1)} %slice.287), channel_id=1, source_target_pairs={{0,1},{1,2},{2,3},{3,0},{4,5},{5,6},{6,7},{7,4},{8,9},{9,10},{10,1... | collective-permute-start | bytes 2359304 | tf_op jit(solution)/shard_map/ppermute | solution.py:52
  150.4 25.6 %collective-permute-start.4 = (bf16[512,768]{1,0:T(8,128)(2,1)S(1)}, bf16[512,768]{1,0:T(8,128)(2,1)S(1)}, u32[]{:S(2)}, u32[]{:S(2)}) collective-permute-start(bf16[512,768]{1,0:T(8,128)(2,1)S(1)} %slice.288), channel_id=1, source_target_pairs={{0,3},{1,0},{2,1},{3,2},{4,7},{5,4},{6,5},{7,6},{8,11},{9,8},{10,9... | collective-permute-start | bytes 2359304 | tf_op jit(solution)/shard_map/ppermute | solution.py:52
  200.5 67.4 %collective-permute-start.37 = (bf16[256,4096]{1,0:T(8,128)(2,1)S(1)}, bf16[256,4096]{1,0:T(8,128)(2,1)}, u32[]{:S(2)}, u32[]{:S(2)}) collective-permute-start(bf16[256,4096]{1,0:T(8,128)(2,1)S(1)} %get-tuple-element.45), channel_id=1, source_target_pairs={{0,8},{1,9},{2,10},{3,11},{4,12},{5,13},{6,14},{7,15},{8,0},{9,1},... | collective-permute-start | bytes 6291464 | tf_op jit(solution)/shard_map/ppermute | solution.py:52
  201.4 29.1 %collective-permute-start.34 = (f32[32,2048]{1,0:T(8,128)}, f32[32,2048]{1,0:T(8,128)}, u32[]{:S(2)}, u32[]{:S(2)}) collective-permute-start(f32[32,2048]{1,0:T(8,128)} %constant_dynamic-slice_fusion.7), channel_id=1, source_target_pairs={{0,1},{1,0},{2,3},{3,2},{4,5},{5,4},{6,7},{7,6},{8,9},{9,8},{10,11... | collective-permute-start | bytes 786440 | tf_op jit(solution)/shard_map/ppermute | solution.py:52
  217.0 23.1 %all-to-all-start = ((f32[64,1,1280]{2,1,0:T(1,128)}), f32[64,1,1280]{2,1,0:T(1,128)}, u32[]{:S(2)}, u32[]{:S(2)}) async-start(f32[64,1,1280]{2,1,0:T(1,128)} %all_to_all.13), calls=%async_computation | async-start | bytes 655360 | tf_op jit(solution)/shard_map/all_to_all | solution.py:442
  229.0 45.7 %collective-permute-start.39 = (bf16[256,2048]{1,0:T(8,128)(2,1)}, bf16[256,2048]{1,0:T(8,128)(2,1)}, u32[]{:S(2)}, u32[]{:S(2)}) collective-permute-start(bf16[256,2048]{1,0:T(8,128)(2,1)} %get-tuple-element.66), channel_id=1, source_target_pairs={{0,8},{1,9},{2,10},{3,11},{4,12},{5,13},{6,14},{7,15},{8,0},{9,1},... | collective-permute-start | bytes 3145736 | tf_op jit(solution)/shard_map/ppermute | solution.py:52
  231.6 8.6 %collective-permute-start.35 = (f32[16,2048]{1,0:T(8,128)S(1)}, f32[16,2048]{1,0:T(8,128)S(1)}, u32[]{:S(2)}, u32[]{:S(2)}) collective-permute-start(f32[16,2048]{1,0:T(8,128)S(1)} %constant_dynamic-slice_fusion.6), channel_id=1, source_target_pairs={{0,96},{1,97},{2,98},{3,99},{4,100},{5,101},{6,102},{7,103},{8,104... | collective-permute-start | bytes 393224 | tf_op jit(solution)/shard_map/ppermute | solution.py:52
  242.2 17.2 %all-to-all-start.1 = ((f32[64,1,1280]{2,1,0:T(1,128)}), f32[64,1,1280]{2,1,0:T(1,128)S(1)}, u32[]{:S(2)}, u32[]{:S(2)}) async-start(f32[64,1,1280]{2,1,0:T(1,128)} %broadcast_in_dim.99), calls=%async_computation.1 | async-start | bytes 655360 | tf_op jit(solution)/shard_map/all_to_all | solution.py:442
  250.4 22.8 %collective-permute-start.36 = (f32[8,2048]{1,0:T(8,128)}, f32[8,2048]{1,0:T(8,128)}, u32[]{:S(2)}, u32[]{:S(2)}) collective-permute-start(f32[8,2048]{1,0:T(8,128)} %constant_dynamic-slice_fusion.5), channel_id=1, source_target_pairs={{0,32},{1,33},{2,34},{3,35},{4,36},{5,37},{6,38},{7,39},{8,40},{9,... | collective-permute-start | bytes 196616 | tf_op jit(solution)/shard_map/ppermute | solution.py:52
  (44 other events, 438.9 us)

commit v3 on v2

--- a/solution.py
+++ b/solution.py
@@ -69,11 +69,14 @@
     a_own, a_par, r_own, r_par, low, up, q_rows, q_f = refs[n_src : n_src + 8]
     rest = refs[n_src + 8 :]
     if first:
-        hid_out, st_out, y_out = rest[:3]
-        w_s, a_s, r_s, hid, hb_s, y_s, w_sem, in_sem, out_sem = rest[3:]
+        hid_out, st_out, y_q, y_out = rest[:4]
+        scratch = rest[4:]
     else:
-        y_in, st_in, _, hid_out, st_out, y_own, y_par, y_q = rest[:8]
-        w_s, a_s, r_s, hid, hb_s, y_s, w_sem, in_sem, out_sem, yo_s, yp_s = rest[8:]
+        y_in, st_in, vq_in, _, hid_out, st_out, y_q, y_own, y_par = rest[:9]
+        scratch = rest[9:]
+    w_s, a_s, r_s, hid, ht_s, y_s, up_s, qf_s, qb_s, qt_s, w_sem, in_sem, out_sem = scratch[:13]
+    if not first:
+        yo_s, yp_s = scratch[13:]
     half = pl.multiple_of(scal[12], 2048)
     inputs = [
         pltpu.make_async_copy(a_own, a_s.at[pl.ds(0, 256), :], in_sem.at[0]),
@@ -112,43 +115,61 @@
     for copy in inputs:
         copy.wait()
     st_out[...] = jnp.zeros_like(st_out) if first else st_in[...]
+    qb_s[...] = jnp.zeros_like(qb_s)
+    for j in range(4):
+        here = pl.ds(j * 256, 256)
+        col = pl.ds(pl.multiple_of(scal[8 + j] * 256, 256), 256)
+        up_s[:, here] = up[:, col]
+        qf_s[:, here] = q_f[:, col]
+        qb_s[pl.ds(0, 16), here] = q_rows[:, col]
+    qt_s[...] = qb_s[...].T
 
     def forward(j, carry):
-        here = pl.ds(pl.multiple_of(j * 256, 256), 256)
-        col = pl.ds(pl.multiple_of(scal[8 + j] * 256, 256), 256)
-        pltpu.make_async_copy(w_s.at[:, here], w_s.at[:, here], w_sem.at[j]).wait()
+        here = pl.ds(pl.multiple_of(j * 512, 512), 512)
+        for k in range(2):
+            part = pl.ds(pl.multiple_of(j * 512 + k * 256, 256), 256)
+            pltpu.make_async_copy(w_s.at[:, part], w_s.at[:, part], w_sem.at[2 * j + k]).wait()
         value = (
             r_s[:, here].astype(f32)
-            + adapter_scale * jnp.dot(low[...], up[:, col], preferred_element_type=f32)
+            + adapter_scale * jnp.dot(low[...], up_s[:, here], preferred_element_type=f32)
             + jnp.dot(a_s[...], w_s[:, here], preferred_element_type=f32)
         )
         hid[:, here] = value
-        pltpu.make_async_copy(hid.at[:, here], hid_out.at[:, col], out_sem.at[2]).start()
-        hb_s[pl.ds(0, 512), here] = value.astype(bf16)
-        hb_s[pl.ds(512, 16), here] = q_rows[:, col]
-        st_out[:, 0:16] += lax.dot_general(
-            hb_s[:, here], up[:, col], NT, preferred_element_type=f32
+        for k in range(2):
+            part = pl.ds(pl.multiple_of(j * 512 + k * 256, 256), 256)
+            col = pl.ds(pl.multiple_of(scal[8 + 2 * j + k] * 256, 256), 256)
+            pltpu.make_async_copy(hid.at[:, part], hid_out.at[:, col], out_sem.at[2]).start()
+        short = value.astype(bf16)
+        ht_s[here, :] = short.T
+        st_out[0:512, 0:16] += lax.dot_general(
+            short, up_s[:, here], NT, preferred_element_type=f32
+        )
+        st_out[512:528, 0:16] += lax.dot_general(
+            qb_s[0:16, here], up_s[:, here], NT, preferred_element_type=f32
         )
         st_out[0:512, 16:17] += jnp.sum(value * value, axis=1, keepdims=True)
-        st_out[0:256, 17:18] += jnp.sum(value[:256] * q_f[0:1, col], axis=1, keepdims=True)
-        st_out[256:512, 17:18] += jnp.sum(value[256:] * q_f[1:2, col], axis=1, keepdims=True)
+        st_out[0:256, 17:18] += jnp.sum(value[:256] * qf_s[0:1, here], axis=1, keepdims=True)
+        st_out[256:512, 17:18] += jnp.sum(value[256:] * qf_s[1:2, here], axis=1, keepdims=True)
         return carry
 
-    lax.fori_loop(0, 4, forward, 0)
+    lax.fori_loop(0, 2, forward, 0)
     if not first:
         y_copy.wait()
 
     def backward(shard, carry):
         columns = pl.ds(pl.multiple_of(scal[shard] * 512, 512), 512)
-        part = lax.dot_general(hb_s[...], w_s[columns, :], NT, preferred_element_type=f32)
+        rows = w_s[columns, :]
+        part = jnp.dot(rows, ht_s[...], preferred_element_type=f32)
+        vq = jnp.dot(rows, qt_s[...], preferred_element_type=f32).T[:16]
         if first:
-            y_s[:, columns] = part
-            pltpu.make_async_copy(y_s.at[:, columns], y_out.at[:, columns], out_sem.at[0]).start()
+            y_q[:, columns] = vq
+            y_s[columns, :] = part
+            pltpu.make_async_copy(y_s.at[columns, :], y_out.at[columns, :], out_sem.at[0]).start()
         else:
-            part += y_s[:, columns]
-            yo_s[:, columns] = part[:256]
-            yp_s[:, columns] = part[256:512].astype(bf16)
-            y_q[:, columns] = part[512:]
+            y_q[:, columns] = vq + vq_in[:, columns]
+            turned = (part + y_s[columns, :]).astype(bf16).T
+            yo_s[:, columns] = turned[:256]
+            yp_s[:, columns] = turned[256:]
             pltpu.make_async_copy(yo_s.at[:, columns], y_own.at[:, columns], out_sem.at[0]).start()
             pltpu.make_async_copy(yp_s.at[:, columns], y_par.at[:, columns], out_sem.at[1]).start()
         return carry
@@ -166,7 +187,12 @@
     vm = pl.BlockSpec(memory_space=pltpu.VMEM)
     anyspace = pl.BlockSpec(memory_space=pltpu.HBM)
     first = carry is None
-    shapes = [jax.ShapeDtypeStruct((512, 2048), f32), jax.ShapeDtypeStruct((528, 128), f32)]
+    shapes = [
+        jax.ShapeDtypeStruct((512, 2048), f32),
+        jax.ShapeDtypeStruct((528, 128), f32),
+        jax.ShapeDtypeStruct((16, 4096), f32),
+    ]
+    out_specs = [anyspace, vm, vm]
     args = [scal, *srcs, a_own, a_par, r_own, r_par, low, up, q_rows, q_f]
     in_specs = [pl.BlockSpec(memory_space=pltpu.SMEM)] + [anyspace] * (len(srcs) + 4) + [vm] * 4
     scratch = [
@@ -174,26 +200,26 @@
         pltpu.VMEM((512, 4096), bf16),
         pltpu.VMEM((512, 1024), bf16),
         pltpu.VMEM((512, 1024), f32),
-        pltpu.VMEM((528, 1024), bf16),
-        pltpu.VMEM((528, 4096), f32),
+        pltpu.VMEM((1024, 512), bf16),
+        pltpu.VMEM((4096, 512), f32),
+        pltpu.VMEM((16, 1024), bf16),
+        pltpu.VMEM((8, 1024), f32),
+        pltpu.VMEM((128, 1024), bf16),
+        pltpu.VMEM((1024, 128), bf16),
         pltpu.SemaphoreType.DMA((4,)),
         pltpu.SemaphoreType.DMA((11,)),
         pltpu.SemaphoreType.DMA((3,)),
     ]
     if first:
-        shapes += [jax.ShapeDtypeStruct((528, 4096), f32)]
-        out_specs = [anyspace, vm, anyspace]
+        shapes += [jax.ShapeDtypeStruct((4096, 512), f32)]
+        out_specs += [anyspace]
         aliases = {}
     else:
-        shapes += [
-            jax.ShapeDtypeStruct((256, 4096), f32),
-            jax.ShapeDtypeStruct((256, 4096), bf16),
-            jax.ShapeDtypeStruct((16, 4096), f32),
-        ]
-        out_specs = [anyspace, vm, anyspace, anyspace, vm]
-        scratch += [pltpu.VMEM((256, 4096), f32), pltpu.VMEM((256, 4096), bf16)]
-        in_specs += [anyspace, vm, anyspace]
-        args += [carry[2], carry[1], carry[0]]
+        shapes += [jax.ShapeDtypeStruct((256, 4096), bf16)] * 2
+        out_specs += [anyspace, anyspace]
+        scratch += [pltpu.VMEM((256, 4096), bf16)] * 2
+        in_specs += [anyspace, vm, vm, anyspace]
+        args += [carry[3], carry[1], carry[2], carry[0]]
         aliases = {len(args) - 1: 0}
     args = [
         pltpu.with_memory_space_constraint(arg, pltpu.HBM) if spec is anyspace else arg
@@ -393,7 +419,7 @@
     late.land(y_far1, [(2, 256, 256), five[4]] + two, 0)
     shared = (a_own, a_par, res_own, r_par, low, up_half, q_rows, q_f)
     carry = block_call(early.copies, early.srcs, numbers(ring[:3] + [4]), *shared, None)
-    hidden, stats_own, y_own, y_par, y_q = block_call(
+    hidden, stats_own, y_q, y_own, y_par = block_call(
         late.copies, late.srcs, numbers(ring[3:] + [5, 6, 7]), *shared, carry
     )
 
@@ -428,7 +454,7 @@
     residual_grad = ordered(c, res_grad[:256], r_got, axis=1)
     attn_grad = (
         lead[:256, None] * v
-        - back[:256, None] * (y_own + y_got.astype(f32))
+        - back[:256, None] * (y_own.astype(f32) + y_got.astype(f32))
         + lax.dot_general(low_grad[:256], adapter_down_weight, NT, preferred_element_type=f32)
     ).astype(bf16)
 

time: 282 us -> 283 us (level)
  Pallas kernels: 38.5 us -> 41.9 us
    pallas_call x2, Pallas kernels: 38.5 us -> 41.9 us  [block_call(): pl.pallas_call(functools.partial(block_kernel, copies, len(srcs), first),...]
    unnamed x64 -> x74, local copies, waits for them, and re-layouts: 7.19 us -> 7.24 us
  transfers between devices with their start and end apart: 42 -> 42, of which waited for: 15 -> 14; matrix products, arithmetic and copies ran while one was open for 21% -> 20% of each run, Pallas kernels for 14% -> 15%
where the time goes in v3:
time: 283 us; the launch traced here: 282 us
  waiting for transfers between devices  83.2 us (29%)
  starting transfers between devices  80.8 us (29%)
  Pallas kernels  41.9 us (15%)
  local copies, waits for them, and re-layouts  32.1 us (11%)
  other arithmetic  24.1 us (9%)
  matrix products  11.1 us (4%)
  between operations  8.64 us (3%)
    ppermute x40, waiting for transfers between devices, send(): return lax.ppermute(value, AX, MOVES[move])  74.7 us
    ppermute x40, starting transfers between devices, send(): return lax.ppermute(value, AX, MOVES[move])  61.5 us
    pallas_call x2, Pallas kernels, block_call(): pl.pallas_call(functools.partial(block_kernel, copies, len(srcs), first),...  41.9 us
    all_to_all x2, starting transfers between devices, compute(): lax.all_to_all(value, AX, 0, 0, axis_index_groups=sides, tiled=True)  19.3 us
    all_to_all x2, waiting for transfers between devices, compute(): lax.all_to_all(value, AX, 0, 0, axis_index_groups=sides, tiled=True)  8.5 us
    dynamic_slice x13, local copies, waits for them, and re-layouts, pick(): return lax.dynamic_slice_in_dim(value, start, size, axis=axis)  7.86 us
    unnamed x74, local copies, waits for them, and re-layouts  7.24 us
  transfers between devices with their start and end apart: 42, of which 14 were waited for; matrix products, arithmetic and copies ran while one was open for 20% of the time, Pallas kernels for 15%

profile of v3, /device:TPU:1, one launch (start us, length us, event | category | flops | bytes accessed | tf_op | source)
XLA Modules:
  0.0 281.9 jit_solution(17603900570229715558)
XLA Ops:
  2.6 3.3 %collective-permute-start.5 = (bf16[512,256]{1,0:T(8,128)(2,1)}, bf16[512,256]{1,0:T(8,128)(2,1)}, u32[]{:S(2)}, u32[]{:S(2)}) collective-permute-start(bf16[512,256]{1,0:T(8,128)(2,1)} %get-tuple-element.65), channel_id=1, source_target_pairs={{0,20},{1,21},{2,22},{3,23},{4,16},{5,17},{6,18},{7,19},{8,28},{9,... | collective-permute-start | bytes 786440 | tf_op jit(solution)/shard_map/ppermute | solution.py:52
  9.4 2.3 constant_dynamic-slice_fusion.15
  29.7 2.6 collective-permute-start.21
  34.3 2.3 collective-permute-start.23
  38.4 3.8 %collective-permute-done.23 = bf16[64,2048]{1,0:T(8,128)(2,1)S(1)} collective-permute-done((bf16[64,2048]{1,0:T(8,128)(2,1)S(1)}, bf16[64,2048]{1,0:T(8,128)(2,1)S(1)}, u32[]{:S(2)}, u32[]{:S(2)}) %collective-permute-start.23) | collective-permute-done | bytes 262176 | tf_op jit(solution)/shard_map/ppermute | solution.py:52
  48.6 2.4 collective-permute-start.7
  51.0 2.2 collective-permute-start.26
  55.8 2.2 collective-permute-start.27
  61.3 3.4 %collective-permute-done.28 = f32[8,2048]{1,0:T(8,128)S(1)} collective-permute-done((f32[8,2048]{1,0:T(8,128)S(1)}, f32[8,2048]{1,0:T(8,128)S(1)}, u32[]{:S(2)}, u32[]{:S(2)}) %collective-permute-start.28) | collective-permute-done | bytes 65568 | tf_op jit(solution)/shard_map/ppermute | solution.py:52
  64.7 3.3 %collective-permute-done.6.refs_8_ = bf16[1536,256]{1,0:T(8,128)(2,1)S(1)} collective-permute-done((bf16[1536,256]{1,0:T(8,128)(2,1)S(1)}, bf16[1536,256]{1,0:T(8,128)(2,1)S(1)}, u32[]{:S(2)}, u32[]{:S(2)}) %collective-permute-start.6) | collective-permute-done | bytes 786464 | tf_op jit(solution)/shard_map/ppermute | solution.py:52
  68.3 2.7 collective-permute-start.12
  72.2 2.3 collective-permute-start.10
  74.5 4.0 %collective-permute-done.11.refs_10_ = bf16[768,256]{1,0:T(8,128)(2,1)S(1)} collective-permute-done((bf16[768,256]{1,0:T(8,128)(2,1)S(1)}, bf16[768,256]{1,0:T(8,128)(2,1)S(1)}, u32[]{:S(2)}, u32[]{:S(2)}) %collective-permute-start.11) | collective-permute-done | bytes 393248 | tf_op jit(solution)/shard_map/ppermute | solution.py:52
  79.6 2.3 collective-permute-start.13
  83.1 28.9 %collective-permute-done.13.refs_6_ = bf16[1024,256]{1,0:T(8,128)(2,1)S(1)} collective-permute-done((bf16[1024,256]{1,0:T(8,128)(2,1)}, bf16[1024,256]{1,0:T(8,128)(2,1)S(1)}, u32[]{:S(2)}, u32[]{:S(2)}) %collective-permute-start.13) | collective-permute-done | bytes 524320 | tf_op jit(solution)/shard_map/ppermute | solution.py:52
  114.0 2.9 %collective-permute-start.19 = (bf16[256,2048]{1,0:T(8,128)(2,1)}, bf16[256,2048]{1,0:T(8,128)(2,1)}, u32[]{:S(2)}, u32[]{:S(2)}) collective-permute-start(bf16[256,2048]{1,0:T(8,128)(2,1)} %constant_dynamic-slice_fusion.13), channel_id=1, source_target_pairs={{0,8},{1,9},{2,10},{3,11},{4,12},{5,13},{6,14},{7,15},{8,0},{9,1},... | collective-permute-start | bytes 3145736 | tf_op jit(solution)/shard_map/ppermute | solution.py:52
  116.9 2.3 collective-permute-start.30
  122.2 3.3 %collective-permute-start.14 = (bf16[1792,256]{1,0:T(8,128)(2,1)}, bf16[1792,256]{1,0:T(8,128)(2,1)}, u32[]{:S(2)}, u32[]{:S(2)}) collective-permute-start(bf16[1792,256]{1,0:T(8,128)(2,1)} %pad_maximum_fusion.2), channel_id=1, source_target_pairs={{0,96},{1,97},{2,98},{3,99},{4,100},{5,101},{6,102},{7,103},{8,104... | collective-permute-start | bytes 2752520 | tf_op jit(solution)/shard_map/ppermute | solution.py:52
  125.5 19.6 %collective-permute-done.2.refs_3_ = bf16[1024,768]{1,0:T(8,128)(2,1)S(1)} collective-permute-done((bf16[1024,768]{1,0:T(8,128)(2,1)S(1)}, bf16[1024,768]{1,0:T(8,128)(2,1)S(1)}, u32[]{:S(2)}, u32[]{:S(2)}) %collective-permute-start.2) | collective-permute-done | bytes 1572896 | tf_op jit(solution)/shard_map/ppermute | solution.py:52
  147.9 2.5 collective-permute-start.33
  150.4 2.7 collective-permute-start.4
  153.1 20.9 %block_first.1 = (f32[512,2048]{1,0:T(8,128)S(1)}, f32[528,128]{1,0:T(8,128)S(1)}, f32[16,4096]{1,0:T(8,128)S(1)}, f32[4096,512]{1,0:T(8,128)}) custom-call(s32[13]{0:T(128)S(1)} %stack.101.scal, bf16[512,4096]{1,0:T(8,128)(2,1)} %refs_0_.3, bf16[2560,256]{1,0:T(8,128)(2,1)} %copy-done.16, bf16[1024,256]{1,0:T(8,128)(2,1)} %pad_maximum_fusion.5.refs_2_, ...), custom_call_target="tpu_custom_call" | custom-call | flops 8589934592 | bytes 25165824 | tf_op jit(solution)/shard_map/block_first/pallas_call | solution.py:228
  177.3 20.9 %block_last.1 = (f32[512,2048]{1,0:T(8,128)}, f32[528,128]{1,0:T(8,128)S(1)}, f32[16,4096]{1,0:T(8,128)S(1)}, bf16[256,4096]{1,0:T(8,128)(2,1)S(1)}, bf16[256,4096]{1,0:T(8,128)(2,1)}) custom-call(s32[13]{0:T(128)S(1)} %stack.91.scal, bf16[512,4096]{1,0:T(8,128)(2,1)} %refs_0_.3, bf16[512,1024]{1,0:T(8,128)(2,1)} %copy-done.12, ...), custom_call_target="tpu_custom_call", output_to_operand_aliasing={{0}: (20, {})} | custom-call | flops 8589934592 | bytes 25165824 | tf_op jit(solution)/shard_map/block_last/pallas_call | solution.py:228
  198.4 4.5 %collective-permute-start.31 = (f32[560,128]{1,0:T(8,128)S(1)}, f32[560,128]{1,0:T(8,128)S(1)}, u32[]{:S(2)}, u32[]{:S(2)}) collective-permute-start(f32[560,128]{1,0:T(8,128)S(1)} %pad_maximum_fusion.8), channel_id=1, source_target_pairs={{0,8},{1,9},{2,10},{3,11},{4,12},{5,13},{6,14},{7,15},{8,0},{9,1},... | collective-permute-start | bytes 860168 | tf_op jit(solution)/shard_map/ppermute | solution.py:52
  219.4 11.7 %all-to-all-start = ((f32[64,1,1280]{2,1,0:T(1,128)}), f32[64,1,1280]{2,1,0:T(1,128)}, u32[]{:S(2)}, u32[]{:S(2)}) async-start(f32[64,1,1280]{2,1,0:T(1,128)} %all_to_all.13), calls=%async_computation | async-start | bytes 655360 | tf_op jit(solution)/shard_map/all_to_all | solution.py:468
  233.2 2.7 collective-permute-start.35
  237.1 4.6 %collective-permute-done.35 = f32[16,2048]{1,0:T(8,128)S(1)} collective-permute-done((f32[16,2048]{1,0:T(8,128)S(1)}, f32[16,2048]{1,0:T(8,128)S(1)}, u32[]{:S(2)}, u32[]{:S(2)}) %collective-permute-start.35) | collective-permute-done | bytes 131104 | tf_op jit(solution)/shard_map/ppermute | solution.py:52
  243.8 7.6 %all-to-all-start.1 = ((f32[64,1,1280]{2,1,0:T(1,128)}), f32[64,1,1280]{2,1,0:T(1,128)S(1)}, u32[]{:S(2)}, u32[]{:S(2)}) async-start(f32[64,1,1280]{2,1,0:T(1,128)} %broadcast_in_dim.99), calls=%async_computation.1 | async-start | bytes 655360 | tf_op jit(solution)/shard_map/all_to_all | solution.py:468
  252.6 8.5 %all-to-all-done.1 = f32[64,1,1280]{2,1,0:T(1,128)S(1)} async-done(((f32[64,1,1280]{2,1,0:T(1,128)}), f32[64,1,1280]{2,1,0:T(1,128)S(1)}, u32[]{:S(2)}, u32[]{:S(2)}) %all-to-all-start.1) | async-done | bytes 327712 | tf_op jit(solution)/shard_map/all_to_all | solution.py:468
  261.9 2.4 collective-permute-start.32
  269.6 4.2 %add_convert_fusion = bf16[256,4096]{1,0:T(8,128)(2,1)} fusion(bf16[256,4096]{1,0:T(8,128)(2,1)} %collective-permute-done.37, bf16[256,4096]{1,0:T(8,128)(2,1)S(1)} %get-tuple-element.46, f32[256]{0:T(256)} %slice.277, f32[4096]{0:T(1024)S(1)} %bitcast.128, f32[256]{0:T(256)} %slice.273, bf16[4096,16]{0,1:T(8,128)(2,1)S(1)} %copy-done, ...), kind=kOutput, calls=%fused_computation.3 | convolution fusion | flops 41943040 | bytes 6506496 | tf_op jit(solution)/shard_map/dot_general | solution.py:458
  275.2 3.7 %maximum_select_fusion = bf16[1,256,4096]{2,1,0:T(8,128)(2,1)} fusion(bf16[1,256,2048]{2,1,0:T(8,128)(2,1)} %bitcast.42, bf16[1,256,2048]{2,1,0:T(8,128)(2,1)S(1)} %copy-done.6, pred[]{:T(512)S(6)} %eq.71), kind=kLoop, calls=%fused_computation.9 | loop fusion | flops 9437184 | bytes 4194305 | tf_op jit(solution)/shard_map/jit(_where)/select_n | solution.py:56
  (270 shorter events, 80.3 us)
Async XLA Ops:
  2.6 44.6 %collective-permute-start.5 = (bf16[512,256]{1,0:T(8,128)(2,1)}, bf16[512,256]{1,0:T(8,128)(2,1)}, u32[]{:S(2)}, u32[]{:S(2)}) collective-permute-start(bf16[512,256]{1,0:T(8,128)(2,1)} %get-tuple-element.65), channel_id=1, source_target_pairs={{0,20},{1,21},{2,22},{3,23},{4,16},{5,17},{6,18},{7,19},{8,28},{9,... | collective-permute-start | bytes 786440 | tf_op jit(solution)/shard_map/ppermute | solution.py:52
  8.4 10.3 %collective-permute-start.15 = (bf16[8,2176]{1,0:T(8,128)(2,1)S(1)}, bf16[8,2176]{1,0:T(8,128)(2,1)S(1)}, u32[]{:S(2)}, u32[]{:S(2)}) collective-permute-start(bf16[8,2176]{1,0:T(8,128)(2,1)S(1)} %get-tuple-element.98), channel_id=1, source_target_pairs={{0,8},{1,9},{2,10},{3,11},{4,12},{5,13},{6,14},{7,15},{8,0},{9,1},... | collective-permute-start | bytes 104456 | tf_op jit(solution)/shard_map/ppermute | solution.py:52
  11.7 70.4 %collective-permute-start = (bf16[512,1024]{1,0:T(8,128)(2,1)}, bf16[512,1024]{1,0:T(8,128)(2,1)S(1)}, u32[]{:S(2)}, u32[]{:S(2)}) collective-permute-start(bf16[512,1024]{1,0:T(8,128)(2,1)} %constant_dynamic-slice_fusion.15), channel_id=1, source_target_pairs={{0,20},{1,21},{2,22},{3,23},{4,16},{5,17},{6,18},{7,19},{8,28},{9,... | collective-permute-start | bytes 3145736 | tf_op jit(solution)/shard_map/ppermute | solution.py:52
  18.7 10.9 %collective-permute-start.20 = (bf16[8,2176]{1,0:T(8,128)(2,1)S(1)}, bf16[8,2176]{1,0:T(8,128)(2,1)S(1)}, u32[]{:S(2)}, u32[]{:S(2)}) collective-permute-start(bf16[8,2176]{1,0:T(8,128)(2,1)S(1)} %maximum_select_fusion.10), channel_id=1, source_target_pairs={{0,16},{1,17},{2,18},{3,19},{4,20},{5,21},{6,22},{7,23},{8,24},{9,... | collective-permute-start | bytes 104456 | tf_op jit(solution)/shard_map/ppermute | solution.py:52
  27.9 6.3 %collective-permute-start.22 = (bf16[32,2048]{1,0:T(8,128)(2,1)S(1)}, bf16[32,2048]{1,0:T(8,128)(2,1)S(1)}, u32[]{:S(2)}, u32[]{:S(2)}) collective-permute-start(bf16[32,2048]{1,0:T(8,128)(2,1)S(1)} %maximum_select_fusion.6), channel_id=1, source_target_pairs={{0,1},{1,0},{2,3},{3,2},{4,5},{5,4},{6,7},{7,6},{8,9},{9,8},{10,11... | collective-permute-start | bytes 393224 | tf_op jit(solution)/shard_map/ppermute | solution.py:52
  29.7 12.6 %collective-permute-start.21 = (bf16[16,2176]{1,0:T(8,128)(2,1)S(1)}, bf16[16,2176]{1,0:T(8,128)(2,1)S(1)}, u32[]{:S(2)}, u32[]{:S(2)}) collective-permute-start(bf16[16,2176]{1,0:T(8,128)(2,1)S(1)} %maximum_select_fusion.8), channel_id=1, source_target_pairs={{0,20},{1,21},{2,22},{3,23},{4,16},{5,17},{6,18},{7,19},{8,28},{9,... | collective-permute-start | bytes 208904 | tf_op jit(solution)/shard_map/ppermute | solution.py:52
  32.2 81.8 %collective-permute-start.18 = (bf16[256,4096]{1,0:T(8,128)(2,1)S(1)}, bf16[256,4096]{1,0:T(8,128)(2,1)S(1)}, u32[]{:S(2)}, u32[]{:S(2)}) collective-permute-start(bf16[256,4096]{1,0:T(8,128)(2,1)S(1)} %bitcast.117), channel_id=1, source_target_pairs={{0,8},{1,9},{2,10},{3,11},{4,12},{5,13},{6,14},{7,15},{8,0},{9,1},... | collective-permute-start | bytes 6291464 | tf_op jit(solution)/shard_map/ppermute | solution.py:52
  34.3 7.9 %collective-permute-start.23 = (bf16[64,2048]{1,0:T(8,128)(2,1)S(1)}, bf16[64,2048]{1,0:T(8,128)(2,1)S(1)}, u32[]{:S(2)}, u32[]{:S(2)}) collective-permute-start(bf16[64,2048]{1,0:T(8,128)(2,1)S(1)} %maximum_select_fusion.2), channel_id=1, source_target_pairs={{0,3},{1,2},{2,1},{3,0},{4,7},{5,6},{6,5},{7,4},{8,11},{9,10},{10,... | collective-permute-start | bytes 786440 | tf_op jit(solution)/shard_map/ppermute | solution.py:52
  48.2 19.8 %collective-permute-start.6 = (bf16[1536,256]{1,0:T(8,128)(2,1)S(1)}, bf16[1536,256]{1,0:T(8,128)(2,1)S(1)}, u32[]{:S(2)}, u32[]{:S(2)}) collective-permute-start(bf16[1536,256]{1,0:T(8,128)(2,1)S(1)} %pad_maximum_fusion.3), channel_id=1, source_target_pairs={{0,1},{1,2},{2,3},{3,0},{4,5},{5,6},{6,7},{7,4},{8,9},{9,10},{10,1... | collective-permute-start | bytes 2359304 | tf_op jit(solution)/shard_map/ppermute | solution.py:52
  48.6 19.6 %collective-permute-start.7 = (bf16[1536,256]{1,0:T(8,128)(2,1)S(1)}, bf16[1536,256]{1,0:T(8,128)(2,1)S(1)}, u32[]{:S(2)}, u32[]{:S(2)}) collective-permute-start(bf16[1536,256]{1,0:T(8,128)(2,1)S(1)} %pad_maximum_fusion.3), channel_id=1, source_target_pairs={{0,3},{1,0},{2,1},{3,2},{4,7},{5,4},{6,5},{7,6},{8,11},{9,8},{10,9... | collective-permute-start | bytes 2359304 | tf_op jit(solution)/shard_map/ppermute | solution.py:52
  68.1 10.5 %collective-permute-start.11 = (bf16[768,256]{1,0:T(8,128)(2,1)S(1)}, bf16[768,256]{1,0:T(8,128)(2,1)S(1)}, u32[]{:S(2)}, u32[]{:S(2)}) collective-permute-start(bf16[768,256]{1,0:T(8,128)(2,1)S(1)} %pad_maximum_fusion.6), channel_id=1, source_target_pairs={{0,1},{1,2},{2,3},{3,0},{4,5},{5,6},{6,7},{7,4},{8,9},{9,10},{10,1... | collective-permute-start | bytes 1179656 | tf_op jit(solution)/shard_map/ppermute | solution.py:52
  68.3 10.3 %collective-permute-start.12 = (bf16[768,256]{1,0:T(8,128)(2,1)S(1)}, bf16[768,256]{1,0:T(8,128)(2,1)S(1)}, u32[]{:S(2)}, u32[]{:S(2)}) collective-permute-start(bf16[768,256]{1,0:T(8,128)(2,1)S(1)} %pad_maximum_fusion.7), channel_id=1, source_target_pairs={{0,3},{1,0},{2,1},{3,2},{4,7},{5,4},{6,5},{7,6},{8,11},{9,8},{10,9... | collective-permute-start | bytes 1179656 | tf_op jit(solution)/shard_map/ppermute | solution.py:52
  72.2 44.7 %collective-permute-start.10 = (bf16[2560,256]{1,0:T(8,128)(2,1)S(1)}, bf16[2560,256]{1,0:T(8,128)(2,1)S(1)}, u32[]{:S(2)}, u32[]{:S(2)}) collective-permute-start(bf16[2560,256]{1,0:T(8,128)(2,1)S(1)} %pad_maximum_fusion.1.refs_1_), channel_id=1, source_target_pairs={{0,96},{1,97},{2,98},{3,99},{4,100},{5,101},{6,102},{7,103},{8,104... | collective-permute-start | bytes 3932168 | tf_op jit(solution)/shard_map/ppermute | solution.py:52
  79.6 32.3 %collective-permute-start.13 = (bf16[1024,256]{1,0:T(8,128)(2,1)}, bf16[1024,256]{1,0:T(8,128)(2,1)S(1)}, u32[]{:S(2)}, u32[]{:S(2)}) collective-permute-start(bf16[1024,256]{1,0:T(8,128)(2,1)} %pad_maximum_fusion.5.refs_2_), channel_id=1, source_target_pairs={{0,96},{1,97},{2,98},{3,99},{4,100},{5,101},{6,102},{7,103},{8,104... | collective-permute-start | bytes 1572872 | tf_op jit(solution)/shard_map/ppermute | solution.py:52
  81.9 37.4 %collective-permute-start.8 = (bf16[2560,256]{1,0:T(8,128)(2,1)S(1)}, bf16[2560,256]{1,0:T(8,128)(2,1)S(1)}, u32[]{:S(2)}, u32[]{:S(2)}) collective-permute-start(bf16[2560,256]{1,0:T(8,128)(2,1)S(1)} %pad_maximum_fusion.1.refs_1_), channel_id=1, source_target_pairs={{0,32},{1,33},{2,34},{3,35},{4,36},{5,37},{6,38},{7,39},{8,40},{9,... | collective-permute-start | bytes 3932168 | tf_op jit(solution)/shard_map/ppermute | solution.py:52
  83.1 39.1 %collective-permute-start.1 = (bf16[1024,768]{1,0:T(8,128)(2,1)S(1)}, bf16[1024,768]{1,0:T(8,128)(2,1)S(1)}, u32[]{:S(2)}, u32[]{:S(2)}) collective-permute-start(bf16[1024,768]{1,0:T(8,128)(2,1)S(1)} %pad_maximum_fusion), channel_id=1, source_target_pairs={{0,1},{1,2},{2,3},{3,0},{4,5},{5,6},{6,7},{7,4},{8,9},{9,10},{10,1... | collective-permute-start | bytes 4718600 | tf_op jit(solution)/shard_map/ppermute | solution.py:52
  112.0 33.1 %collective-permute-start.2 = (bf16[1024,768]{1,0:T(8,128)(2,1)S(1)}, bf16[1024,768]{1,0:T(8,128)(2,1)S(1)}, u32[]{:S(2)}, u32[]{:S(2)}) collective-permute-start(bf16[1024,768]{1,0:T(8,128)(2,1)S(1)} %pad_maximum_fusion), channel_id=1, source_target_pairs={{0,3},{1,0},{2,1},{3,2},{4,7},{5,4},{6,5},{7,6},{8,11},{9,8},{10,9... | collective-permute-start | bytes 4718600 | tf_op jit(solution)/shard_map/ppermute | solution.py:52
  114.0 33.9 %collective-permute-start.19 = (bf16[256,2048]{1,0:T(8,128)(2,1)}, bf16[256,2048]{1,0:T(8,128)(2,1)}, u32[]{:S(2)}, u32[]{:S(2)}) collective-permute-start(bf16[256,2048]{1,0:T(8,128)(2,1)} %constant_dynamic-slice_fusion.13), channel_id=1, source_target_pairs={{0,8},{1,9},{2,10},{3,11},{4,12},{5,13},{6,14},{7,15},{8,0},{9,1},... | collective-permute-start | bytes 3145736 | tf_op jit(solution)/shard_map/ppermute | solution.py:52
  116.9 33.5 %collective-permute-start.30 = (bf16[1536,256]{1,0:T(8,128)(2,1)}, bf16[1536,256]{1,0:T(8,128)(2,1)}, u32[]{:S(2)}, u32[]{:S(2)}) collective-permute-start(bf16[1536,256]{1,0:T(8,128)(2,1)} %pad_maximum_fusion.4), channel_id=1, source_target_pairs={{0,20},{1,21},{2,22},{3,23},{4,16},{5,17},{6,18},{7,19},{8,28},{9,... | collective-permute-start | bytes 2359304 | tf_op jit(solution)/shard_map/ppermute | solution.py:52
  119.3 31.1 %collective-permute-start.29 = (bf16[1024,256]{1,0:T(8,128)(2,1)}, bf16[1024,256]{1,0:T(8,128)(2,1)S(1)}, u32[]{:S(2)}, u32[]{:S(2)}) collective-permute-start(bf16[1024,256]{1,0:T(8,128)(2,1)} %pad_maximum_fusion.5.refs_2_), channel_id=1, source_target_pairs={{0,32},{1,33},{2,34},{3,35},{4,36},{5,37},{6,38},{7,39},{8,40},{9,... | collective-permute-start | bytes 1572872 | tf_op jit(solution)/shard_map/ppermute | solution.py:52
  122.2 54.0 %collective-permute-start.14 = (bf16[1792,256]{1,0:T(8,128)(2,1)}, bf16[1792,256]{1,0:T(8,128)(2,1)}, u32[]{:S(2)}, u32[]{:S(2)}) collective-permute-start(bf16[1792,256]{1,0:T(8,128)(2,1)} %pad_maximum_fusion.2), channel_id=1, source_target_pairs={{0,96},{1,97},{2,98},{3,99},{4,100},{5,101},{6,102},{7,103},{8,104... | collective-permute-start | bytes 2752520 | tf_op jit(solution)/shard_map/ppermute | solution.py:52
  145.0 31.1 %collective-permute-start.9 = (bf16[1792,256]{1,0:T(8,128)(2,1)}, bf16[1792,256]{1,0:T(8,128)(2,1)}, u32[]{:S(2)}, u32[]{:S(2)}) collective-permute-start(bf16[1792,256]{1,0:T(8,128)(2,1)} %slice.291), channel_id=1, source_target_pairs={{0,32},{1,33},{2,34},{3,35},{4,36},{5,37},{6,38},{7,39},{8,40},{9,... | collective-permute-start | bytes 2752520 | tf_op jit(solution)/shard_map/ppermute | solution.py:52
  147.9 55.1 %collective-permute-start.33 = (f32[64,2048]{1,0:T(8,128)}, f32[64,2048]{1,0:T(8,128)S(1)}, u32[]{:S(2)}, u32[]{:S(2)}) collective-permute-start(f32[64,2048]{1,0:T(8,128)} %constant_dynamic-slice_fusion.8), channel_id=1, source_target_pairs={{0,3},{1,2},{2,1},{3,0},{4,7},{5,6},{6,5},{7,4},{8,11},{9,10},{10,... | collective-permute-start | bytes 1572872 | tf_op jit(solution)/shard_map/ppermute | solution.py:52
  150.4 25.7 %collective-permute-start.3 = (bf16[512,768]{1,0:T(8,128)(2,1)S(1)}, bf16[512,768]{1,0:T(8,128)(2,1)S(1)}, u32[]{:S(2)}, u32[]{:S(2)}) collective-permute-start(bf16[512,768]{1,0:T(8,128)(2,1)S(1)} %slice.287), channel_id=1, source_target_pairs={{0,1},{1,2},{2,3},{3,0},{4,5},{5,6},{6,7},{7,4},{8,9},{9,10},{10,1... | collective-permute-start | bytes 2359304 | tf_op jit(solution)/shard_map/ppermute | solution.py:52
  150.4 25.7 %collective-permute-start.4 = (bf16[512,768]{1,0:T(8,128)(2,1)S(1)}, bf16[512,768]{1,0:T(8,128)(2,1)S(1)}, u32[]{:S(2)}, u32[]{:S(2)}) collective-permute-start(bf16[512,768]{1,0:T(8,128)(2,1)S(1)} %slice.288), channel_id=1, source_target_pairs={{0,3},{1,0},{2,1},{3,2},{4,7},{5,4},{6,5},{7,6},{8,11},{9,8},{10,9... | collective-permute-start | bytes 2359304 | tf_op jit(solution)/shard_map/ppermute | solution.py:52
  202.9 66.7 %collective-permute-start.37 = (bf16[256,4096]{1,0:T(8,128)(2,1)}, bf16[256,4096]{1,0:T(8,128)(2,1)}, u32[]{:S(2)}, u32[]{:S(2)}) collective-permute-start(bf16[256,4096]{1,0:T(8,128)(2,1)} %get-tuple-element.47), channel_id=1, source_target_pairs={{0,8},{1,9},{2,10},{3,11},{4,12},{5,13},{6,14},{7,15},{8,0},{9,1},... | collective-permute-start | bytes 6291464 | tf_op jit(solution)/shard_map/ppermute | solution.py:52
  203.8 28.4 %collective-permute-start.34 = (f32[32,2048]{1,0:T(8,128)}, f32[32,2048]{1,0:T(8,128)}, u32[]{:S(2)}, u32[]{:S(2)}) collective-permute-start(f32[32,2048]{1,0:T(8,128)} %constant_dynamic-slice_fusion.7), channel_id=1, source_target_pairs={{0,1},{1,0},{2,3},{3,2},{4,5},{5,4},{6,7},{7,6},{8,9},{9,8},{10,11... | collective-permute-start | bytes 786440 | tf_op jit(solution)/shard_map/ppermute | solution.py:52
  219.4 22.3 %all-to-all-start = ((f32[64,1,1280]{2,1,0:T(1,128)}), f32[64,1,1280]{2,1,0:T(1,128)}, u32[]{:S(2)}, u32[]{:S(2)}) async-start(f32[64,1,1280]{2,1,0:T(1,128)} %all_to_all.13), calls=%async_computation | async-start | bytes 655360 | tf_op jit(solution)/shard_map/all_to_all | solution.py:468
  231.1 44.1 %collective-permute-start.39 = (bf16[256,2048]{1,0:T(8,128)(2,1)}, bf16[256,2048]{1,0:T(8,128)(2,1)}, u32[]{:S(2)}, u32[]{:S(2)}) collective-permute-start(bf16[256,2048]{1,0:T(8,128)(2,1)} %get-tuple-element.68), channel_id=1, source_target_pairs={{0,8},{1,9},{2,10},{3,11},{4,12},{5,13},{6,14},{7,15},{8,0},{9,1},... | collective-permute-start | bytes 3145736 | tf_op jit(solution)/shard_map/ppermute | solution.py:52
  233.2 8.5 %collective-permute-start.35 = (f32[16,2048]{1,0:T(8,128)S(1)}, f32[16,2048]{1,0:T(8,128)S(1)}, u32[]{:S(2)}, u32[]{:S(2)}) collective-permute-start(f32[16,2048]{1,0:T(8,128)S(1)} %constant_dynamic-slice_fusion.6), channel_id=1, source_target_pairs={{0,96},{1,97},{2,98},{3,99},{4,100},{5,101},{6,102},{7,103},{8,104... | collective-permute-start | bytes 393224 | tf_op jit(solution)/shard_map/ppermute | solution.py:52
  243.8 17.3 %all-to-all-start.1 = ((f32[64,1,1280]{2,1,0:T(1,128)}), f32[64,1,1280]{2,1,0:T(1,128)S(1)}, u32[]{:S(2)}, u32[]{:S(2)}) async-start(f32[64,1,1280]{2,1,0:T(1,128)} %broadcast_in_dim.99), calls=%async_computation.1 | async-start | bytes 655360 | tf_op jit(solution)/shard_map/all_to_all | solution.py:468
  251.5 22.4 %collective-permute-start.36 = (f32[8,2048]{1,0:T(8,128)S(1)}, f32[8,2048]{1,0:T(8,128)}, u32[]{:S(2)}, u32[]{:S(2)}) collective-permute-start(f32[8,2048]{1,0:T(8,128)S(1)} %constant_dynamic-slice_fusion.5), channel_id=1, source_target_pairs={{0,32},{1,33},{2,34},{3,35},{4,36},{5,37},{6,38},{7,39},{8,40},{9,... | collective-permute-start | bytes 196616 | tf_op jit(solution)/shard_map/ppermute | solution.py:52
  (49 other events, 525.2 us)

commit v4 on v3

--- a/solution.py
+++ b/solution.py
@@ -69,14 +69,12 @@
     a_own, a_par, r_own, r_par, low, up, q_rows, q_f = refs[n_src : n_src + 8]
     rest = refs[n_src + 8 :]
     if first:
-        hid_out, st_out, y_q, y_out = rest[:4]
+        hid_out, st_out = rest[:2]
+        scratch = rest[2:]
+    else:
+        st_in, _, hid_out, st_out = rest[:4]
         scratch = rest[4:]
-    else:
-        y_in, st_in, vq_in, _, hid_out, st_out, y_q, y_own, y_par = rest[:9]
-        scratch = rest[9:]
-    w_s, a_s, r_s, hid, ht_s, y_s, up_s, qf_s, qb_s, qt_s, w_sem, in_sem, out_sem = scratch[:13]
-    if not first:
-        yo_s, yp_s = scratch[13:]
+    w_s, a_s, r_s, hid, up_s, qf_s, w_sem, in_sem, out_sem = scratch
     half = pl.multiple_of(scal[12], 2048)
     inputs = [
         pltpu.make_async_copy(a_own, a_s.at[pl.ds(0, 256), :], in_sem.at[0]),
@@ -109,118 +107,153 @@
             w_s.at[pl.ds(row, rows), pl.ds(block * 256, 256)],
             w_sem.at[block],
         ).start()
-    if not first:
-        y_copy = pltpu.make_async_copy(y_in, y_s, in_sem.at[10])
-        y_copy.start()
     for copy in inputs:
         copy.wait()
     st_out[...] = jnp.zeros_like(st_out) if first else st_in[...]
-    qb_s[...] = jnp.zeros_like(qb_s)
     for j in range(4):
         here = pl.ds(j * 256, 256)
         col = pl.ds(pl.multiple_of(scal[8 + j] * 256, 256), 256)
         up_s[:, here] = up[:, col]
         qf_s[:, here] = q_f[:, col]
-        qb_s[pl.ds(0, 16), here] = q_rows[:, col]
-    qt_s[...] = qb_s[...].T
 
     def forward(j, carry):
         here = pl.ds(pl.multiple_of(j * 512, 512), 512)
         for k in range(2):
             part = pl.ds(pl.multiple_of(j * 512 + k * 256, 256), 256)
             pltpu.make_async_copy(w_s.at[:, part], w_s.at[:, part], w_sem.at[2 * j + k]).wait()
-        value = (
-            r_s[:, here].astype(f32)
-            + adapter_scale * jnp.dot(low[...], up_s[:, here], preferred_element_type=f32)
-            + jnp.dot(a_s[...], w_s[:, here], preferred_element_type=f32)
-        )
-        hid[:, here] = value
+        hid[:, here] = jnp.dot(a_s[...], w_s[:, here], preferred_element_type=f32)
+
+        def finish(i, carry):
+            some = pl.ds(pl.multiple_of(i * 128, 128), 128)
+            value = (
+                hid[some, here]
+                + r_s[some, here].astype(f32)
+                + adapter_scale * jnp.dot(low[some, :], up_s[:, here], preferred_element_type=f32)
+            )
+            hid[some, here] = value
+            short = value.astype(bf16)
+            st_out[some, 0:16] += lax.dot_general(
+                short, up_s[:, here], NT, preferred_element_type=f32
+            )
+            q_row = qf_s[pl.ds(i // 2, 1), here]
+            st_out[some, 16:17] += jnp.sum(value * value, axis=1, keepdims=True)
+            st_out[some, 17:18] += jnp.sum(value * q_row, axis=1, keepdims=True)
+            return carry
+
+        lax.fori_loop(0, 4, finish, 0)
         for k in range(2):
             part = pl.ds(pl.multiple_of(j * 512 + k * 256, 256), 256)
             col = pl.ds(pl.multiple_of(scal[8 + 2 * j + k] * 256, 256), 256)
             pltpu.make_async_copy(hid.at[:, part], hid_out.at[:, col], out_sem.at[2]).start()
-        short = value.astype(bf16)
-        ht_s[here, :] = short.T
-        st_out[0:512, 0:16] += lax.dot_general(
-            short, up_s[:, here], NT, preferred_element_type=f32
+        return carry
+
+    lax.fori_loop(0, 2, forward, 0)
+    if first:
+        st_out[512:528, 0:16] = lax.dot_general(
+            q_rows[...], up[...], NT, preferred_element_type=f32
         )
-        st_out[512:528, 0:16] += lax.dot_general(
-            qb_s[0:16, here], up_s[:, here], NT, preferred_element_type=f32
-        )
-        st_out[0:512, 16:17] += jnp.sum(value * value, axis=1, keepdims=True)
-        st_out[0:256, 17:18] += jnp.sum(value[:256] * qf_s[0:1, here], axis=1, keepdims=True)
-        st_out[256:512, 17:18] += jnp.sum(value[256:] * qf_s[1:2, here], axis=1, keepdims=True)
+    pltpu.make_async_copy(hid, hid, out_sem.at[2]).wait()
+
+
+def back_kernel(copies, n_src, scal, *refs):
+    srcs = refs[:n_src]
+    grad, low_t, down, y_own, y_par, w_s, t_s, y_s, yo_s, yp_s, w_sem, out_sem = refs[n_src:]
+    half = pl.multiple_of(scal[16], 2048)
+    for wanted in range(8):
+        for src, src_row, src_col, from_half, rows, shard, dst_row, block in copies:
+            if shard != wanted:
+                continue
+            at = pl.multiple_of(scal[8 + block] * 256, 256)
+            row = pl.multiple_of(scal[shard] * 512 + dst_row, 256)
+            pltpu.make_async_copy(
+                srcs[src].at[pl.ds(src_row, rows), pl.ds(half + at if from_half else src_col, 256)],
+                w_s.at[pl.ds(row, rows), pl.ds(at, 256)],
+                w_sem.at[shard],
+            ).start()
+
+    def flip(i, carry):
+        some = pl.ds(pl.multiple_of(i * 256, 256), 256)
+        t_s[some, :] = grad[:, some].T
         return carry
 
-    lax.fori_loop(0, 2, forward, 0)
-    if not first:
-        y_copy.wait()
+    lax.fori_loop(0, 8, flip, 0)
 
     def backward(shard, carry):
         columns = pl.ds(pl.multiple_of(scal[shard] * 512, 512), 512)
-        rows = w_s[columns, :]
-        part = jnp.dot(rows, ht_s[...], preferred_element_type=f32)
-        vq = jnp.dot(rows, qt_s[...], preferred_element_type=f32).T[:16]
-        if first:
-            y_q[:, columns] = vq
-            y_s[columns, :] = part
-            pltpu.make_async_copy(y_s.at[columns, :], y_out.at[columns, :], out_sem.at[0]).start()
-        else:
-            y_q[:, columns] = vq + vq_in[:, columns]
-            turned = (part + y_s[columns, :]).astype(bf16).T
-            yo_s[:, columns] = turned[:256]
-            yp_s[:, columns] = turned[256:]
-            pltpu.make_async_copy(yo_s.at[:, columns], y_own.at[:, columns], out_sem.at[0]).start()
-            pltpu.make_async_copy(yp_s.at[:, columns], y_par.at[:, columns], out_sem.at[1]).start()
+        pltpu.make_async_copy(w_s.at[columns, :], w_s.at[columns, :], w_sem.at[shard]).wait()
+        y_s[...] = jnp.dot(w_s[columns, :], t_s[...], preferred_element_type=f32)
+
+        def turn(i, carry):
+            part = pl.ds(pl.multiple_of(i * 128, 128), 128)
+            some = pl.ds(pl.multiple_of(scal[shard] * 512 + i * 128, 128), 128)
+            full = y_s[part, :] + lax.dot_general(
+                down[:, some], low_t[...], TN, preferred_element_type=f32
+            )
+            turned = full.astype(bf16).T
+            yo_s[:, some] = turned[:256]
+            yp_s[:, some] = turned[256:]
+            return carry
+
+        lax.fori_loop(0, 4, turn, 0)
+        pltpu.make_async_copy(yo_s.at[:, columns], y_own.at[:, columns], out_sem.at[0]).start()
+        pltpu.make_async_copy(yp_s.at[:, columns], y_par.at[:, columns], out_sem.at[1]).start()
         return carry
 
     lax.fori_loop(0, 8, backward, 0)
-    if first:
-        pltpu.make_async_copy(y_s, y_out, out_sem.at[0]).wait()
-    else:
-        pltpu.make_async_copy(yo_s, y_own, out_sem.at[0]).wait()
-        pltpu.make_async_copy(yp_s, y_par, out_sem.at[1]).wait()
-    pltpu.make_async_copy(hid, hid, out_sem.at[2]).wait()
+    pltpu.make_async_copy(yo_s, y_own, out_sem.at[0]).wait()
+    pltpu.make_async_copy(yp_s, y_par, out_sem.at[1]).wait()
+
+
+def back_call(copies, srcs, scal, grad, low_t, down):
+    vm = pl.BlockSpec(memory_space=pltpu.VMEM)
+    anyspace = pl.BlockSpec(memory_space=pltpu.HBM)
+    srcs = [pltpu.with_memory_space_constraint(src, pltpu.HBM) for src in srcs]
+    return pl.pallas_call(
+        functools.partial(back_kernel, copies, len(srcs)),
+        out_shape=[jax.ShapeDtypeStruct((256, 4096), bf16)] * 2,
+        in_specs=[pl.BlockSpec(memory_space=pltpu.SMEM)] + [anyspace] * len(srcs) + [vm] * 3,
+        out_specs=[anyspace, anyspace],
+        scratch_shapes=[
+            pltpu.VMEM((4096, 2048), bf16),
+            pltpu.VMEM((2048, 512), bf16),
+            pltpu.VMEM((512, 512), f32),
+            pltpu.VMEM((256, 4096), bf16),
+            pltpu.VMEM((256, 4096), bf16),
+            pltpu.SemaphoreType.DMA((8,)),
+            pltpu.SemaphoreType.DMA((2,)),
+        ],
+        compiler_params=pltpu.CompilerParams(vmem_limit_bytes=40 * 1024 * 1024),
+        cost_estimate=pl.CostEstimate(
+            flops=2 * 512 * 4096 * 2048, transcendentals=0, bytes_accessed=24 << 20
+        ),
+        name="back",
+    )(scal, *srcs, grad, low_t, down)
 
 
 def block_call(copies, srcs, scal, a_own, a_par, r_own, r_par, low, up, q_rows, q_f, carry):
     vm = pl.BlockSpec(memory_space=pltpu.VMEM)
     anyspace = pl.BlockSpec(memory_space=pltpu.HBM)
     first = carry is None
-    shapes = [
-        jax.ShapeDtypeStruct((512, 2048), f32),
-        jax.ShapeDtypeStruct((528, 128), f32),
-        jax.ShapeDtypeStruct((16, 4096), f32),
-    ]
-    out_specs = [anyspace, vm, vm]
+    shapes = [jax.ShapeDtypeStruct((512, 2048), f32), jax.ShapeDtypeStruct((528, 128), f32)]
+    out_specs = [anyspace, vm]
     args = [scal, *srcs, a_own, a_par, r_own, r_par, low, up, q_rows, q_f]
     in_specs = [pl.BlockSpec(memory_space=pltpu.SMEM)] + [anyspace] * (len(srcs) + 4) + [vm] * 4
+    aliases = {}
+    if not first:
+        in_specs += [vm, anyspace]
+        args += [carry[1], carry[0]]
+        aliases = {len(args) - 1: 0}
     scratch = [
         pltpu.VMEM((4096, 1024), bf16),
         pltpu.VMEM((512, 4096), bf16),
         pltpu.VMEM((512, 1024), bf16),
         pltpu.VMEM((512, 1024), f32),
-        pltpu.VMEM((1024, 512), bf16),
-        pltpu.VMEM((4096, 512), f32),
         pltpu.VMEM((16, 1024), bf16),
         pltpu.VMEM((8, 1024), f32),
-        pltpu.VMEM((128, 1024), bf16),
-        pltpu.VMEM((1024, 128), bf16),
         pltpu.SemaphoreType.DMA((4,)),
-        pltpu.SemaphoreType.DMA((11,)),
+        pltpu.SemaphoreType.DMA((10,)),
         pltpu.SemaphoreType.DMA((3,)),
     ]
-    if first:
-        shapes += [jax.ShapeDtypeStruct((4096, 512), f32)]
-        out_specs += [anyspace]
-        aliases = {}
-    else:
-        shapes += [jax.ShapeDtypeStruct((256, 4096), bf16)] * 2
-        out_specs += [anyspace, anyspace]
-        scratch += [pltpu.VMEM((256, 4096), bf16)] * 2
-        in_specs += [anyspace, vm, vm, anyspace]
-        args += [carry[3], carry[1], carry[2], carry[0]]
-        aliases = {len(args) - 1: 0}
     args = [
         pltpu.with_memory_space_constraint(arg, pltpu.HBM) if spec is anyspace else arg
         for arg, spec in zip(args, in_specs)
@@ -232,9 +265,9 @@
         out_specs=out_specs,
         scratch_shapes=scratch,
         input_output_aliases=aliases,
-        compiler_params=pltpu.CompilerParams(vmem_limit_bytes=44 * 1024 * 1024),
+        compiler_params=pltpu.CompilerParams(vmem_limit_bytes=28 * 1024 * 1024),
         cost_estimate=pl.CostEstimate(
-            flops=4 * 512 * 4096 * 1024, transcendentals=0, bytes_accessed=24 << 20
+            flops=2 * 512 * 4096 * 1024, transcendentals=0, bytes_accessed=16 << 20
         ),
         name="block_first" if first else "block_last",
     )(*args)
@@ -419,18 +452,14 @@
     late.land(y_far1, [(2, 256, 256), five[4]] + two, 0)
     shared = (a_own, a_par, res_own, r_par, low, up_half, q_rows, q_f)
     carry = block_call(early.copies, early.srcs, numbers(ring[:3] + [4]), *shared, None)
-    hidden, stats_own, y_q, y_own, y_par = block_call(
+    hidden, stats_own = block_call(
         late.copies, late.srcs, numbers(ring[3:] + [5, 6, 7]), *shared, carry
     )
 
-    v_own, v_par = y_q[0:1] + y_q[2:3], y_q[1:2] + y_q[3:4]
-    packed = jnp.concatenate([stats_own, v_par.reshape(32, 128)], axis=0)
-    got = send(packed, "core")
-    y_got = send(y_par, "core")
+    got = send(stats_own, "core")
     tok = stats_own[:512] + jnp.concatenate([got[256:512], got[:256]], axis=0)
     qu_own = stats_own[512, :16] + stats_own[514, :16] + got[513, :16] + got[515, :16]
     qu_par = stats_own[513, :16] + stats_own[515, :16] + got[512, :16] + got[514, :16]
-    v = v_own + got[528:].reshape(1, 4096)
     position = jnp.arange(256, dtype=jnp.int32).astype(f32)
     len_own = lengths[0].astype(f32)
     w_tok = jnp.concatenate(
@@ -452,11 +481,25 @@
     res_grad = (lead[:, None] * q_tok - back[:, None] * hidden).astype(bf16)
     r_got = send(res_grad[256:], "core")
     residual_grad = ordered(c, res_grad[:256], r_got, axis=1)
-    attn_grad = (
-        lead[:256, None] * v
-        - back[:256, None] * (y_own.astype(f32) + y_got.astype(f32))
-        + lax.dot_general(low_grad[:256], adapter_down_weight, NT, preferred_element_type=f32)
-    ).astype(bf16)
+    srcs, copies = [], []
+    for plan, shift in ((early, 0), (late, 4)):
+        for index, at, column, from_half, rows, shard, dst_row, block in plan.copies:
+            value = plan.srcs[index]
+            if not any(value is known for known in srcs):
+                srcs.append(value)
+            index = [value is known for known in srcs].index(True)
+            copies.append((index, at, column, from_half, rows, shard, dst_row, block + shift))
+    low_t = jnp.concatenate([low_grad[:256], jnp.zeros((256, 16), bf16)], axis=0).T
+    y_own, y_par = back_call(
+        copies,
+        srcs,
+        numbers(ring[:3] + [4] + ring[3:] + [5, 6, 7]),
+        res_grad,
+        low_t,
+        adapter_down_weight.T,
+    )
+    y_got = send(y_par, "core")
+    attn_grad = (y_own.astype(f32) + y_got.astype(f32)).astype(bf16)
 
     up_part = adapter_scale * lax.dot_general(low, res_grad, TN, preferred_element_type=f32)
     down_part = lax.dot_general(

time: 283 us -> 282 us (level)
  waiting for transfers between devices: 83.2 us -> 92.2 us
  Pallas kernels: 41.9 us -> 49.8 us
  matrix products: 11.1 us -> 3.76 us
  local copies, waits for them, and re-layouts: 32.1 us -> 28 us
  starting transfers between devices: 80.8 us -> 77.5 us
    pallas_call x0 -> x1, Pallas kernels: none -> 22.5 us  [back_call(): pl.pallas_call(functools.partial(back_kernel, copies, len(srcs)), out_sha...]
    pallas_call x2, Pallas kernels: 41.9 us -> 27.3 us  [block_call(): pl.pallas_call(functools.partial(block_kernel, copies, len(srcs), first),...]
    ppermute x40, waiting for transfers between devices: 74.7 us -> 85.2 us  [send(): return lax.ppermute(value, AX, MOVES[move])]
    dot_general x1 -> x0, matrix products: 4.2 us -> none  [compute(): lax.dot_general(low_grad[:256], adapter_down_weight, NT, preferred_elemen...]
    unnamed x74 -> x68, local copies, waits for them, and re-layouts: 7.24 us -> 7.28 us
  transfers between devices with their start and end apart: 42 -> 42, of which waited for: 14 -> 13; matrix products, arithmetic and copies ran while one was open for 20% -> 15% of each run, Pallas kernels for 15% -> 18%
where the time goes in v4:
time: 282 us
  waiting for transfers between devices  92.2 us (33%)
  starting transfers between devices  77.5 us (27%)
  Pallas kernels  49.8 us (18%)
  local copies, waits for them, and re-layouts  28 us (10%)
  other arithmetic  21.4 us (8%)
  between operations  8.86 us (3%)
  matrix products  3.76 us (1%)
    ppermute x40, waiting for transfers between devices, send(): return lax.ppermute(value, AX, MOVES[move])  85.2 us
    ppermute x40, starting transfers between devices, send(): return lax.ppermute(value, AX, MOVES[move])  59.4 us
    pallas_call x2, Pallas kernels, block_call(): pl.pallas_call(functools.partial(block_kernel, copies, len(srcs), first),...  27.3 us
    pallas_call x1, Pallas kernels, back_call(): pl.pallas_call(functools.partial(back_kernel, copies, len(srcs)), out_sha...  22.5 us
    all_to_all x2, starting transfers between devices, compute(): lax.all_to_all(value, AX, 0, 0, axis_index_groups=sides, tiled=True)  18.1 us
    unnamed x68, local copies, waits for them, and re-layouts  7.28 us
    all_to_all x2, waiting for transfers between devices, compute(): lax.all_to_all(value, AX, 0, 0, axis_index_groups=sides, tiled=True)  6.91 us
    dynamic_slice x13, local copies, waits for them, and re-layouts, pick(): return lax.dynamic_slice_in_dim(value, start, size, axis=axis)  5.9 us
  transfers between devices with their start and end apart: 42, of which 13 were waited for; matrix products, arithmetic and copies ran while one was open for 15% of the time, Pallas kernels for 18%

profile of v4, /device:TPU:1, one launch (start us, length us, event | category | flops | bytes accessed | tf_op | source)
XLA Modules:
  0.0 281.5 jit_solution(15577526194274668313)
XLA Ops:
  1.8 3.4 %collective-permute-start.5 = (bf16[512,256]{1,0:T(8,128)(2,1)S(1)}, bf16[512,256]{1,0:T(8,128)(2,1)S(1)}, u32[]{:S(2)}, u32[]{:S(2)}) collective-permute-start(bf16[512,256]{1,0:T(8,128)(2,1)S(1)} %get-tuple-element.57), channel_id=1, source_target_pairs={{0,20},{1,21},{2,22},{3,23},{4,16},{5,17},{6,18},{7,19},{8,28},{9,... | collective-permute-start | bytes 786440 | tf_op jit(solution)/shard_map/ppermute | solution.py:52
  8.7 2.3 constant_dynamic-slice_fusion.15
  11.1 2.2 constant_dynamic-slice_fusion.1
  18.2 2.9 %collective-permute-start.17 = (bf16[16,2048]{1,0:T(8,128)(2,1)S(1)}, bf16[16,2048]{1,0:T(8,128)(2,1)S(1)}, u32[]{:S(2)}, u32[]{:S(2)}) collective-permute-start(bf16[16,2048]{1,0:T(8,128)(2,1)S(1)} %maximum_select_fusion.9), channel_id=1, source_target_pairs={{0,96},{1,97},{2,98},{3,99},{4,100},{5,101},{6,102},{7,103},{8,104... | collective-permute-start | bytes 196616 | tf_op jit(solution)/shard_map/ppermute | solution.py:52
  21.1 2.0 collective-permute-done.17
  24.9 2.4 collective-permute-start.21
  27.4 2.3 collective-permute-start.18
  29.7 2.3 collective-permute-start.23
  32.8 5.0 %collective-permute-done.23 = bf16[64,2048]{1,0:T(8,128)(2,1)S(1)} collective-permute-done((bf16[64,2048]{1,0:T(8,128)(2,1)S(1)}, bf16[64,2048]{1,0:T(8,128)(2,1)S(1)}, u32[]{:S(2)}, u32[]{:S(2)}) %collective-permute-start.23) | collective-permute-done | bytes 262176 | tf_op jit(solution)/shard_map/ppermute | solution.py:52
  42.8 2.2 collective-permute-start.7
  46.9 2.2 collective-permute-done.26
  52.9 2.3 collective-permute-done.27
  55.2 7.2 %collective-permute-done.6.refs_8_ = bf16[1536,256]{1,0:T(8,128)(2,1)S(1)} collective-permute-done((bf16[1536,256]{1,0:T(8,128)(2,1)S(1)}, bf16[1536,256]{1,0:T(8,128)(2,1)S(1)}, u32[]{:S(2)}, u32[]{:S(2)}) %collective-permute-start.6) | collective-permute-done | bytes 786464 | tf_op jit(solution)/shard_map/ppermute | solution.py:52
  62.7 2.7 collective-permute-start.12
  66.9 6.5 %collective-permute-done.11.refs_10_ = bf16[768,256]{1,0:T(8,128)(2,1)S(1)} collective-permute-done((bf16[768,256]{1,0:T(8,128)(2,1)S(1)}, bf16[768,256]{1,0:T(8,128)(2,1)S(1)}, u32[]{:S(2)}, u32[]{:S(2)}) %collective-permute-start.11) | collective-permute-done | bytes 393248 | tf_op jit(solution)/shard_map/ppermute | solution.py:52
  73.5 2.9 %collective-permute-start.10 = (bf16[2560,256]{1,0:T(8,128)(2,1)S(1)}, bf16[2560,256]{1,0:T(8,128)(2,1)S(1)}, u32[]{:S(2)}, u32[]{:S(2)}) collective-permute-start(bf16[2560,256]{1,0:T(8,128)(2,1)S(1)} %pad_maximum_fusion.1.refs_1_), channel_id=1, source_target_pairs={{0,96},{1,97},{2,98},{3,99},{4,100},{5,101},{6,102},{7,103},{8,104... | collective-permute-start | bytes 3932168 | tf_op jit(solution)/shard_map/ppermute | solution.py:52
  79.6 34.4 %collective-permute-done.13.refs_6_ = bf16[1024,256]{1,0:T(8,128)(2,1)S(1)} collective-permute-done((bf16[1024,256]{1,0:T(8,128)(2,1)S(1)}, bf16[1024,256]{1,0:T(8,128)(2,1)S(1)}, u32[]{:S(2)}, u32[]{:S(2)}) %collective-permute-start.13) | collective-permute-done | bytes 524320 | tf_op jit(solution)/shard_map/ppermute | solution.py:52
  114.1 2.9 %collective-permute-start.19 = (bf16[256,2048]{1,0:T(8,128)(2,1)S(1)}, bf16[256,2048]{1,0:T(8,128)(2,1)S(1)}, u32[]{:S(2)}, u32[]{:S(2)}) collective-permute-start(bf16[256,2048]{1,0:T(8,128)(2,1)S(1)} %constant_dynamic-slice_fusion.13), channel_id=1, source_target_pairs={{0,8},{1,9},{2,10},{3,11},{4,12},{5,13},{6,14},{7,15},{8,0},{9,1},... | collective-permute-start | bytes 3145736 | tf_op jit(solution)/shard_map/ppermute | solution.py:52
  121.2 2.9 %collective-permute-start.14 = (bf16[1792,256]{1,0:T(8,128)(2,1)}, bf16[1792,256]{1,0:T(8,128)(2,1)}, u32[]{:S(2)}, u32[]{:S(2)}) collective-permute-start(bf16[1792,256]{1,0:T(8,128)(2,1)} %pad_maximum_fusion.2), channel_id=1, source_target_pairs={{0,96},{1,97},{2,98},{3,99},{4,100},{5,101},{6,102},{7,103},{8,104... | collective-permute-start | bytes 2752520 | tf_op jit(solution)/shard_map/ppermute | solution.py:52
  124.1 23.2 %collective-permute-done.2.refs_3_.refs_14_ = bf16[1024,768]{1,0:T(8,128)(2,1)S(1)} collective-permute-done((bf16[1024,768]{1,0:T(8,128)(2,1)S(1)}, bf16[1024,768]{1,0:T(8,128)(2,1)S(1)}, u32[]{:S(2)}, u32[]{:S(2)}) %collective-permute-start.2) | collective-permute-done | bytes 1572896 | tf_op jit(solution)/shard_map/ppermute | solution.py:52
  150.1 2.7 collective-permute-start.4
  154.3 13.3 %block_first.1 = (f32[512,2048]{1,0:T(8,128)S(1)}, f32[528,128]{1,0:T(8,128)S(1)}) custom-call(s32[13]{0:T(128)S(1)} %stack.117.scal, bf16[512,4096]{1,0:T(8,128)(2,1)} %refs_0_.5, bf16[2560,256]{1,0:T(8,128)(2,1)} %copy-done.12, bf16[1024,256]{1,0:T(8,128)(2,1)} %copy-done.23, bf16[2560,256]{1,0:T(8,128)(2,1)} %copy-done.17, bf16[1024,256]{1,0:T(8,128)(2,1)} %copy-done.30, ...), custom_call_target="tpu_custom_call" | custom-call | flops 4294967296 | bytes 16777216 | tf_op jit(solution)/shard_map/block_first/pallas_call | solution.py:261
  170.5 14.0 %block_last.1 = (f32[512,2048]{1,0:T(8,128)}, f32[528,128]{1,0:T(8,128)S(1)}) custom-call(s32[13]{0:T(128)S(1)} %stack.107.scal, bf16[512,4096]{1,0:T(8,128)(2,1)} %refs_0_.5, bf16[512,1024]{1,0:T(8,128)(2,1)} %collective-permute-done.refs_7_.refs_1_, bf16[1024,768]{1,0:T(8,128)(2,1)} %copy-done.18, ...), custom_call_target="tpu_custom_call", output_to_operand_aliasing={{0}: (18, {})} | custom-call | flops 4294967296 | bytes 16777216 | tf_op jit(solution)/shard_map/block_last/pallas_call | solution.py:261
  184.7 6.2 %collective-permute-start.31 = (f32[528,128]{0,1:T(8,128)S(1)}, f32[528,128]{0,1:T(8,128)S(1)}, u32[]{:S(2)}, u32[]{:S(2)}) collective-permute-start(f32[528,128]{0,1:T(8,128)S(1)} %copy.44), channel_id=1, source_target_pairs={{0,8},{1,9},{2,10},{3,11},{4,12},{5,13},{6,14},{7,15},{8,0},{9,1},... | collective-permute-start | bytes 811016 | tf_op jit(solution)/shard_map/ppermute | solution.py:52
  199.5 10.6 %all-to-all-start = ((f32[64,1,1280]{2,1,0:T(1,128)}), f32[64,1,1280]{2,1,0:T(1,128)}, u32[]{:S(2)}, u32[]{:S(2)}) async-start(f32[64,1,1280]{2,1,0:T(1,128)} %all_to_all.13), calls=%async_computation | async-start | bytes 655360 | tf_op jit(solution)/shard_map/all_to_all | solution.py:511
  213.1 2.9 %collective-permute-start.35 = (f32[16,2048]{1,0:T(8,128)S(1)}, f32[16,2048]{1,0:T(8,128)}, u32[]{:S(2)}, u32[]{:S(2)}) collective-permute-start(f32[16,2048]{1,0:T(8,128)S(1)} %constant_dynamic-slice_fusion.6), channel_id=1, source_target_pairs={{0,96},{1,97},{2,98},{3,99},{4,100},{5,101},{6,102},{7,103},{8,104... | collective-permute-start | bytes 393224 | tf_op jit(solution)/shard_map/ppermute | solution.py:52
  216.0 22.5 %back.1 = (bf16[256,4096]{1,0:T(8,128)(2,1)S(1)}, bf16[256,4096]{1,0:T(8,128)(2,1)}) custom-call(s32[17]{0:T(128)S(1)} %stack.119.scal, bf16[512,4096]{1,0:T(8,128)(2,1)} %refs_0_.5, bf16[2560,256]{1,0:T(8,128)(2,1)} %copy-done.12, bf16[1024,256]{1,0:T(8,128)(2,1)} %copy-done.23, bf16[2560,256]{1,0:T(8,128)(2,1)} %copy-done.17, ...), custom_call_target="tpu_custom_call" | custom-call | flops 8589934592 | bytes 25165824 | tf_op jit(solution)/shard_map/back/pallas_call | solution.py:211
  242.3 7.5 %all-to-all-start.1 = ((f32[64,1,1280]{2,1,0:T(1,128)}), f32[64,1,1280]{2,1,0:T(1,128)S(1)}, u32[]{:S(2)}, u32[]{:S(2)}) async-start(f32[64,1,1280]{2,1,0:T(1,128)} %broadcast_in_dim.98), calls=%async_computation.1 | async-start | bytes 655360 | tf_op jit(solution)/shard_map/all_to_all | solution.py:511
  252.6 6.9 %all-to-all-done.1 = f32[64,1,1280]{2,1,0:T(1,128)S(1)} async-done(((f32[64,1,1280]{2,1,0:T(1,128)}), f32[64,1,1280]{2,1,0:T(1,128)S(1)}, u32[]{:S(2)}, u32[]{:S(2)}) %all-to-all-start.1) | async-done | bytes 327712 | tf_op jit(solution)/shard_map/all_to_all | solution.py:511
  262.2 2.3 collective-permute-start.32
  269.8 3.7 %add_convert_fusion = bf16[256,4096]{1,0:T(8,128)(2,1)} fusion(bf16[256,4096]{1,0:T(8,128)(2,1)} %collective-permute-done.37, bf16[256,4096]{1,0:T(8,128)(2,1)S(1)} %copy-done.5), kind=kLoop, calls=%fused_computation.3 | loop fusion | flops 4194304 | bytes 6291456 | tf_op jit(solution)/shard_map/convert_element_type | solution.py:502
  274.9 3.7 %maximum_select_fusion = bf16[1,256,4096]{2,1,0:T(8,128)(2,1)} fusion(bf16[1,256,2048]{2,1,0:T(8,128)(2,1)} %bitcast.40, bf16[1,256,2048]{2,1,0:T(8,128)(2,1)S(1)} %get-tuple-element.59, pred[]{:T(512)S(6)} %eq.71), kind=kLoop, calls=%fused_computation.9 | loop fusion | flops 9437184 | bytes 4194305 | tf_op jit(solution)/shard_map/jit(_where)/select_n | solution.py:56
  (253 shorter events, 61.9 us)
Async XLA Ops:
  1.8 39.9 %collective-permute-start.5 = (bf16[512,256]{1,0:T(8,128)(2,1)S(1)}, bf16[512,256]{1,0:T(8,128)(2,1)S(1)}, u32[]{:S(2)}, u32[]{:S(2)}) collective-permute-start(bf16[512,256]{1,0:T(8,128)(2,1)S(1)} %get-tuple-element.57), channel_id=1, source_target_pairs={{0,20},{1,21},{2,22},{3,23},{4,16},{5,17},{6,18},{7,19},{8,28},{9,... | collective-permute-start | bytes 786440 | tf_op jit(solution)/shard_map/ppermute | solution.py:52
  7.7 7.2 %collective-permute-start.15 = (bf16[8,2176]{1,0:T(8,128)(2,1)S(1)}, bf16[8,2176]{1,0:T(8,128)(2,1)S(1)}, u32[]{:S(2)}, u32[]{:S(2)}) collective-permute-start(bf16[8,2176]{1,0:T(8,128)(2,1)S(1)} %get-tuple-element.88), channel_id=1, source_target_pairs={{0,8},{1,9},{2,10},{3,11},{4,12},{5,13},{6,14},{7,15},{8,0},{9,1},... | collective-permute-start | bytes 104456 | tf_op jit(solution)/shard_map/ppermute | solution.py:52
  11.0 67.2 %collective-permute-start = (bf16[512,1024]{1,0:T(8,128)(2,1)}, bf16[512,1024]{1,0:T(8,128)(2,1)}, u32[]{:S(2)}, u32[]{:S(2)}) collective-permute-start(bf16[512,1024]{1,0:T(8,128)(2,1)} %constant_dynamic-slice_fusion.15), channel_id=1, source_target_pairs={{0,20},{1,21},{2,22},{3,23},{4,16},{5,17},{6,18},{7,19},{8,28},{9,... | collective-permute-start | bytes 3145736 | tf_op jit(solution)/shard_map/ppermute | solution.py:52
  16.5 8.4 %collective-permute-start.20 = (bf16[8,2176]{1,0:T(8,128)(2,1)S(1)}, bf16[8,2176]{1,0:T(8,128)(2,1)S(1)}, u32[]{:S(2)}, u32[]{:S(2)}) collective-permute-start(bf16[8,2176]{1,0:T(8,128)(2,1)S(1)} %maximum_select_fusion.10), channel_id=1, source_target_pairs={{0,16},{1,17},{2,18},{3,19},{4,20},{5,21},{6,22},{7,23},{8,24},{9,... | collective-permute-start | bytes 104456 | tf_op jit(solution)/shard_map/ppermute | solution.py:52
  24.9 13.6 %collective-permute-start.21 = (bf16[16,2176]{1,0:T(8,128)(2,1)S(1)}, bf16[16,2176]{1,0:T(8,128)(2,1)S(1)}, u32[]{:S(2)}, u32[]{:S(2)}) collective-permute-start(bf16[16,2176]{1,0:T(8,128)(2,1)S(1)} %maximum_select_fusion.8), channel_id=1, source_target_pairs={{0,20},{1,21},{2,22},{3,23},{4,16},{5,17},{6,18},{7,19},{8,28},{9,... | collective-permute-start | bytes 208904 | tf_op jit(solution)/shard_map/ppermute | solution.py:52
  27.4 122.7 %collective-permute-start.18 = (bf16[256,4096]{1,0:T(8,128)(2,1)S(1)}, bf16[256,4096]{1,0:T(8,128)(2,1)S(1)}, u32[]{:S(2)}, u32[]{:S(2)}) collective-permute-start(bf16[256,4096]{1,0:T(8,128)(2,1)S(1)} %bitcast.114), channel_id=1, source_target_pairs={{0,8},{1,9},{2,10},{3,11},{4,12},{5,13},{6,14},{7,15},{8,0},{9,1},... | collective-permute-start | bytes 6291464 | tf_op jit(solution)/shard_map/ppermute | solution.py:52
  29.7 8.1 %collective-permute-start.23 = (bf16[64,2048]{1,0:T(8,128)(2,1)S(1)}, bf16[64,2048]{1,0:T(8,128)(2,1)S(1)}, u32[]{:S(2)}, u32[]{:S(2)}) collective-permute-start(bf16[64,2048]{1,0:T(8,128)(2,1)S(1)} %maximum_select_fusion.2), channel_id=1, source_target_pairs={{0,3},{1,2},{2,1},{3,0},{4,7},{5,6},{6,5},{7,4},{8,11},{9,10},{10,... | collective-permute-start | bytes 786440 | tf_op jit(solution)/shard_map/ppermute | solution.py:52
  41.7 20.7 %collective-permute-start.6 = (bf16[1536,256]{1,0:T(8,128)(2,1)S(1)}, bf16[1536,256]{1,0:T(8,128)(2,1)S(1)}, u32[]{:S(2)}, u32[]{:S(2)}) collective-permute-start(bf16[1536,256]{1,0:T(8,128)(2,1)S(1)} %pad_maximum_fusion.3), channel_id=1, source_target_pairs={{0,1},{1,2},{2,3},{3,0},{4,5},{5,6},{6,7},{7,4},{8,9},{9,10},{10,1... | collective-permute-start | bytes 2359304 | tf_op jit(solution)/shard_map/ppermute | solution.py:52
  42.8 19.8 %collective-permute-start.7 = (bf16[1536,256]{1,0:T(8,128)(2,1)S(1)}, bf16[1536,256]{1,0:T(8,128)(2,1)S(1)}, u32[]{:S(2)}, u32[]{:S(2)}) collective-permute-start(bf16[1536,256]{1,0:T(8,128)(2,1)S(1)} %pad_maximum_fusion.3), channel_id=1, source_target_pairs={{0,3},{1,0},{2,1},{3,2},{4,7},{5,4},{6,5},{7,6},{8,11},{9,8},{10,9... | collective-permute-start | bytes 2359304 | tf_op jit(solution)/shard_map/ppermute | solution.py:52
  62.5 10.9 %collective-permute-start.11 = (bf16[768,256]{1,0:T(8,128)(2,1)S(1)}, bf16[768,256]{1,0:T(8,128)(2,1)S(1)}, u32[]{:S(2)}, u32[]{:S(2)}) collective-permute-start(bf16[768,256]{1,0:T(8,128)(2,1)S(1)} %pad_maximum_fusion.6), channel_id=1, source_target_pairs={{0,1},{1,2},{2,3},{3,0},{4,5},{5,6},{6,7},{7,4},{8,9},{9,10},{10,1... | collective-permute-start | bytes 1179656 | tf_op jit(solution)/shard_map/ppermute | solution.py:52
  62.7 13.7 %collective-permute-start.12 = (bf16[768,256]{1,0:T(8,128)(2,1)S(1)}, bf16[768,256]{1,0:T(8,128)(2,1)S(1)}, u32[]{:S(2)}, u32[]{:S(2)}) collective-permute-start(bf16[768,256]{1,0:T(8,128)(2,1)S(1)} %pad_maximum_fusion.7), channel_id=1, source_target_pairs={{0,3},{1,0},{2,1},{3,2},{4,7},{5,4},{6,5},{7,6},{8,11},{9,8},{10,9... | collective-permute-start | bytes 1179656 | tf_op jit(solution)/shard_map/ppermute | solution.py:52
  65.4 11.6 %collective-permute-start.28 = (f32[8,2048]{1,0:T(8,128)S(1)}, f32[8,2048]{1,0:T(8,128)S(1)}, u32[]{:S(2)}, u32[]{:S(2)}) collective-permute-start(f32[8,2048]{1,0:T(8,128)S(1)} %constant_dynamic-slice_fusion.10), channel_id=1, source_target_pairs={{0,16},{1,17},{2,18},{3,19},{4,20},{5,21},{6,22},{7,23},{8,24},{9,... | collective-permute-start | bytes 196616 | tf_op jit(solution)/shard_map/ppermute | solution.py:52
  73.5 40.6 %collective-permute-start.10 = (bf16[2560,256]{1,0:T(8,128)(2,1)S(1)}, bf16[2560,256]{1,0:T(8,128)(2,1)S(1)}, u32[]{:S(2)}, u32[]{:S(2)}) collective-permute-start(bf16[2560,256]{1,0:T(8,128)(2,1)S(1)} %pad_maximum_fusion.1.refs_1_), channel_id=1, source_target_pairs={{0,96},{1,97},{2,98},{3,99},{4,100},{5,101},{6,102},{7,103},{8,104... | collective-permute-start | bytes 3932168 | tf_op jit(solution)/shard_map/ppermute | solution.py:52
  76.5 37.5 %collective-permute-start.13 = (bf16[1024,256]{1,0:T(8,128)(2,1)S(1)}, bf16[1024,256]{1,0:T(8,128)(2,1)S(1)}, u32[]{:S(2)}, u32[]{:S(2)}) collective-permute-start(bf16[1024,256]{1,0:T(8,128)(2,1)S(1)} %pad_maximum_fusion.5.refs_2_), channel_id=1, source_target_pairs={{0,96},{1,97},{2,98},{3,99},{4,100},{5,101},{6,102},{7,103},{8,104... | collective-permute-start | bytes 1572872 | tf_op jit(solution)/shard_map/ppermute | solution.py:52
  77.1 41.0 %collective-permute-start.8 = (bf16[2560,256]{1,0:T(8,128)(2,1)S(1)}, bf16[2560,256]{1,0:T(8,128)(2,1)S(1)}, u32[]{:S(2)}, u32[]{:S(2)}) collective-permute-start(bf16[2560,256]{1,0:T(8,128)(2,1)S(1)} %pad_maximum_fusion.1.refs_1_), channel_id=1, source_target_pairs={{0,32},{1,33},{2,34},{3,35},{4,36},{5,37},{6,38},{7,39},{8,40},{9,... | collective-permute-start | bytes 3932168 | tf_op jit(solution)/shard_map/ppermute | solution.py:52
  79.5 41.7 %collective-permute-start.1 = (bf16[1024,768]{1,0:T(8,128)(2,1)S(1)}, bf16[1024,768]{1,0:T(8,128)(2,1)S(1)}, u32[]{:S(2)}, u32[]{:S(2)}) collective-permute-start(bf16[1024,768]{1,0:T(8,128)(2,1)S(1)} %pad_maximum_fusion), channel_id=1, source_target_pairs={{0,1},{1,2},{2,3},{3,0},{4,5},{5,6},{6,7},{7,4},{8,9},{9,10},{10,1... | collective-permute-start | bytes 4718600 | tf_op jit(solution)/shard_map/ppermute | solution.py:52
  114.0 33.3 %collective-permute-start.2 = (bf16[1024,768]{1,0:T(8,128)(2,1)S(1)}, bf16[1024,768]{1,0:T(8,128)(2,1)S(1)}, u32[]{:S(2)}, u32[]{:S(2)}) collective-permute-start(bf16[1024,768]{1,0:T(8,128)(2,1)S(1)} %pad_maximum_fusion), channel_id=1, source_target_pairs={{0,3},{1,0},{2,1},{3,2},{4,7},{5,4},{6,5},{7,6},{8,11},{9,8},{10,9... | collective-permute-start | bytes 4718600 | tf_op jit(solution)/shard_map/ppermute | solution.py:52
  118.2 31.9 %collective-permute-start.29 = (bf16[1024,256]{1,0:T(8,128)(2,1)S(1)}, bf16[1024,256]{1,0:T(8,128)(2,1)S(1)}, u32[]{:S(2)}, u32[]{:S(2)}) collective-permute-start(bf16[1024,256]{1,0:T(8,128)(2,1)S(1)} %pad_maximum_fusion.5.refs_2_), channel_id=1, source_target_pairs={{0,32},{1,33},{2,34},{3,35},{4,36},{5,37},{6,38},{7,39},{8,40},{9,... | collective-permute-start | bytes 1572872 | tf_op jit(solution)/shard_map/ppermute | solution.py:52
  121.0 32.6 %collective-permute-start.30 = (bf16[1536,256]{1,0:T(8,128)(2,1)}, bf16[1536,256]{1,0:T(8,128)(2,1)}, u32[]{:S(2)}, u32[]{:S(2)}) collective-permute-start(bf16[1536,256]{1,0:T(8,128)(2,1)} %pad_maximum_fusion.4), channel_id=1, source_target_pairs={{0,20},{1,21},{2,22},{3,23},{4,16},{5,17},{6,18},{7,19},{8,28},{9,... | collective-permute-start | bytes 2359304 | tf_op jit(solution)/shard_map/ppermute | solution.py:52
  121.2 48.4 %collective-permute-start.14 = (bf16[1792,256]{1,0:T(8,128)(2,1)}, bf16[1792,256]{1,0:T(8,128)(2,1)}, u32[]{:S(2)}, u32[]{:S(2)}) collective-permute-start(bf16[1792,256]{1,0:T(8,128)(2,1)} %pad_maximum_fusion.2), channel_id=1, source_target_pairs={{0,96},{1,97},{2,98},{3,99},{4,100},{5,101},{6,102},{7,103},{8,104... | collective-permute-start | bytes 2752520 | tf_op jit(solution)/shard_map/ppermute | solution.py:52
  147.3 22.3 %collective-permute-start.9 = (bf16[1792,256]{1,0:T(8,128)(2,1)}, bf16[1792,256]{1,0:T(8,128)(2,1)}, u32[]{:S(2)}, u32[]{:S(2)}) collective-permute-start(bf16[1792,256]{1,0:T(8,128)(2,1)} %slice.264), channel_id=1, source_target_pairs={{0,32},{1,33},{2,34},{3,35},{4,36},{5,37},{6,38},{7,39},{8,40},{9,... | collective-permute-start | bytes 2752520 | tf_op jit(solution)/shard_map/ppermute | solution.py:52
  150.1 19.5 %collective-permute-start.3 = (bf16[512,768]{1,0:T(8,128)(2,1)}, bf16[512,768]{1,0:T(8,128)(2,1)}, u32[]{:S(2)}, u32[]{:S(2)}) collective-permute-start(bf16[512,768]{1,0:T(8,128)(2,1)} %slice.260), channel_id=1, source_target_pairs={{0,1},{1,2},{2,3},{3,0},{4,5},{5,6},{6,7},{7,4},{8,9},{9,10},{10,1... | collective-permute-start | bytes 2359304 | tf_op jit(solution)/shard_map/ppermute | solution.py:52
  150.1 19.5 %collective-permute-start.4 = (bf16[512,768]{1,0:T(8,128)(2,1)}, bf16[512,768]{1,0:T(8,128)(2,1)S(1)}, u32[]{:S(2)}, u32[]{:S(2)}) collective-permute-start(bf16[512,768]{1,0:T(8,128)(2,1)} %slice.261), channel_id=1, source_target_pairs={{0,3},{1,0},{2,1},{3,2},{4,7},{5,4},{6,5},{7,6},{8,11},{9,8},{10,9... | collective-permute-start | bytes 2359304 | tf_op jit(solution)/shard_map/ppermute | solution.py:52
  153.6 37.4 %collective-permute-start.33 = (f32[64,2048]{1,0:T(8,128)}, f32[64,2048]{1,0:T(8,128)}, u32[]{:S(2)}, u32[]{:S(2)}) collective-permute-start(f32[64,2048]{1,0:T(8,128)} %constant_dynamic-slice_fusion.8), channel_id=1, source_target_pairs={{0,3},{1,2},{2,1},{3,0},{4,7},{5,6},{6,5},{7,4},{8,11},{9,10},{10,... | collective-permute-start | bytes 1572872 | tf_op jit(solution)/shard_map/ppermute | solution.py:52
  184.7 8.3 %collective-permute-start.31 = (f32[528,128]{0,1:T(8,128)S(1)}, f32[528,128]{0,1:T(8,128)S(1)}, u32[]{:S(2)}, u32[]{:S(2)}) collective-permute-start(f32[528,128]{0,1:T(8,128)S(1)} %copy.44), channel_id=1, source_target_pairs={{0,8},{1,9},{2,10},{3,11},{4,12},{5,13},{6,14},{7,15},{8,0},{9,1},... | collective-permute-start | bytes 811016 | tf_op jit(solution)/shard_map/ppermute | solution.py:52
  193.0 19.1 %collective-permute-start.34 = (f32[32,2048]{1,0:T(8,128)}, f32[32,2048]{1,0:T(8,128)}, u32[]{:S(2)}, u32[]{:S(2)}) collective-permute-start(f32[32,2048]{1,0:T(8,128)} %constant_dynamic-slice_fusion.7), channel_id=1, source_target_pairs={{0,1},{1,0},{2,3},{3,2},{4,5},{5,4},{6,7},{7,6},{8,9},{9,8},{10,11... | collective-permute-start | bytes 786440 | tf_op jit(solution)/shard_map/ppermute | solution.py:52
  199.5 40.7 %all-to-all-start = ((f32[64,1,1280]{2,1,0:T(1,128)}), f32[64,1,1280]{2,1,0:T(1,128)}, u32[]{:S(2)}, u32[]{:S(2)}) async-start(f32[64,1,1280]{2,1,0:T(1,128)} %all_to_all.13), calls=%async_computation | async-start | bytes 655360 | tf_op jit(solution)/shard_map/all_to_all | solution.py:511
  211.3 63.6 %collective-permute-start.39 = (bf16[256,2048]{1,0:T(8,128)(2,1)}, bf16[256,2048]{1,0:T(8,128)(2,1)}, u32[]{:S(2)}, u32[]{:S(2)}) collective-permute-start(bf16[256,2048]{1,0:T(8,128)(2,1)} %get-tuple-element.60), channel_id=1, source_target_pairs={{0,8},{1,9},{2,10},{3,11},{4,12},{5,13},{6,14},{7,15},{8,0},{9,1},... | collective-permute-start | bytes 3145736 | tf_op jit(solution)/shard_map/ppermute | solution.py:52
  213.1 27.1 %collective-permute-start.35 = (f32[16,2048]{1,0:T(8,128)S(1)}, f32[16,2048]{1,0:T(8,128)}, u32[]{:S(2)}, u32[]{:S(2)}) collective-permute-start(f32[16,2048]{1,0:T(8,128)S(1)} %constant_dynamic-slice_fusion.6), channel_id=1, source_target_pairs={{0,96},{1,97},{2,98},{3,99},{4,100},{5,101},{6,102},{7,103},{8,104... | collective-permute-start | bytes 393224 | tf_op jit(solution)/shard_map/ppermute | solution.py:52
  239.9 29.9 %collective-permute-start.37 = (bf16[256,4096]{1,0:T(8,128)(2,1)}, bf16[256,4096]{1,0:T(8,128)(2,1)}, u32[]{:S(2)}, u32[]{:S(2)}) collective-permute-start(bf16[256,4096]{1,0:T(8,128)(2,1)} %get-tuple-element.41), channel_id=1, source_target_pairs={{0,8},{1,9},{2,10},{3,11},{4,12},{5,13},{6,14},{7,15},{8,0},{9,1},... | collective-permute-start | bytes 6291464 | tf_op jit(solution)/shard_map/ppermute | solution.py:52
  242.3 17.2 %all-to-all-start.1 = ((f32[64,1,1280]{2,1,0:T(1,128)}), f32[64,1,1280]{2,1,0:T(1,128)S(1)}, u32[]{:S(2)}, u32[]{:S(2)}) async-start(f32[64,1,1280]{2,1,0:T(1,128)} %broadcast_in_dim.98), calls=%async_computation.1 | async-start | bytes 655360 | tf_op jit(solution)/shard_map/all_to_all | solution.py:511
  251.6 21.9 %collective-permute-start.36 = (f32[8,2048]{1,0:T(8,128)}, f32[8,2048]{1,0:T(8,128)}, u32[]{:S(2)}, u32[]{:S(2)}) collective-permute-start(f32[8,2048]{1,0:T(8,128)} %constant_dynamic-slice_fusion.5), channel_id=1, source_target_pairs={{0,32},{1,33},{2,34},{3,35},{4,36},{5,37},{6,38},{7,39},{8,40},{9,... | collective-permute-start | bytes 196616 | tf_op jit(solution)/shard_map/ppermute | solution.py:52
  (45 other events, 499.9 us)

commit v5 on v4

--- a/solution.py
+++ b/solution.py
@@ -157,7 +157,7 @@
 
 def back_kernel(copies, n_src, scal, *refs):
     srcs = refs[:n_src]
-    grad, low_t, down, y_own, y_par, w_s, t_s, y_s, yo_s, yp_s, w_sem, out_sem = refs[n_src:]
+    grad, low, down, y_own, y_par, w_s, y_s, yo_s, yp_s, w_sem, out_sem = refs[n_src:]
     half = pl.multiple_of(scal[16], 2048)
     for wanted in range(8):
         for src, src_row, src_col, from_half, rows, shard, dst_row, block in copies:
@@ -171,30 +171,16 @@
                 w_sem.at[shard],
             ).start()
 
-    def flip(i, carry):
-        some = pl.ds(pl.multiple_of(i * 256, 256), 256)
-        t_s[some, :] = grad[:, some].T
-        return carry
-
-    lax.fori_loop(0, 8, flip, 0)
-
     def backward(shard, carry):
         columns = pl.ds(pl.multiple_of(scal[shard] * 512, 512), 512)
         pltpu.make_async_copy(w_s.at[columns, :], w_s.at[columns, :], w_sem.at[shard]).wait()
-        y_s[...] = jnp.dot(w_s[columns, :], t_s[...], preferred_element_type=f32)
-
-        def turn(i, carry):
-            part = pl.ds(pl.multiple_of(i * 128, 128), 128)
-            some = pl.ds(pl.multiple_of(scal[shard] * 512 + i * 128, 128), 128)
-            full = y_s[part, :] + lax.dot_general(
-                down[:, some], low_t[...], TN, preferred_element_type=f32
-            )
-            turned = full.astype(bf16).T
-            yo_s[:, some] = turned[:256]
-            yp_s[:, some] = turned[256:]
-            return carry
-
-        lax.fori_loop(0, 4, turn, 0)
+        y_s[...] = lax.dot_general(grad[...], w_s[columns, :], NT, preferred_element_type=f32)
+        for i in range(2):
+            some = pl.ds(i * 128, 128)
+            yo_s[some, columns] = (
+                y_s[some, :] + jnp.dot(low[some, :], down[:, columns], preferred_element_type=f32)
+            ).astype(bf16)
+            yp_s[some, columns] = y_s[pl.ds(256 + i * 128, 128), :].astype(bf16)
         pltpu.make_async_copy(yo_s.at[:, columns], y_own.at[:, columns], out_sem.at[0]).start()
         pltpu.make_async_copy(yp_s.at[:, columns], y_par.at[:, columns], out_sem.at[1]).start()
         return carry
@@ -204,7 +190,7 @@
     pltpu.make_async_copy(yp_s, y_par, out_sem.at[1]).wait()
 
 
-def back_call(copies, srcs, scal, grad, low_t, down):
+def back_call(copies, srcs, scal, grad, low, down):
     vm = pl.BlockSpec(memory_space=pltpu.VMEM)
     anyspace = pl.BlockSpec(memory_space=pltpu.HBM)
     srcs = [pltpu.with_memory_space_constraint(src, pltpu.HBM) for src in srcs]
@@ -215,7 +201,6 @@
         out_specs=[anyspace, anyspace],
         scratch_shapes=[
             pltpu.VMEM((4096, 2048), bf16),
-            pltpu.VMEM((2048, 512), bf16),
             pltpu.VMEM((512, 512), f32),
             pltpu.VMEM((256, 4096), bf16),
             pltpu.VMEM((256, 4096), bf16),
@@ -227,7 +212,7 @@
             flops=2 * 512 * 4096 * 2048, transcendentals=0, bytes_accessed=24 << 20
         ),
         name="back",
-    )(scal, *srcs, grad, low_t, down)
+    )(scal, *srcs, grad, low, down)
 
 
 def block_call(copies, srcs, scal, a_own, a_par, r_own, r_par, low, up, q_rows, q_f, carry):
@@ -322,11 +307,11 @@
     o_g = send(s_g, "xflip")
     o_ab = send(s_ab, "xflip")
 
-    p_blk = ordered(y % 2, p_chip, send(p_chip, "ynear"))
+    p_blk = ordered(z % 2, p_chip, send(p_chip, "znear"))
+    p_blk = ordered(z // 2, p_blk, send(p_blk, "zflip"))
+    p_half = p_blk
+    p_blk = ordered(y % 2, p_blk, send(p_blk, "ynear"))
     p_blk = ordered(y // 2, p_blk, send(p_blk, "yflip"))
-    p_half = p_blk
-    p_blk = ordered(z % 2, p_blk, send(p_blk, "znear"))
-    p_blk = ordered(z // 2, p_blk, send(p_blk, "zflip"))
     q_blk = ordered(x % 2, q_chip, send(q_chip, "xnear"))
     q_far, q_blk, _ = lax.optimization_barrier((send(q_blk, "xflip"), q_blk, p_blk))
     q_blk = ordered(x // 2, q_blk, q_far)
@@ -352,7 +337,7 @@
     q_feat = q_blk[:, :2048]
     positive = (q_blk[:, 2048].astype(f32) * 16 + q_blk[:, 2049].astype(f32)).astype(jnp.int32)
     row = jnp.arange(128, dtype=jnp.int32)
-    row_c, row_y, row_z = (row // 4) % 2, (row // 8) % 4, row // 32
+    row_c, row_z, row_y = (row // 4) % 2, (row // 8) % 4, row // 32
     passage_id = (((row_y * 2 + x_lo) * 2 + row_c) * 8 + x_hi * 4 + row_z) * 4 + row % 4
     partial = lax.dot_general(q_feat, p_blk, NT, preferred_element_type=f32)
     logits = logit_scale * (partial + send(partial, "core"))
@@ -489,13 +474,12 @@
                 srcs.append(value)
             index = [value is known for known in srcs].index(True)
             copies.append((index, at, column, from_half, rows, shard, dst_row, block + shift))
-    low_t = jnp.concatenate([low_grad[:256], jnp.zeros((256, 16), bf16)], axis=0).T
     y_own, y_par = back_call(
         copies,
         srcs,
         numbers(ring[:3] + [4] + ring[3:] + [5, 6, 7]),
         res_grad,
-        low_t,
+        low_grad[:256],
         adapter_down_weight.T,
     )
     y_got = send(y_par, "core")
@@ -522,10 +506,10 @@
 
     p_sum = p_part
     for bit, n, move, until in (
-        (z // 2, 64, "zflip", stats_own),
-        (z % 2, 32, "znear", packed_total),
-        (y // 2, 16, "yflip", part),
-        (y % 2, 8, "ynear", attn_grad),
+        (y // 2, 64, "yflip", stats_own),
+        (y % 2, 32, "ynear", packed_total),
+        (z // 2, 16, "zflip", y_par),
+        (z % 2, 8, "znear", attn_grad),
     ):
         got = send(pick(p_sum, n * (1 - bit), n), move)
         got, p_sum, _ = lax.optimization_barrier((got, p_sum, until))

time: 282 us -> 271 us (0.961)
  Pallas kernels: 49.8 us -> 41 us
  starting transfers between devices: 77.5 us -> 71.4 us
    pallas_call x1, Pallas kernels: 22.5 us -> 13.9 us  [back_call(): pl.pallas_call(functools.partial(back_kernel, copies, len(srcs)), out_sha...]
    all_to_all x2, starting transfers between devices: 18.1 us -> 13.3 us  [compute(): lax.all_to_all(value, AX, 0, 0, axis_index_groups=sides, tiled=True)]
    unnamed x68 -> x78, local copies, waits for them, and re-layouts: 7.28 us -> 7.4 us
  transfers between devices with their start and end apart: 42 -> 42, of which waited for: 13 -> 12; matrix products, arithmetic and copies ran while one was open for 15% -> 17% of each run, Pallas kernels for 18% -> 15%
where the time goes in v5:
time: 271 us; the launch traced here: 270 us
  waiting for transfers between devices  93.1 us (34%)
  starting transfers between devices  71.4 us (26%)
  Pallas kernels  41 us (15%)
  local copies, waits for them, and re-layouts  30.1 us (11%)
  other arithmetic  21.8 us (8%)
  between operations  8.97 us (3%)
  matrix products  3.79 us (1%)
    ppermute x40, waiting for transfers between devices, send(): return lax.ppermute(value, AX, MOVES[move])  86 us
    ppermute x40, starting transfers between devices, send(): return lax.ppermute(value, AX, MOVES[move])  58 us
    pallas_call x2, Pallas kernels, block_call(): pl.pallas_call(functools.partial(block_kernel, copies, len(srcs), first),...  27.1 us
    pallas_call x1, Pallas kernels, back_call(): pl.pallas_call(functools.partial(back_kernel, copies, len(srcs)), out_sha...  13.9 us
    all_to_all x2, starting transfers between devices, compute(): lax.all_to_all(value, AX, 0, 0, axis_index_groups=sides, tiled=True)  13.3 us
    unnamed x78, local copies, waits for them, and re-layouts  7.4 us
    all_to_all x2, waiting for transfers between devices, compute(): lax.all_to_all(value, AX, 0, 0, axis_index_groups=sides, tiled=True)  7.06 us
    dynamic_slice x13, local copies, waits for them, and re-layouts, pick(): return lax.dynamic_slice_in_dim(value, start, size, axis=axis)  5.89 us
  transfers between devices with their start and end apart: 42, of which 12 were waited for; matrix products, arithmetic and copies ran while one was open for 17% of the time, Pallas kernels for 15%

profile of v5, /device:TPU:1, one launch (start us, length us, event | category | flops | bytes accessed | tf_op | source)
XLA Modules:
  0.0 270.2 jit_solution(11185534342980275622)
XLA Ops:
  1.8 3.4 %collective-permute-start.5 = (bf16[512,256]{1,0:T(8,128)(2,1)S(1)}, bf16[512,256]{1,0:T(8,128)(2,1)S(1)}, u32[]{:S(2)}, u32[]{:S(2)}) collective-permute-start(bf16[512,256]{1,0:T(8,128)(2,1)S(1)} %get-tuple-element.55), channel_id=1, source_target_pairs={{0,20},{1,21},{2,22},{3,23},{4,16},{5,17},{6,18},{7,19},{8,28},{9,... | collective-permute-start | bytes 786440 | tf_op jit(solution)/shard_map/ppermute | solution.py:52
  8.7 2.3 constant_dynamic-slice_fusion.15
  11.1 2.2 constant_dynamic-slice_fusion.1
  19.0 3.7 %collective-permute-start.17 = (bf16[16,2048]{1,0:T(8,128)(2,1)S(1)}, bf16[16,2048]{1,0:T(8,128)(2,1)S(1)}, u32[]{:S(2)}, u32[]{:S(2)}) collective-permute-start(bf16[16,2048]{1,0:T(8,128)(2,1)S(1)} %maximum_select_fusion.9), channel_id=1, source_target_pairs={{0,3},{1,2},{2,1},{3,0},{4,7},{5,6},{6,5},{7,4},{8,11},{9,10},{10,... | collective-permute-start | bytes 196616 | tf_op jit(solution)/shard_map/ppermute | solution.py:52
  22.7 2.0 collective-permute-done.17
  26.1 2.4 collective-permute-start.21
  28.6 2.1 collective-permute-start.18
  33.4 5.7 %collective-permute-done.23 = bf16[64,2048]{1,0:T(8,128)(2,1)S(1)} collective-permute-done((bf16[64,2048]{1,0:T(8,128)(2,1)S(1)}, bf16[64,2048]{1,0:T(8,128)(2,1)S(1)}, u32[]{:S(2)}, u32[]{:S(2)}) %collective-permute-start.23) | collective-permute-done | bytes 262176 | tf_op jit(solution)/shard_map/ppermute | solution.py:52
  42.8 2.8 %collective-permute-start.7 = (bf16[1536,256]{1,0:T(8,128)(2,1)S(1)}, bf16[1536,256]{1,0:T(8,128)(2,1)S(1)}, u32[]{:S(2)}, u32[]{:S(2)}) collective-permute-start(bf16[1536,256]{1,0:T(8,128)(2,1)S(1)} %pad_maximum_fusion.3), channel_id=1, source_target_pairs={{0,3},{1,0},{2,1},{3,2},{4,7},{5,4},{6,5},{7,6},{8,11},{9,8},{10,9... | collective-permute-start | bytes 2359304 | tf_op jit(solution)/shard_map/ppermute | solution.py:52
  46.7 3.0 %collective-permute-done.26 = f32[4,32]{1,0:T(4,128)S(1)} collective-permute-done((f32[4,32]{1,0:T(4,128)S(1)}, f32[4,32]{1,0:T(4,128)S(1)}, u32[]{:S(2)}, u32[]{:S(2)}) %collective-permute-start.26) | collective-permute-done | bytes 544 | tf_op jit(solution)/shard_map/ppermute | solution.py:52
  53.2 2.7 collective-permute-done.27
  55.8 7.3 %collective-permute-done.6.refs_8_ = bf16[1536,256]{1,0:T(8,128)(2,1)S(1)} collective-permute-done((bf16[1536,256]{1,0:T(8,128)(2,1)S(1)}, bf16[1536,256]{1,0:T(8,128)(2,1)S(1)}, u32[]{:S(2)}, u32[]{:S(2)}) %collective-permute-start.6) | collective-permute-done | bytes 786464 | tf_op jit(solution)/shard_map/ppermute | solution.py:52
  63.4 2.7 %collective-permute-start.12 = (bf16[768,256]{1,0:T(8,128)(2,1)S(1)}, bf16[768,256]{1,0:T(8,128)(2,1)S(1)}, u32[]{:S(2)}, u32[]{:S(2)}) collective-permute-start(bf16[768,256]{1,0:T(8,128)(2,1)S(1)} %pad_maximum_fusion.7), channel_id=1, source_target_pairs={{0,3},{1,0},{2,1},{3,2},{4,7},{5,4},{6,5},{7,6},{8,11},{9,8},{10,9... | collective-permute-start | bytes 1179656 | tf_op jit(solution)/shard_map/ppermute | solution.py:52
  67.5 6.7 %collective-permute-done.11.refs_10_ = bf16[768,256]{1,0:T(8,128)(2,1)S(1)} collective-permute-done((bf16[768,256]{1,0:T(8,128)(2,1)S(1)}, bf16[768,256]{1,0:T(8,128)(2,1)S(1)}, u32[]{:S(2)}, u32[]{:S(2)}) %collective-permute-start.11) | collective-permute-done | bytes 393248 | tf_op jit(solution)/shard_map/ppermute | solution.py:52
  74.3 2.1 collective-permute-start.10
  79.6 34.5 %collective-permute-done.13.refs_6_ = bf16[1024,256]{1,0:T(8,128)(2,1)S(1)} collective-permute-done((bf16[1024,256]{1,0:T(8,128)(2,1)S(1)}, bf16[1024,256]{1,0:T(8,128)(2,1)S(1)}, u32[]{:S(2)}, u32[]{:S(2)}) %collective-permute-start.13) | collective-permute-done | bytes 524320 | tf_op jit(solution)/shard_map/ppermute | solution.py:52
  114.1 2.9 %collective-permute-start.19 = (bf16[256,2048]{1,0:T(8,128)(2,1)S(1)}, bf16[256,2048]{1,0:T(8,128)(2,1)S(1)}, u32[]{:S(2)}, u32[]{:S(2)}) collective-permute-start(bf16[256,2048]{1,0:T(8,128)(2,1)S(1)} %constant_dynamic-slice_fusion.13), channel_id=1, source_target_pairs={{0,8},{1,9},{2,10},{3,11},{4,12},{5,13},{6,14},{7,15},{8,0},{9,1},... | collective-permute-start | bytes 3145736 | tf_op jit(solution)/shard_map/ppermute | solution.py:52
  121.6 3.4 %collective-permute-start.14 = (bf16[1792,256]{1,0:T(8,128)(2,1)}, bf16[1792,256]{1,0:T(8,128)(2,1)}, u32[]{:S(2)}, u32[]{:S(2)}) collective-permute-start(bf16[1792,256]{1,0:T(8,128)(2,1)} %pad_maximum_fusion.2), channel_id=1, source_target_pairs={{0,96},{1,97},{2,98},{3,99},{4,100},{5,101},{6,102},{7,103},{8,104... | collective-permute-start | bytes 2752520 | tf_op jit(solution)/shard_map/ppermute | solution.py:52
  125.0 22.3 %collective-permute-done.2.refs_3_.refs_14_ = bf16[1024,768]{1,0:T(8,128)(2,1)S(1)} collective-permute-done((bf16[1024,768]{1,0:T(8,128)(2,1)S(1)}, bf16[1024,768]{1,0:T(8,128)(2,1)S(1)}, u32[]{:S(2)}, u32[]{:S(2)}) %collective-permute-start.2) | collective-permute-done | bytes 1572896 | tf_op jit(solution)/shard_map/ppermute | solution.py:52
  150.1 2.7 collective-permute-start.4
  153.6 2.8 %collective-permute-start.33 = (f32[64,2048]{1,0:T(8,128)S(1)}, f32[64,2048]{1,0:T(8,128)S(1)}, u32[]{:S(2)}, u32[]{:S(2)}) collective-permute-start(f32[64,2048]{1,0:T(8,128)S(1)} %copy-done.34), channel_id=1, source_target_pairs={{0,96},{1,97},{2,98},{3,99},{4,100},{5,101},{6,102},{7,103},{8,104... | collective-permute-start | bytes 1572872 | tf_op jit(solution)/shard_map/ppermute | solution.py:52
  156.5 13.3 %block_first.1 = (f32[512,2048]{1,0:T(8,128)S(1)}, f32[528,128]{1,0:T(8,128)S(1)}) custom-call(s32[13]{0:T(128)S(1)} %stack.117.scal, bf16[512,4096]{1,0:T(8,128)(2,1)} %refs_0_.5, bf16[2560,256]{1,0:T(8,128)(2,1)} %copy-done.12, bf16[1024,256]{1,0:T(8,128)(2,1)} %copy-done.24, bf16[2560,256]{1,0:T(8,128)(2,1)} %copy-done.18, bf16[1024,256]{1,0:T(8,128)(2,1)} %copy-done.31, ...), custom_call_target="tpu_custom_call" | custom-call | flops 4294967296 | bytes 16777216 | tf_op jit(solution)/shard_map/block_first/pallas_call | solution.py:246
  172.7 13.8 %block_last.1 = (f32[512,2048]{1,0:T(8,128)}, f32[528,128]{1,0:T(8,128)S(1)}) custom-call(s32[13]{0:T(128)S(1)} %stack.107.scal, bf16[512,4096]{1,0:T(8,128)(2,1)} %refs_0_.5, bf16[512,1024]{1,0:T(8,128)(2,1)} %collective-permute-done.refs_7_.refs_1_, bf16[1024,768]{1,0:T(8,128)(2,1)} %copy-done.19, ...), custom_call_target="tpu_custom_call", output_to_operand_aliasing={{0}: (18, {})} | custom-call | flops 4294967296 | bytes 16777216 | tf_op jit(solution)/shard_map/block_last/pallas_call | solution.py:246
  186.5 4.5 %collective-permute-start.31 = (f32[528,128]{1,0:T(8,128)S(1)}, f32[528,128]{1,0:T(8,128)}, u32[]{:S(2)}, u32[]{:S(2)}) collective-permute-start(f32[528,128]{1,0:T(8,128)S(1)} %get-tuple-element.32), channel_id=1, source_target_pairs={{0,8},{1,9},{2,10},{3,11},{4,12},{5,13},{6,14},{7,15},{8,0},{9,1},... | collective-permute-start | bytes 811016 | tf_op jit(solution)/shard_map/ppermute | solution.py:52
  202.3 5.5 %all-to-all-start = ((f32[64,1,1280]{2,1,0:T(1,128)}), f32[64,1,1280]{2,1,0:T(1,128)}, u32[]{:S(2)}, u32[]{:S(2)}) async-start(f32[64,1,1280]{2,1,0:T(1,128)} %all_to_all.13), calls=%async_computation | async-start | bytes 655360 | tf_op jit(solution)/shard_map/all_to_all | solution.py:495
  210.3 2.6 collective-permute-start.35
  212.9 13.9 %back.1 = (bf16[256,4096]{1,0:T(8,128)(2,1)S(1)}, bf16[256,4096]{1,0:T(8,128)(2,1)}) custom-call(s32[17]{0:T(128)S(1)} %stack.119.scal, bf16[512,4096]{1,0:T(8,128)(2,1)} %refs_0_.5, bf16[2560,256]{1,0:T(8,128)(2,1)} %copy-done.12, bf16[1024,256]{1,0:T(8,128)(2,1)} %copy-done.24, bf16[2560,256]{1,0:T(8,128)(2,1)} %copy-done.18, ...), custom_call_target="tpu_custom_call" | custom-call | flops 8589934592 | bytes 25165824 | tf_op jit(solution)/shard_map/back/pallas_call | solution.py:197
  230.6 7.9 %all-to-all-start.1 = ((f32[64,1,1280]{2,1,0:T(1,128)}), f32[64,1,1280]{2,1,0:T(1,128)S(1)}, u32[]{:S(2)}, u32[]{:S(2)}) async-start(f32[64,1,1280]{2,1,0:T(1,128)} %broadcast_in_dim.97), calls=%async_computation.1 | async-start | bytes 655360 | tf_op jit(solution)/shard_map/all_to_all | solution.py:495
  241.3 7.1 %all-to-all-done.1 = f32[64,1,1280]{2,1,0:T(1,128)S(1)} async-done(((f32[64,1,1280]{2,1,0:T(1,128)}), f32[64,1,1280]{2,1,0:T(1,128)S(1)}, u32[]{:S(2)}, u32[]{:S(2)}) %all-to-all-start.1) | async-done | bytes 327712 | tf_op jit(solution)/shard_map/all_to_all | solution.py:495
  251.0 2.1 collective-permute-start.32
  258.4 3.7 %add_convert_fusion = bf16[256,4096]{1,0:T(8,128)(2,1)} fusion(bf16[256,4096]{1,0:T(8,128)(2,1)} %collective-permute-done.37, bf16[256,4096]{1,0:T(8,128)(2,1)S(1)} %copy-done.5), kind=kLoop, calls=%fused_computation.3 | loop fusion | flops 4194304 | bytes 6291456 | tf_op jit(solution)/shard_map/convert_element_type | solution.py:486
  263.5 3.7 %maximum_select_fusion = bf16[1,256,4096]{2,1,0:T(8,128)(2,1)} fusion(bf16[1,256,2048]{2,1,0:T(8,128)(2,1)} %bitcast.39, bf16[1,256,2048]{2,1,0:T(8,128)(2,1)S(1)} %get-tuple-element.57, pred[]{:T(512)S(6)} %eq.71), kind=kLoop, calls=%fused_computation.9 | loop fusion | flops 9437184 | bytes 4194305 | tf_op jit(solution)/shard_map/jit(_where)/select_n | solution.py:56
  (270 shorter events, 63.3 us)
Async XLA Ops:
  1.8 40.7 %collective-permute-start.5 = (bf16[512,256]{1,0:T(8,128)(2,1)S(1)}, bf16[512,256]{1,0:T(8,128)(2,1)S(1)}, u32[]{:S(2)}, u32[]{:S(2)}) collective-permute-start(bf16[512,256]{1,0:T(8,128)(2,1)S(1)} %get-tuple-element.55), channel_id=1, source_target_pairs={{0,20},{1,21},{2,22},{3,23},{4,16},{5,17},{6,18},{7,19},{8,28},{9,... | collective-permute-start | bytes 786440 | tf_op jit(solution)/shard_map/ppermute | solution.py:52
  7.7 7.7 %collective-permute-start.15 = (bf16[8,2176]{1,0:T(8,128)(2,1)S(1)}, bf16[8,2176]{1,0:T(8,128)(2,1)S(1)}, u32[]{:S(2)}, u32[]{:S(2)}) collective-permute-start(bf16[8,2176]{1,0:T(8,128)(2,1)S(1)} %get-tuple-element.86), channel_id=1, source_target_pairs={{0,8},{1,9},{2,10},{3,11},{4,12},{5,13},{6,14},{7,15},{8,0},{9,1},... | collective-permute-start | bytes 104456 | tf_op jit(solution)/shard_map/ppermute | solution.py:52
  11.0 67.2 %collective-permute-start = (bf16[512,1024]{1,0:T(8,128)(2,1)}, bf16[512,1024]{1,0:T(8,128)(2,1)}, u32[]{:S(2)}, u32[]{:S(2)}) collective-permute-start(bf16[512,1024]{1,0:T(8,128)(2,1)} %constant_dynamic-slice_fusion.15), channel_id=1, source_target_pairs={{0,20},{1,21},{2,22},{3,23},{4,16},{5,17},{6,18},{7,19},{8,28},{9,... | collective-permute-start | bytes 3145736 | tf_op jit(solution)/shard_map/ppermute | solution.py:52
  17.3 8.8 %collective-permute-start.20 = (bf16[8,2176]{1,0:T(8,128)(2,1)S(1)}, bf16[8,2176]{1,0:T(8,128)(2,1)S(1)}, u32[]{:S(2)}, u32[]{:S(2)}) collective-permute-start(bf16[8,2176]{1,0:T(8,128)(2,1)S(1)} %maximum_select_fusion.10), channel_id=1, source_target_pairs={{0,16},{1,17},{2,18},{3,19},{4,20},{5,21},{6,22},{7,23},{8,24},{9,... | collective-permute-start | bytes 104456 | tf_op jit(solution)/shard_map/ppermute | solution.py:52
  26.1 13.2 %collective-permute-start.21 = (bf16[16,2176]{1,0:T(8,128)(2,1)S(1)}, bf16[16,2176]{1,0:T(8,128)(2,1)S(1)}, u32[]{:S(2)}, u32[]{:S(2)}) collective-permute-start(bf16[16,2176]{1,0:T(8,128)(2,1)S(1)} %maximum_select_fusion.8), channel_id=1, source_target_pairs={{0,20},{1,21},{2,22},{3,23},{4,16},{5,17},{6,18},{7,19},{8,28},{9,... | collective-permute-start | bytes 208904 | tf_op jit(solution)/shard_map/ppermute | solution.py:52
  28.6 121.5 %collective-permute-start.18 = (bf16[256,4096]{1,0:T(8,128)(2,1)S(1)}, bf16[256,4096]{1,0:T(8,128)(2,1)S(1)}, u32[]{:S(2)}, u32[]{:S(2)}) collective-permute-start(bf16[256,4096]{1,0:T(8,128)(2,1)S(1)} %bitcast.114), channel_id=1, source_target_pairs={{0,8},{1,9},{2,10},{3,11},{4,12},{5,13},{6,14},{7,15},{8,0},{9,1},... | collective-permute-start | bytes 6291464 | tf_op jit(solution)/shard_map/ppermute | solution.py:52
  30.7 8.5 %collective-permute-start.23 = (bf16[64,2048]{1,0:T(8,128)(2,1)S(1)}, bf16[64,2048]{1,0:T(8,128)(2,1)S(1)}, u32[]{:S(2)}, u32[]{:S(2)}) collective-permute-start(bf16[64,2048]{1,0:T(8,128)(2,1)S(1)} %maximum_select_fusion.2), channel_id=1, source_target_pairs={{0,96},{1,97},{2,98},{3,99},{4,100},{5,101},{6,102},{7,103},{8,104... | collective-permute-start | bytes 786440 | tf_op jit(solution)/shard_map/ppermute | solution.py:52
  42.5 20.6 %collective-permute-start.6 = (bf16[1536,256]{1,0:T(8,128)(2,1)S(1)}, bf16[1536,256]{1,0:T(8,128)(2,1)S(1)}, u32[]{:S(2)}, u32[]{:S(2)}) collective-permute-start(bf16[1536,256]{1,0:T(8,128)(2,1)S(1)} %pad_maximum_fusion.3), channel_id=1, source_target_pairs={{0,1},{1,2},{2,3},{3,0},{4,5},{5,6},{6,7},{7,4},{8,9},{9,10},{10,1... | collective-permute-start | bytes 2359304 | tf_op jit(solution)/shard_map/ppermute | solution.py:52
  42.8 20.5 %collective-permute-start.7 = (bf16[1536,256]{1,0:T(8,128)(2,1)S(1)}, bf16[1536,256]{1,0:T(8,128)(2,1)S(1)}, u32[]{:S(2)}, u32[]{:S(2)}) collective-permute-start(bf16[1536,256]{1,0:T(8,128)(2,1)S(1)} %pad_maximum_fusion.3), channel_id=1, source_target_pairs={{0,3},{1,0},{2,1},{3,2},{4,7},{5,4},{6,5},{7,6},{8,11},{9,8},{10,9... | collective-permute-start | bytes 2359304 | tf_op jit(solution)/shard_map/ppermute | solution.py:52
  63.2 11.0 %collective-permute-start.11 = (bf16[768,256]{1,0:T(8,128)(2,1)S(1)}, bf16[768,256]{1,0:T(8,128)(2,1)S(1)}, u32[]{:S(2)}, u32[]{:S(2)}) collective-permute-start(bf16[768,256]{1,0:T(8,128)(2,1)S(1)} %pad_maximum_fusion.6), channel_id=1, source_target_pairs={{0,1},{1,2},{2,3},{3,0},{4,5},{5,6},{6,7},{7,4},{8,9},{9,10},{10,1... | collective-permute-start | bytes 1179656 | tf_op jit(solution)/shard_map/ppermute | solution.py:52
  63.4 13.0 %collective-permute-start.12 = (bf16[768,256]{1,0:T(8,128)(2,1)S(1)}, bf16[768,256]{1,0:T(8,128)(2,1)S(1)}, u32[]{:S(2)}, u32[]{:S(2)}) collective-permute-start(bf16[768,256]{1,0:T(8,128)(2,1)S(1)} %pad_maximum_fusion.7), channel_id=1, source_target_pairs={{0,3},{1,0},{2,1},{3,2},{4,7},{5,4},{6,5},{7,6},{8,11},{9,8},{10,9... | collective-permute-start | bytes 1179656 | tf_op jit(solution)/shard_map/ppermute | solution.py:52
  66.2 10.9 %collective-permute-start.28 = (f32[8,2048]{1,0:T(8,128)S(1)}, f32[8,2048]{1,0:T(8,128)S(1)}, u32[]{:S(2)}, u32[]{:S(2)}) collective-permute-start(f32[8,2048]{1,0:T(8,128)S(1)} %constant_dynamic-slice_fusion.10), channel_id=1, source_target_pairs={{0,16},{1,17},{2,18},{3,19},{4,20},{5,21},{6,22},{7,23},{8,24},{9,... | collective-permute-start | bytes 196616 | tf_op jit(solution)/shard_map/ppermute | solution.py:52
  74.3 39.9 %collective-permute-start.10 = (bf16[2560,256]{1,0:T(8,128)(2,1)S(1)}, bf16[2560,256]{1,0:T(8,128)(2,1)S(1)}, u32[]{:S(2)}, u32[]{:S(2)}) collective-permute-start(bf16[2560,256]{1,0:T(8,128)(2,1)S(1)} %pad_maximum_fusion.1.refs_1_), channel_id=1, source_target_pairs={{0,96},{1,97},{2,98},{3,99},{4,100},{5,101},{6,102},{7,103},{8,104... | collective-permute-start | bytes 3932168 | tf_op jit(solution)/shard_map/ppermute | solution.py:52
  76.5 37.5 %collective-permute-start.13 = (bf16[1024,256]{1,0:T(8,128)(2,1)S(1)}, bf16[1024,256]{1,0:T(8,128)(2,1)S(1)}, u32[]{:S(2)}, u32[]{:S(2)}) collective-permute-start(bf16[1024,256]{1,0:T(8,128)(2,1)S(1)} %pad_maximum_fusion.5.refs_2_), channel_id=1, source_target_pairs={{0,96},{1,97},{2,98},{3,99},{4,100},{5,101},{6,102},{7,103},{8,104... | collective-permute-start | bytes 1572872 | tf_op jit(solution)/shard_map/ppermute | solution.py:52
  77.1 41.1 %collective-permute-start.8 = (bf16[2560,256]{1,0:T(8,128)(2,1)S(1)}, bf16[2560,256]{1,0:T(8,128)(2,1)S(1)}, u32[]{:S(2)}, u32[]{:S(2)}) collective-permute-start(bf16[2560,256]{1,0:T(8,128)(2,1)S(1)} %pad_maximum_fusion.1.refs_1_), channel_id=1, source_target_pairs={{0,32},{1,33},{2,34},{3,35},{4,36},{5,37},{6,38},{7,39},{8,40},{9,... | collective-permute-start | bytes 3932168 | tf_op jit(solution)/shard_map/ppermute | solution.py:52
  79.5 42.1 %collective-permute-start.1 = (bf16[1024,768]{1,0:T(8,128)(2,1)S(1)}, bf16[1024,768]{1,0:T(8,128)(2,1)S(1)}, u32[]{:S(2)}, u32[]{:S(2)}) collective-permute-start(bf16[1024,768]{1,0:T(8,128)(2,1)S(1)} %pad_maximum_fusion), channel_id=1, source_target_pairs={{0,1},{1,2},{2,3},{3,0},{4,5},{5,6},{6,7},{7,4},{8,9},{9,10},{10,1... | collective-permute-start | bytes 4718600 | tf_op jit(solution)/shard_map/ppermute | solution.py:52
  114.1 33.3 %collective-permute-start.2 = (bf16[1024,768]{1,0:T(8,128)(2,1)S(1)}, bf16[1024,768]{1,0:T(8,128)(2,1)S(1)}, u32[]{:S(2)}, u32[]{:S(2)}) collective-permute-start(bf16[1024,768]{1,0:T(8,128)(2,1)S(1)} %pad_maximum_fusion), channel_id=1, source_target_pairs={{0,3},{1,0},{2,1},{3,2},{4,7},{5,4},{6,5},{7,6},{8,11},{9,8},{10,9... | collective-permute-start | bytes 4718600 | tf_op jit(solution)/shard_map/ppermute | solution.py:52
  114.1 6.8 %collective-permute-start.19 = (bf16[256,2048]{1,0:T(8,128)(2,1)S(1)}, bf16[256,2048]{1,0:T(8,128)(2,1)S(1)}, u32[]{:S(2)}, u32[]{:S(2)}) collective-permute-start(bf16[256,2048]{1,0:T(8,128)(2,1)S(1)} %constant_dynamic-slice_fusion.13), channel_id=1, source_target_pairs={{0,8},{1,9},{2,10},{3,11},{4,12},{5,13},{6,14},{7,15},{8,0},{9,1},... | collective-permute-start | bytes 3145736 | tf_op jit(solution)/shard_map/ppermute | solution.py:52
  118.2 31.8 %collective-permute-start.29 = (bf16[1024,256]{1,0:T(8,128)(2,1)S(1)}, bf16[1024,256]{1,0:T(8,128)(2,1)S(1)}, u32[]{:S(2)}, u32[]{:S(2)}) collective-permute-start(bf16[1024,256]{1,0:T(8,128)(2,1)S(1)} %pad_maximum_fusion.5.refs_2_), channel_id=1, source_target_pairs={{0,32},{1,33},{2,34},{3,35},{4,36},{5,37},{6,38},{7,39},{8,40},{9,... | collective-permute-start | bytes 1572872 | tf_op jit(solution)/shard_map/ppermute | solution.py:52
  121.0 32.6 %collective-permute-start.30 = (bf16[1536,256]{1,0:T(8,128)(2,1)}, bf16[1536,256]{1,0:T(8,128)(2,1)}, u32[]{:S(2)}, u32[]{:S(2)}) collective-permute-start(bf16[1536,256]{1,0:T(8,128)(2,1)} %pad_maximum_fusion.4), channel_id=1, source_target_pairs={{0,20},{1,21},{2,22},{3,23},{4,16},{5,17},{6,18},{7,19},{8,28},{9,... | collective-permute-start | bytes 2359304 | tf_op jit(solution)/shard_map/ppermute | solution.py:52
  121.6 50.2 %collective-permute-start.14 = (bf16[1792,256]{1,0:T(8,128)(2,1)}, bf16[1792,256]{1,0:T(8,128)(2,1)}, u32[]{:S(2)}, u32[]{:S(2)}) collective-permute-start(bf16[1792,256]{1,0:T(8,128)(2,1)} %pad_maximum_fusion.2), channel_id=1, source_target_pairs={{0,96},{1,97},{2,98},{3,99},{4,100},{5,101},{6,102},{7,103},{8,104... | collective-permute-start | bytes 2752520 | tf_op jit(solution)/shard_map/ppermute | solution.py:52
  147.4 24.4 %collective-permute-start.9 = (bf16[1792,256]{1,0:T(8,128)(2,1)}, bf16[1792,256]{1,0:T(8,128)(2,1)}, u32[]{:S(2)}, u32[]{:S(2)}) collective-permute-start(bf16[1792,256]{1,0:T(8,128)(2,1)} %slice.263), channel_id=1, source_target_pairs={{0,32},{1,33},{2,34},{3,35},{4,36},{5,37},{6,38},{7,39},{8,40},{9,... | collective-permute-start | bytes 2752520 | tf_op jit(solution)/shard_map/ppermute | solution.py:52
  150.1 21.7 %collective-permute-start.3 = (bf16[512,768]{1,0:T(8,128)(2,1)}, bf16[512,768]{1,0:T(8,128)(2,1)}, u32[]{:S(2)}, u32[]{:S(2)}) collective-permute-start(bf16[512,768]{1,0:T(8,128)(2,1)} %slice.259), channel_id=1, source_target_pairs={{0,1},{1,2},{2,3},{3,0},{4,5},{5,6},{6,7},{7,4},{8,9},{9,10},{10,1... | collective-permute-start | bytes 2359304 | tf_op jit(solution)/shard_map/ppermute | solution.py:52
  150.1 21.7 %collective-permute-start.4 = (bf16[512,768]{1,0:T(8,128)(2,1)}, bf16[512,768]{1,0:T(8,128)(2,1)S(1)}, u32[]{:S(2)}, u32[]{:S(2)}) collective-permute-start(bf16[512,768]{1,0:T(8,128)(2,1)} %slice.260), channel_id=1, source_target_pairs={{0,3},{1,0},{2,1},{3,2},{4,7},{5,4},{6,5},{7,6},{8,11},{9,8},{10,9... | collective-permute-start | bytes 2359304 | tf_op jit(solution)/shard_map/ppermute | solution.py:52
  153.6 37.4 %collective-permute-start.33 = (f32[64,2048]{1,0:T(8,128)S(1)}, f32[64,2048]{1,0:T(8,128)S(1)}, u32[]{:S(2)}, u32[]{:S(2)}) collective-permute-start(f32[64,2048]{1,0:T(8,128)S(1)} %copy-done.34), channel_id=1, source_target_pairs={{0,96},{1,97},{2,98},{3,99},{4,100},{5,101},{6,102},{7,103},{8,104... | collective-permute-start | bytes 1572872 | tf_op jit(solution)/shard_map/ppermute | solution.py:52
  191.9 17.4 %collective-permute-start.34 = (f32[32,2048]{1,0:T(8,128)}, f32[32,2048]{1,0:T(8,128)}, u32[]{:S(2)}, u32[]{:S(2)}) collective-permute-start(f32[32,2048]{1,0:T(8,128)} %constant_dynamic-slice_fusion.7), channel_id=1, source_target_pairs={{0,32},{1,33},{2,34},{3,35},{4,36},{5,37},{6,38},{7,39},{8,40},{9,... | collective-permute-start | bytes 786440 | tf_op jit(solution)/shard_map/ppermute | solution.py:52
  202.3 26.2 %all-to-all-start = ((f32[64,1,1280]{2,1,0:T(1,128)}), f32[64,1,1280]{2,1,0:T(1,128)}, u32[]{:S(2)}, u32[]{:S(2)}) async-start(f32[64,1,1280]{2,1,0:T(1,128)} %all_to_all.13), calls=%async_computation | async-start | bytes 655360 | tf_op jit(solution)/shard_map/all_to_all | solution.py:495
  208.9 54.6 %collective-permute-start.39 = (bf16[256,2048]{1,0:T(8,128)(2,1)}, bf16[256,2048]{1,0:T(8,128)(2,1)}, u32[]{:S(2)}, u32[]{:S(2)}) collective-permute-start(bf16[256,2048]{1,0:T(8,128)(2,1)} %get-tuple-element.58), channel_id=1, source_target_pairs={{0,8},{1,9},{2,10},{3,11},{4,12},{5,13},{6,14},{7,15},{8,0},{9,1},... | collective-permute-start | bytes 3145736 | tf_op jit(solution)/shard_map/ppermute | solution.py:52
  210.3 18.2 %collective-permute-start.35 = (f32[16,2048]{1,0:T(8,128)S(1)}, f32[16,2048]{1,0:T(8,128)}, u32[]{:S(2)}, u32[]{:S(2)}) collective-permute-start(f32[16,2048]{1,0:T(8,128)S(1)} %constant_dynamic-slice_fusion.6), channel_id=1, source_target_pairs={{0,3},{1,2},{2,1},{3,0},{4,7},{5,6},{6,5},{7,4},{8,11},{9,10},{10,... | collective-permute-start | bytes 393224 | tf_op jit(solution)/shard_map/ppermute | solution.py:52
  228.2 30.2 %collective-permute-start.37 = (bf16[256,4096]{1,0:T(8,128)(2,1)}, bf16[256,4096]{1,0:T(8,128)(2,1)}, u32[]{:S(2)}, u32[]{:S(2)}) collective-permute-start(bf16[256,4096]{1,0:T(8,128)(2,1)} %get-tuple-element.38), channel_id=1, source_target_pairs={{0,8},{1,9},{2,10},{3,11},{4,12},{5,13},{6,14},{7,15},{8,0},{9,1},... | collective-permute-start | bytes 6291464 | tf_op jit(solution)/shard_map/ppermute | solution.py:52
  230.6 17.8 %all-to-all-start.1 = ((f32[64,1,1280]{2,1,0:T(1,128)}), f32[64,1,1280]{2,1,0:T(1,128)S(1)}, u32[]{:S(2)}, u32[]{:S(2)}) async-start(f32[64,1,1280]{2,1,0:T(1,128)} %broadcast_in_dim.97), calls=%async_computation.1 | async-start | bytes 655360 | tf_op jit(solution)/shard_map/all_to_all | solution.py:495
  240.3 21.8 %collective-permute-start.36 = (f32[8,2048]{1,0:T(8,128)}, f32[8,2048]{1,0:T(8,128)}, u32[]{:S(2)}, u32[]{:S(2)}) collective-permute-start(f32[8,2048]{1,0:T(8,128)} %constant_dynamic-slice_fusion.5), channel_id=1, source_target_pairs={{0,1},{1,0},{2,3},{3,2},{4,5},{5,4},{6,7},{7,6},{8,9},{9,8},{10,11... | collective-permute-start | bytes 196616 | tf_op jit(solution)/shard_map/ppermute | solution.py:52
  (50 other events, 562.1 us)

commit v6 on v5

--- a/solution.py
+++ b/solution.py
@@ -307,11 +307,11 @@
     o_g = send(s_g, "xflip")
     o_ab = send(s_ab, "xflip")
 
-    p_blk = ordered(z % 2, p_chip, send(p_chip, "znear"))
+    p_blk = ordered(y % 2, p_chip, send(p_chip, "ynear"))
+    p_blk = ordered(y // 2, p_blk, send(p_blk, "yflip"))
+    p_half = p_blk
+    p_blk = ordered(z % 2, p_blk, send(p_blk, "znear"))
     p_blk = ordered(z // 2, p_blk, send(p_blk, "zflip"))
-    p_half = p_blk
-    p_blk = ordered(y % 2, p_blk, send(p_blk, "ynear"))
-    p_blk = ordered(y // 2, p_blk, send(p_blk, "yflip"))
     q_blk = ordered(x % 2, q_chip, send(q_chip, "xnear"))
     q_far, q_blk, _ = lax.optimization_barrier((send(q_blk, "xflip"), q_blk, p_blk))
     q_blk = ordered(x // 2, q_blk, q_far)
@@ -337,7 +337,7 @@
     q_feat = q_blk[:, :2048]
     positive = (q_blk[:, 2048].astype(f32) * 16 + q_blk[:, 2049].astype(f32)).astype(jnp.int32)
     row = jnp.arange(128, dtype=jnp.int32)
-    row_c, row_z, row_y = (row // 4) % 2, (row // 8) % 4, row // 32
+    row_c, row_y, row_z = (row // 4) % 2, (row // 8) % 4, row // 32
     passage_id = (((row_y * 2 + x_lo) * 2 + row_c) * 8 + x_hi * 4 + row_z) * 4 + row % 4
     partial = lax.dot_general(q_feat, p_blk, NT, preferred_element_type=f32)
     logits = logit_scale * (partial + send(partial, "core"))
@@ -506,10 +506,10 @@
 
     p_sum = p_part
     for bit, n, move, until in (
-        (y // 2, 64, "yflip", stats_own),
-        (y % 2, 32, "ynear", packed_total),
-        (z // 2, 16, "zflip", y_par),
-        (z % 2, 8, "znear", attn_grad),
+        (z // 2, 64, "zflip", stats_own),
+        (z % 2, 32, "znear", packed_total),
+        (y // 2, 16, "yflip", y_par),
+        (y % 2, 8, "ynear", attn_grad),
     ):
         got = send(pick(p_sum, n * (1 - bit), n), move)
         got, p_sum, _ = lax.optimization_barrier((got, p_sum, until))

time: 271 us -> 276 us (1.018)
  starting transfers between devices: 71.4 us -> 80.8 us
  waiting for transfers between devices: 93.1 us -> 88.2 us
    all_to_all x2, starting transfers between devices: 13.3 us -> 18.2 us  [compute(): lax.all_to_all(value, AX, 0, 0, axis_index_groups=sides, tiled=True)]
    ppermute x40, waiting for transfers between devices: 86 us -> 81.2 us  [send(): return lax.ppermute(value, AX, MOVES[move])]
    ppermute x40, starting transfers between devices: 58 us -> 62.6 us  [send(): return lax.ppermute(value, AX, MOVES[move])]
  transfers between devices with their start and end apart: 42 -> 42, of which waited for: 12 -> 14; matrix products, arithmetic and copies ran while one was open for 17% -> 17% of each run, Pallas kernels for 15% -> 15%
where the time goes in v6:
time: 276 us; the launch traced here: 275 us
  waiting for transfers between devices  88.2 us (32%)
  starting transfers between devices  80.8 us (29%)
  Pallas kernels  41.1 us (15%)
  local copies, waits for them, and re-layouts  30.1 us (11%)
  other arithmetic  21.8 us (8%)
  between operations  8.94 us (3%)
  matrix products  3.79 us (1%)
    ppermute x40, waiting for transfers between devices, send(): return lax.ppermute(value, AX, MOVES[move])  81.2 us
    ppermute x40, starting transfers between devices, send(): return lax.ppermute(value, AX, MOVES[move])  62.6 us
    pallas_call x2, Pallas kernels, block_call(): pl.pallas_call(functools.partial(block_kernel, copies, len(srcs), first),...  27.1 us
    all_to_all x2, starting transfers between devices, compute(): lax.all_to_all(value, AX, 0, 0, axis_index_groups=sides, tiled=True)  18.2 us
    pallas_call x1, Pallas kernels, back_call(): pl.pallas_call(functools.partial(back_kernel, copies, len(srcs)), out_sha...  13.9 us
    unnamed x78, local copies, waits for them, and re-layouts  7.4 us
    all_to_all x2, waiting for transfers between devices, compute(): lax.all_to_all(value, AX, 0, 0, axis_index_groups=sides, tiled=True)  6.91 us
    dynamic_slice x13, local copies, waits for them, and re-layouts, pick(): return lax.dynamic_slice_in_dim(value, start, size, axis=axis)  5.89 us
  transfers between devices with their start and end apart: 42, of which 14 were waited for; matrix products, arithmetic and copies ran while one was open for 17% of the time, Pallas kernels for 15%

profile of v6, /device:TPU:1, one launch (start us, length us, event | category | flops | bytes accessed | tf_op | source)
XLA Modules:
  0.0 274.7 jit_solution(17574620064454393421)
XLA Ops:
  1.8 3.4 %collective-permute-start.5 = (bf16[512,256]{1,0:T(8,128)(2,1)S(1)}, bf16[512,256]{1,0:T(8,128)(2,1)S(1)}, u32[]{:S(2)}, u32[]{:S(2)}) collective-permute-start(bf16[512,256]{1,0:T(8,128)(2,1)S(1)} %get-tuple-element.55), channel_id=1, source_target_pairs={{0,20},{1,21},{2,22},{3,23},{4,16},{5,17},{6,18},{7,19},{8,28},{9,... | collective-permute-start | bytes 786440 | tf_op jit(solution)/shard_map/ppermute | solution.py:52
  8.7 2.3 constant_dynamic-slice_fusion.15
  11.1 2.2 constant_dynamic-slice_fusion.1
  18.7 2.9 %collective-permute-start.17 = (bf16[16,2048]{1,0:T(8,128)(2,1)S(1)}, bf16[16,2048]{1,0:T(8,128)(2,1)S(1)}, u32[]{:S(2)}, u32[]{:S(2)}) collective-permute-start(bf16[16,2048]{1,0:T(8,128)(2,1)S(1)} %maximum_select_fusion.9), channel_id=1, source_target_pairs={{0,96},{1,97},{2,98},{3,99},{4,100},{5,101},{6,102},{7,103},{8,104... | collective-permute-start | bytes 196616 | tf_op jit(solution)/shard_map/ppermute | solution.py:52
  21.6 2.0 collective-permute-done.17
  25.5 2.4 collective-permute-start.21
  27.9 2.3 collective-permute-start.18
  30.2 2.3 collective-permute-start.23
  33.3 4.9 %collective-permute-done.23 = bf16[64,2048]{1,0:T(8,128)(2,1)S(1)} collective-permute-done((bf16[64,2048]{1,0:T(8,128)(2,1)S(1)}, bf16[64,2048]{1,0:T(8,128)(2,1)S(1)}, u32[]{:S(2)}, u32[]{:S(2)}) %collective-permute-start.23) | collective-permute-done | bytes 262176 | tf_op jit(solution)/shard_map/ppermute | solution.py:52
  42.8 2.2 collective-permute-start.7
  45.1 2.1 collective-permute-start.26
  49.8 2.1 collective-permute-start.27
  55.2 6.8 %collective-permute-done.6.refs_8_ = bf16[1536,256]{1,0:T(8,128)(2,1)S(1)} collective-permute-done((bf16[1536,256]{1,0:T(8,128)(2,1)S(1)}, bf16[1536,256]{1,0:T(8,128)(2,1)S(1)}, u32[]{:S(2)}, u32[]{:S(2)}) %collective-permute-start.6) | collective-permute-done | bytes 786464 | tf_op jit(solution)/shard_map/ppermute | solution.py:52
  62.3 2.7 collective-permute-start.12
  66.8 5.8 %collective-permute-done.11.refs_10_ = bf16[768,256]{1,0:T(8,128)(2,1)S(1)} collective-permute-done((bf16[768,256]{1,0:T(8,128)(2,1)S(1)}, bf16[768,256]{1,0:T(8,128)(2,1)S(1)}, u32[]{:S(2)}, u32[]{:S(2)}) %collective-permute-start.11) | collective-permute-done | bytes 393248 | tf_op jit(solution)/shard_map/ppermute | solution.py:52
  72.6 3.5 %collective-permute-start.10 = (bf16[2560,256]{1,0:T(8,128)(2,1)S(1)}, bf16[2560,256]{1,0:T(8,128)(2,1)S(1)}, u32[]{:S(2)}, u32[]{:S(2)}) collective-permute-start(bf16[2560,256]{1,0:T(8,128)(2,1)S(1)} %pad_maximum_fusion.1.refs_1_), channel_id=1, source_target_pairs={{0,96},{1,97},{2,98},{3,99},{4,100},{5,101},{6,102},{7,103},{8,104... | collective-permute-start | bytes 3932168 | tf_op jit(solution)/shard_map/ppermute | solution.py:52
  79.3 34.3 %collective-permute-done.13.refs_6_ = bf16[1024,256]{1,0:T(8,128)(2,1)S(1)} collective-permute-done((bf16[1024,256]{1,0:T(8,128)(2,1)S(1)}, bf16[1024,256]{1,0:T(8,128)(2,1)S(1)}, u32[]{:S(2)}, u32[]{:S(2)}) %collective-permute-start.13) | collective-permute-done | bytes 524320 | tf_op jit(solution)/shard_map/ppermute | solution.py:52
  113.7 3.3 %collective-permute-start.19 = (bf16[256,2048]{1,0:T(8,128)(2,1)S(1)}, bf16[256,2048]{1,0:T(8,128)(2,1)S(1)}, u32[]{:S(2)}, u32[]{:S(2)}) collective-permute-start(bf16[256,2048]{1,0:T(8,128)(2,1)S(1)} %constant_dynamic-slice_fusion.13), channel_id=1, source_target_pairs={{0,8},{1,9},{2,10},{3,11},{4,12},{5,13},{6,14},{7,15},{8,0},{9,1},... | collective-permute-start | bytes 3145736 | tf_op jit(solution)/shard_map/ppermute | solution.py:52
  121.4 3.3 %collective-permute-start.14 = (bf16[1792,256]{1,0:T(8,128)(2,1)}, bf16[1792,256]{1,0:T(8,128)(2,1)}, u32[]{:S(2)}, u32[]{:S(2)}) collective-permute-start(bf16[1792,256]{1,0:T(8,128)(2,1)} %pad_maximum_fusion.2), channel_id=1, source_target_pairs={{0,96},{1,97},{2,98},{3,99},{4,100},{5,101},{6,102},{7,103},{8,104... | collective-permute-start | bytes 2752520 | tf_op jit(solution)/shard_map/ppermute | solution.py:52
  124.6 22.1 %collective-permute-done.2.refs_3_.refs_14_ = bf16[1024,768]{1,0:T(8,128)(2,1)S(1)} collective-permute-done((bf16[1024,768]{1,0:T(8,128)(2,1)S(1)}, bf16[1024,768]{1,0:T(8,128)(2,1)S(1)}, u32[]{:S(2)}, u32[]{:S(2)}) %collective-permute-start.2) | collective-permute-done | bytes 1572896 | tf_op jit(solution)/shard_map/ppermute | solution.py:52
  150.1 2.7 collective-permute-start.4
  154.3 13.3 %block_first.1 = (f32[512,2048]{1,0:T(8,128)S(1)}, f32[528,128]{1,0:T(8,128)S(1)}) custom-call(s32[13]{0:T(128)S(1)} %stack.117.scal, bf16[512,4096]{1,0:T(8,128)(2,1)} %refs_0_.5, bf16[2560,256]{1,0:T(8,128)(2,1)} %copy-done.12, bf16[1024,256]{1,0:T(8,128)(2,1)} %copy-done.24, bf16[2560,256]{1,0:T(8,128)(2,1)} %copy-done.18, bf16[1024,256]{1,0:T(8,128)(2,1)} %copy-done.31, ...), custom_call_target="tpu_custom_call" | custom-call | flops 4294967296 | bytes 16777216 | tf_op jit(solution)/shard_map/block_first/pallas_call | solution.py:246
  170.6 13.8 %block_last.1 = (f32[512,2048]{1,0:T(8,128)}, f32[528,128]{1,0:T(8,128)S(1)}) custom-call(s32[13]{0:T(128)S(1)} %stack.107.scal, bf16[512,4096]{1,0:T(8,128)(2,1)} %refs_0_.5, bf16[512,1024]{1,0:T(8,128)(2,1)} %collective-permute-done.refs_7_.refs_1_, bf16[1024,768]{1,0:T(8,128)(2,1)} %copy-done.19, ...), custom_call_target="tpu_custom_call", output_to_operand_aliasing={{0}: (18, {})} | custom-call | flops 4294967296 | bytes 16777216 | tf_op jit(solution)/shard_map/block_last/pallas_call | solution.py:246
  184.4 6.2 %collective-permute-start.31 = (f32[528,128]{1,0:T(8,128)S(1)}, f32[528,128]{1,0:T(8,128)}, u32[]{:S(2)}, u32[]{:S(2)}) collective-permute-start(f32[528,128]{1,0:T(8,128)S(1)} %get-tuple-element.32), channel_id=1, source_target_pairs={{0,8},{1,9},{2,10},{3,11},{4,12},{5,13},{6,14},{7,15},{8,0},{9,1},... | collective-permute-start | bytes 811016 | tf_op jit(solution)/shard_map/ppermute | solution.py:52
  201.3 10.7 %all-to-all-start = ((f32[64,1,1280]{2,1,0:T(1,128)}), f32[64,1,1280]{2,1,0:T(1,128)}, u32[]{:S(2)}, u32[]{:S(2)}) async-start(f32[64,1,1280]{2,1,0:T(1,128)} %all_to_all.13), calls=%async_computation | async-start | bytes 655360 | tf_op jit(solution)/shard_map/all_to_all | solution.py:495
  214.9 2.9 %collective-permute-start.35 = (f32[16,2048]{1,0:T(8,128)S(1)}, f32[16,2048]{1,0:T(8,128)}, u32[]{:S(2)}, u32[]{:S(2)}) collective-permute-start(f32[16,2048]{1,0:T(8,128)S(1)} %constant_dynamic-slice_fusion.6), channel_id=1, source_target_pairs={{0,96},{1,97},{2,98},{3,99},{4,100},{5,101},{6,102},{7,103},{8,104... | collective-permute-start | bytes 393224 | tf_op jit(solution)/shard_map/ppermute | solution.py:52
  217.8 13.9 %back.1 = (bf16[256,4096]{1,0:T(8,128)(2,1)S(1)}, bf16[256,4096]{1,0:T(8,128)(2,1)}) custom-call(s32[17]{0:T(128)S(1)} %stack.119.scal, bf16[512,4096]{1,0:T(8,128)(2,1)} %refs_0_.5, bf16[2560,256]{1,0:T(8,128)(2,1)} %copy-done.12, bf16[1024,256]{1,0:T(8,128)(2,1)} %copy-done.24, bf16[2560,256]{1,0:T(8,128)(2,1)} %copy-done.18, ...), custom_call_target="tpu_custom_call" | custom-call | flops 8589934592 | bytes 25165824 | tf_op jit(solution)/shard_map/back/pallas_call | solution.py:197
  235.5 7.5 %all-to-all-start.1 = ((f32[64,1,1280]{2,1,0:T(1,128)}), f32[64,1,1280]{2,1,0:T(1,128)S(1)}, u32[]{:S(2)}, u32[]{:S(2)}) async-start(f32[64,1,1280]{2,1,0:T(1,128)} %broadcast_in_dim.97), calls=%async_computation.1 | async-start | bytes 655360 | tf_op jit(solution)/shard_map/all_to_all | solution.py:495
  245.8 6.9 %all-to-all-done.1 = f32[64,1,1280]{2,1,0:T(1,128)S(1)} async-done(((f32[64,1,1280]{2,1,0:T(1,128)}), f32[64,1,1280]{2,1,0:T(1,128)S(1)}, u32[]{:S(2)}, u32[]{:S(2)}) %all-to-all-start.1) | async-done | bytes 327712 | tf_op jit(solution)/shard_map/all_to_all | solution.py:495
  255.4 2.3 collective-permute-start.32
  262.9 3.7 %add_convert_fusion = bf16[256,4096]{1,0:T(8,128)(2,1)} fusion(bf16[256,4096]{1,0:T(8,128)(2,1)} %collective-permute-done.37, bf16[256,4096]{1,0:T(8,128)(2,1)S(1)} %copy-done.5), kind=kLoop, calls=%fused_computation.3 | loop fusion | flops 4194304 | bytes 6291456 | tf_op jit(solution)/shard_map/convert_element_type | solution.py:486
  268.0 3.7 %maximum_select_fusion = bf16[1,256,4096]{2,1,0:T(8,128)(2,1)} fusion(bf16[1,256,2048]{2,1,0:T(8,128)(2,1)} %bitcast.39, bf16[1,256,2048]{2,1,0:T(8,128)(2,1)S(1)} %get-tuple-element.57, pred[]{:T(512)S(6)} %eq.71), kind=kLoop, calls=%fused_computation.9 | loop fusion | flops 9437184 | bytes 4194305 | tf_op jit(solution)/shard_map/jit(_where)/select_n | solution.py:56
  (270 shorter events, 65.1 us)
Async XLA Ops:
  1.8 40.4 %collective-permute-start.5 = (bf16[512,256]{1,0:T(8,128)(2,1)S(1)}, bf16[512,256]{1,0:T(8,128)(2,1)S(1)}, u32[]{:S(2)}, u32[]{:S(2)}) collective-permute-start(bf16[512,256]{1,0:T(8,128)(2,1)S(1)} %get-tuple-element.55), channel_id=1, source_target_pairs={{0,20},{1,21},{2,22},{3,23},{4,16},{5,17},{6,18},{7,19},{8,28},{9,... | collective-permute-start | bytes 786440 | tf_op jit(solution)/shard_map/ppermute | solution.py:52
  7.7 7.7 %collective-permute-start.15 = (bf16[8,2176]{1,0:T(8,128)(2,1)S(1)}, bf16[8,2176]{1,0:T(8,128)(2,1)S(1)}, u32[]{:S(2)}, u32[]{:S(2)}) collective-permute-start(bf16[8,2176]{1,0:T(8,128)(2,1)S(1)} %get-tuple-element.86), channel_id=1, source_target_pairs={{0,8},{1,9},{2,10},{3,11},{4,12},{5,13},{6,14},{7,15},{8,0},{9,1},... | collective-permute-start | bytes 104456 | tf_op jit(solution)/shard_map/ppermute | solution.py:52
  11.0 66.9 %collective-permute-start = (bf16[512,1024]{1,0:T(8,128)(2,1)}, bf16[512,1024]{1,0:T(8,128)(2,1)}, u32[]{:S(2)}, u32[]{:S(2)}) collective-permute-start(bf16[512,1024]{1,0:T(8,128)(2,1)} %constant_dynamic-slice_fusion.15), channel_id=1, source_target_pairs={{0,20},{1,21},{2,22},{3,23},{4,16},{5,17},{6,18},{7,19},{8,28},{9,... | collective-permute-start | bytes 3145736 | tf_op jit(solution)/shard_map/ppermute | solution.py:52
  17.0 8.4 %collective-permute-start.20 = (bf16[8,2176]{1,0:T(8,128)(2,1)S(1)}, bf16[8,2176]{1,0:T(8,128)(2,1)S(1)}, u32[]{:S(2)}, u32[]{:S(2)}) collective-permute-start(bf16[8,2176]{1,0:T(8,128)(2,1)S(1)} %maximum_select_fusion.10), channel_id=1, source_target_pairs={{0,16},{1,17},{2,18},{3,19},{4,20},{5,21},{6,22},{7,23},{8,24},{9,... | collective-permute-start | bytes 104456 | tf_op jit(solution)/shard_map/ppermute | solution.py:52
  25.5 13.1 %collective-permute-start.21 = (bf16[16,2176]{1,0:T(8,128)(2,1)S(1)}, bf16[16,2176]{1,0:T(8,128)(2,1)S(1)}, u32[]{:S(2)}, u32[]{:S(2)}) collective-permute-start(bf16[16,2176]{1,0:T(8,128)(2,1)S(1)} %maximum_select_fusion.8), channel_id=1, source_target_pairs={{0,20},{1,21},{2,22},{3,23},{4,16},{5,17},{6,18},{7,19},{8,28},{9,... | collective-permute-start | bytes 208904 | tf_op jit(solution)/shard_map/ppermute | solution.py:52
  27.9 122.2 %collective-permute-start.18 = (bf16[256,4096]{1,0:T(8,128)(2,1)S(1)}, bf16[256,4096]{1,0:T(8,128)(2,1)S(1)}, u32[]{:S(2)}, u32[]{:S(2)}) collective-permute-start(bf16[256,4096]{1,0:T(8,128)(2,1)S(1)} %bitcast.114), channel_id=1, source_target_pairs={{0,8},{1,9},{2,10},{3,11},{4,12},{5,13},{6,14},{7,15},{8,0},{9,1},... | collective-permute-start | bytes 6291464 | tf_op jit(solution)/shard_map/ppermute | solution.py:52
  30.2 8.0 %collective-permute-start.23 = (bf16[64,2048]{1,0:T(8,128)(2,1)S(1)}, bf16[64,2048]{1,0:T(8,128)(2,1)S(1)}, u32[]{:S(2)}, u32[]{:S(2)}) collective-permute-start(bf16[64,2048]{1,0:T(8,128)(2,1)S(1)} %maximum_select_fusion.2), channel_id=1, source_target_pairs={{0,3},{1,2},{2,1},{3,0},{4,7},{5,6},{6,5},{7,4},{8,11},{9,10},{10,... | collective-permute-start | bytes 786440 | tf_op jit(solution)/shard_map/ppermute | solution.py:52
  42.2 19.8 %collective-permute-start.6 = (bf16[1536,256]{1,0:T(8,128)(2,1)S(1)}, bf16[1536,256]{1,0:T(8,128)(2,1)S(1)}, u32[]{:S(2)}, u32[]{:S(2)}) collective-permute-start(bf16[1536,256]{1,0:T(8,128)(2,1)S(1)} %pad_maximum_fusion.3), channel_id=1, source_target_pairs={{0,1},{1,2},{2,3},{3,0},{4,5},{5,6},{6,7},{7,4},{8,9},{9,10},{10,1... | collective-permute-start | bytes 2359304 | tf_op jit(solution)/shard_map/ppermute | solution.py:52
  42.8 19.4 %collective-permute-start.7 = (bf16[1536,256]{1,0:T(8,128)(2,1)S(1)}, bf16[1536,256]{1,0:T(8,128)(2,1)S(1)}, u32[]{:S(2)}, u32[]{:S(2)}) collective-permute-start(bf16[1536,256]{1,0:T(8,128)(2,1)S(1)} %pad_maximum_fusion.3), channel_id=1, source_target_pairs={{0,3},{1,0},{2,1},{3,2},{4,7},{5,4},{6,5},{7,6},{8,11},{9,8},{10,9... | collective-permute-start | bytes 2359304 | tf_op jit(solution)/shard_map/ppermute | solution.py:52
  62.1 10.5 %collective-permute-start.11 = (bf16[768,256]{1,0:T(8,128)(2,1)S(1)}, bf16[768,256]{1,0:T(8,128)(2,1)S(1)}, u32[]{:S(2)}, u32[]{:S(2)}) collective-permute-start(bf16[768,256]{1,0:T(8,128)(2,1)S(1)} %pad_maximum_fusion.6), channel_id=1, source_target_pairs={{0,1},{1,2},{2,3},{3,0},{4,5},{5,6},{6,7},{7,4},{8,9},{9,10},{10,1... | collective-permute-start | bytes 1179656 | tf_op jit(solution)/shard_map/ppermute | solution.py:52
  62.3 13.8 %collective-permute-start.12 = (bf16[768,256]{1,0:T(8,128)(2,1)S(1)}, bf16[768,256]{1,0:T(8,128)(2,1)S(1)}, u32[]{:S(2)}, u32[]{:S(2)}) collective-permute-start(bf16[768,256]{1,0:T(8,128)(2,1)S(1)} %pad_maximum_fusion.7), channel_id=1, source_target_pairs={{0,3},{1,0},{2,1},{3,2},{4,7},{5,4},{6,5},{7,6},{8,11},{9,8},{10,9... | collective-permute-start | bytes 1179656 | tf_op jit(solution)/shard_map/ppermute | solution.py:52
  65.0 12.0 %collective-permute-start.28 = (f32[8,2048]{1,0:T(8,128)S(1)}, f32[8,2048]{1,0:T(8,128)S(1)}, u32[]{:S(2)}, u32[]{:S(2)}) collective-permute-start(f32[8,2048]{1,0:T(8,128)S(1)} %constant_dynamic-slice_fusion.10), channel_id=1, source_target_pairs={{0,16},{1,17},{2,18},{3,19},{4,20},{5,21},{6,22},{7,23},{8,24},{9,... | collective-permute-start | bytes 196616 | tf_op jit(solution)/shard_map/ppermute | solution.py:52
  72.6 41.1 %collective-permute-start.10 = (bf16[2560,256]{1,0:T(8,128)(2,1)S(1)}, bf16[2560,256]{1,0:T(8,128)(2,1)S(1)}, u32[]{:S(2)}, u32[]{:S(2)}) collective-permute-start(bf16[2560,256]{1,0:T(8,128)(2,1)S(1)} %pad_maximum_fusion.1.refs_1_), channel_id=1, source_target_pairs={{0,96},{1,97},{2,98},{3,99},{4,100},{5,101},{6,102},{7,103},{8,104... | collective-permute-start | bytes 3932168 | tf_op jit(solution)/shard_map/ppermute | solution.py:52
  76.2 37.3 %collective-permute-start.13 = (bf16[1024,256]{1,0:T(8,128)(2,1)S(1)}, bf16[1024,256]{1,0:T(8,128)(2,1)S(1)}, u32[]{:S(2)}, u32[]{:S(2)}) collective-permute-start(bf16[1024,256]{1,0:T(8,128)(2,1)S(1)} %pad_maximum_fusion.5.refs_2_), channel_id=1, source_target_pairs={{0,96},{1,97},{2,98},{3,99},{4,100},{5,101},{6,102},{7,103},{8,104... | collective-permute-start | bytes 1572872 | tf_op jit(solution)/shard_map/ppermute | solution.py:52
  77.1 41.0 %collective-permute-start.8 = (bf16[2560,256]{1,0:T(8,128)(2,1)S(1)}, bf16[2560,256]{1,0:T(8,128)(2,1)S(1)}, u32[]{:S(2)}, u32[]{:S(2)}) collective-permute-start(bf16[2560,256]{1,0:T(8,128)(2,1)S(1)} %pad_maximum_fusion.1.refs_1_), channel_id=1, source_target_pairs={{0,32},{1,33},{2,34},{3,35},{4,36},{5,37},{6,38},{7,39},{8,40},{9,... | collective-permute-start | bytes 3932168 | tf_op jit(solution)/shard_map/ppermute | solution.py:52
  79.2 42.2 %collective-permute-start.1 = (bf16[1024,768]{1,0:T(8,128)(2,1)S(1)}, bf16[1024,768]{1,0:T(8,128)(2,1)S(1)}, u32[]{:S(2)}, u32[]{:S(2)}) collective-permute-start(bf16[1024,768]{1,0:T(8,128)(2,1)S(1)} %pad_maximum_fusion), channel_id=1, source_target_pairs={{0,1},{1,2},{2,3},{3,0},{4,5},{5,6},{6,7},{7,4},{8,9},{9,10},{10,1... | collective-permute-start | bytes 4718600 | tf_op jit(solution)/shard_map/ppermute | solution.py:52
  113.6 33.2 %collective-permute-start.2 = (bf16[1024,768]{1,0:T(8,128)(2,1)S(1)}, bf16[1024,768]{1,0:T(8,128)(2,1)S(1)}, u32[]{:S(2)}, u32[]{:S(2)}) collective-permute-start(bf16[1024,768]{1,0:T(8,128)(2,1)S(1)} %pad_maximum_fusion), channel_id=1, source_target_pairs={{0,3},{1,0},{2,1},{3,2},{4,7},{5,4},{6,5},{7,6},{8,11},{9,8},{10,9... | collective-permute-start | bytes 4718600 | tf_op jit(solution)/shard_map/ppermute | solution.py:52
  118.1 32.0 %collective-permute-start.29 = (bf16[1024,256]{1,0:T(8,128)(2,1)S(1)}, bf16[1024,256]{1,0:T(8,128)(2,1)S(1)}, u32[]{:S(2)}, u32[]{:S(2)}) collective-permute-start(bf16[1024,256]{1,0:T(8,128)(2,1)S(1)} %pad_maximum_fusion.5.refs_2_), channel_id=1, source_target_pairs={{0,32},{1,33},{2,34},{3,35},{4,36},{5,37},{6,38},{7,39},{8,40},{9,... | collective-permute-start | bytes 1572872 | tf_op jit(solution)/shard_map/ppermute | solution.py:52
  121.0 32.6 %collective-permute-start.30 = (bf16[1536,256]{1,0:T(8,128)(2,1)}, bf16[1536,256]{1,0:T(8,128)(2,1)}, u32[]{:S(2)}, u32[]{:S(2)}) collective-permute-start(bf16[1536,256]{1,0:T(8,128)(2,1)} %pad_maximum_fusion.4), channel_id=1, source_target_pairs={{0,20},{1,21},{2,22},{3,23},{4,16},{5,17},{6,18},{7,19},{8,28},{9,... | collective-permute-start | bytes 2359304 | tf_op jit(solution)/shard_map/ppermute | solution.py:52
  121.4 48.3 %collective-permute-start.14 = (bf16[1792,256]{1,0:T(8,128)(2,1)}, bf16[1792,256]{1,0:T(8,128)(2,1)}, u32[]{:S(2)}, u32[]{:S(2)}) collective-permute-start(bf16[1792,256]{1,0:T(8,128)(2,1)} %pad_maximum_fusion.2), channel_id=1, source_target_pairs={{0,96},{1,97},{2,98},{3,99},{4,100},{5,101},{6,102},{7,103},{8,104... | collective-permute-start | bytes 2752520 | tf_op jit(solution)/shard_map/ppermute | solution.py:52
  146.8 22.9 %collective-permute-start.9 = (bf16[1792,256]{1,0:T(8,128)(2,1)}, bf16[1792,256]{1,0:T(8,128)(2,1)}, u32[]{:S(2)}, u32[]{:S(2)}) collective-permute-start(bf16[1792,256]{1,0:T(8,128)(2,1)} %slice.263), channel_id=1, source_target_pairs={{0,32},{1,33},{2,34},{3,35},{4,36},{5,37},{6,38},{7,39},{8,40},{9,... | collective-permute-start | bytes 2752520 | tf_op jit(solution)/shard_map/ppermute | solution.py:52
  150.1 19.6 %collective-permute-start.3 = (bf16[512,768]{1,0:T(8,128)(2,1)}, bf16[512,768]{1,0:T(8,128)(2,1)}, u32[]{:S(2)}, u32[]{:S(2)}) collective-permute-start(bf16[512,768]{1,0:T(8,128)(2,1)} %slice.259), channel_id=1, source_target_pairs={{0,1},{1,2},{2,3},{3,0},{4,5},{5,6},{6,7},{7,4},{8,9},{9,10},{10,1... | collective-permute-start | bytes 2359304 | tf_op jit(solution)/shard_map/ppermute | solution.py:52
  150.1 19.5 %collective-permute-start.4 = (bf16[512,768]{1,0:T(8,128)(2,1)}, bf16[512,768]{1,0:T(8,128)(2,1)S(1)}, u32[]{:S(2)}, u32[]{:S(2)}) collective-permute-start(bf16[512,768]{1,0:T(8,128)(2,1)} %slice.260), channel_id=1, source_target_pairs={{0,3},{1,0},{2,1},{3,2},{4,7},{5,4},{6,5},{7,6},{8,11},{9,8},{10,9... | collective-permute-start | bytes 2359304 | tf_op jit(solution)/shard_map/ppermute | solution.py:52
  153.6 37.0 %collective-permute-start.33 = (f32[64,2048]{1,0:T(8,128)S(1)}, f32[64,2048]{1,0:T(8,128)S(1)}, u32[]{:S(2)}, u32[]{:S(2)}) collective-permute-start(f32[64,2048]{1,0:T(8,128)S(1)} %copy-done.34), channel_id=1, source_target_pairs={{0,3},{1,2},{2,1},{3,0},{4,7},{5,6},{6,5},{7,4},{8,11},{9,10},{10,... | collective-permute-start | bytes 1572872 | tf_op jit(solution)/shard_map/ppermute | solution.py:52
  184.4 7.5 %collective-permute-start.31 = (f32[528,128]{1,0:T(8,128)S(1)}, f32[528,128]{1,0:T(8,128)}, u32[]{:S(2)}, u32[]{:S(2)}) collective-permute-start(f32[528,128]{1,0:T(8,128)S(1)} %get-tuple-element.32), channel_id=1, source_target_pairs={{0,8},{1,9},{2,10},{3,11},{4,12},{5,13},{6,14},{7,15},{8,0},{9,1},... | collective-permute-start | bytes 811016 | tf_op jit(solution)/shard_map/ppermute | solution.py:52
  191.5 22.4 %collective-permute-start.34 = (f32[32,2048]{1,0:T(8,128)}, f32[32,2048]{1,0:T(8,128)}, u32[]{:S(2)}, u32[]{:S(2)}) collective-permute-start(f32[32,2048]{1,0:T(8,128)} %constant_dynamic-slice_fusion.7), channel_id=1, source_target_pairs={{0,1},{1,0},{2,3},{3,2},{4,5},{5,4},{6,7},{7,6},{8,9},{9,8},{10,11... | collective-permute-start | bytes 786440 | tf_op jit(solution)/shard_map/ppermute | solution.py:52
  201.3 32.0 %all-to-all-start = ((f32[64,1,1280]{2,1,0:T(1,128)}), f32[64,1,1280]{2,1,0:T(1,128)}, u32[]{:S(2)}, u32[]{:S(2)}) async-start(f32[64,1,1280]{2,1,0:T(1,128)} %all_to_all.13), calls=%async_computation | async-start | bytes 655360 | tf_op jit(solution)/shard_map/all_to_all | solution.py:495
  213.2 54.8 %collective-permute-start.39 = (bf16[256,2048]{1,0:T(8,128)(2,1)}, bf16[256,2048]{1,0:T(8,128)(2,1)}, u32[]{:S(2)}, u32[]{:S(2)}) collective-permute-start(bf16[256,2048]{1,0:T(8,128)(2,1)} %get-tuple-element.58), channel_id=1, source_target_pairs={{0,8},{1,9},{2,10},{3,11},{4,12},{5,13},{6,14},{7,15},{8,0},{9,1},... | collective-permute-start | bytes 3145736 | tf_op jit(solution)/shard_map/ppermute | solution.py:52
  214.9 18.5 %collective-permute-start.35 = (f32[16,2048]{1,0:T(8,128)S(1)}, f32[16,2048]{1,0:T(8,128)}, u32[]{:S(2)}, u32[]{:S(2)}) collective-permute-start(f32[16,2048]{1,0:T(8,128)S(1)} %constant_dynamic-slice_fusion.6), channel_id=1, source_target_pairs={{0,96},{1,97},{2,98},{3,99},{4,100},{5,101},{6,102},{7,103},{8,104... | collective-permute-start | bytes 393224 | tf_op jit(solution)/shard_map/ppermute | solution.py:52
  233.1 29.8 %collective-permute-start.37 = (bf16[256,4096]{1,0:T(8,128)(2,1)}, bf16[256,4096]{1,0:T(8,128)(2,1)}, u32[]{:S(2)}, u32[]{:S(2)}) collective-permute-start(bf16[256,4096]{1,0:T(8,128)(2,1)} %get-tuple-element.38), channel_id=1, source_target_pairs={{0,8},{1,9},{2,10},{3,11},{4,12},{5,13},{6,14},{7,15},{8,0},{9,1},... | collective-permute-start | bytes 6291464 | tf_op jit(solution)/shard_map/ppermute | solution.py:52
  235.5 17.3 %all-to-all-start.1 = ((f32[64,1,1280]{2,1,0:T(1,128)}), f32[64,1,1280]{2,1,0:T(1,128)S(1)}, u32[]{:S(2)}, u32[]{:S(2)}) async-start(f32[64,1,1280]{2,1,0:T(1,128)} %broadcast_in_dim.97), calls=%async_computation.1 | async-start | bytes 655360 | tf_op jit(solution)/shard_map/all_to_all | solution.py:495
  244.8 21.8 %collective-permute-start.36 = (f32[8,2048]{1,0:T(8,128)}, f32[8,2048]{1,0:T(8,128)}, u32[]{:S(2)}, u32[]{:S(2)}) collective-permute-start(f32[8,2048]{1,0:T(8,128)} %constant_dynamic-slice_fusion.5), channel_id=1, source_target_pairs={{0,32},{1,33},{2,34},{3,35},{4,36},{5,37},{6,38},{7,39},{8,40},{9,... | collective-permute-start | bytes 196616 | tf_op jit(solution)/shard_map/ppermute | solution.py:52
  (50 other events, 565.0 us)
